TPU v7x, 32 devices: a whole 2x2x4 slice. The times are simulated.
32 devices in a mesh: dom: 8 (over z, y), grp: 4 (over x, core).
Axes of the slice: x: 2, y: 2, z: 4, core: 2. Of those that a mesh axis runs over, the one named last changes fastest.
Arguments:
- a_blocks: bfloat16 [32, 7, 48, 64, 448], P('dom', None, 'grp'), may hold values from -0.25 to 0.25
- prolong: bfloat16 [32, 7, 48, 64, 128], P('dom', None, 'grp'), may hold values from -0.75 to 0.75
- zagg: int32 [32], replicated, may hold values from 0 to 15, as said below
- xlen: int32 [4, 4], replicated, may hold values from 1 to 6, 12 in all within a row
Outputs:
- coarse_operator: bfloat16 [16, 16, 128, 640], P('dom', 'grp')
Inputs may be any that keep to these rules, and one draw needn't show every extreme that they name: zagg starts at 0, never falls and rises by 0 or 1 from layer to layer; every run of 4 layers of one index of dom holds exactly 2 layers where a new interval begins, the first layer of all among them.
All inputs are finite; a program needn't handle non-finite values.
Results may differ from a plain program's by a relative error of at most 0.005.
Values may be sent and summed in bfloat16 or wider, within the bound.
No kernel may reach another device: no remote copies, remote signals or barrier semaphores. Data moves between devices by JAX's collectives and lax.ppermute only.
A program may use at most 256 MiB of HBM per device.

v0:
```python
import jax
import jax.numpy as jnp
from jax import lax
from jax.sharding import PartitionSpec as P


def with_halo(block, sides, width):
    for axis, dim in sides:
        count = lax.axis_size(axis)
        forward = [(i, i + 1) for i in range(count - 1)]
        backward = [(target, source) for source, target in forward]
        low = lax.ppermute(
            lax.slice_in_dim(block, block.shape[dim] - width, None, axis=dim), axis, forward
        )
        high = lax.ppermute(lax.slice_in_dim(block, 0, width, axis=dim), axis, backward)
        block = jnp.concatenate([low, block, high], axis=dim)
    return block


def passed_along(block, axis, distance):
    devices = range(lax.axis_size(axis))
    route = [(i - distance, i) for i in devices if i - distance in devices]
    return lax.ppermute(block, axis, route)


def neighbour_products(a_blocks, padded):
    width = a_blocks.shape[-1] // 7
    centre = padded[1:-1, 1:-1, 1:-1]
    beside = [
        centre,
        padded[1:-1, 1:-1, :-2],
        padded[1:-1, 1:-1, 2:],
        padded[1:-1, :-2, 1:-1],
        padded[1:-1, 2:, 1:-1],
        padded[:-2, 1:-1, 1:-1],
        padded[2:, 1:-1, 1:-1],
    ]
    return [
        jnp.einsum(
            "zyxrs,zyxsc->zyxrc",
            a_blocks[..., k * width : (k + 1) * width],
            beside[k],
            preferred_element_type=jnp.float32,
        )
        for k in range(7)
    ]


def route_slots(products, same_xm, same_xp, same_zm, same_zp):
    self_sum = (
        products[0]
        + products[3]
        + products[4]
        + same_xm * products[1]
        + same_xp * products[2]
        + same_zm * products[5]
        + same_zp * products[6]
    )
    slots = [
        self_sum,
        (1.0 - same_xm) * products[1],
        (1.0 - same_xp) * products[2],
        (1.0 - same_zm) * products[5],
        (1.0 - same_zp) * products[6],
    ]
    return jnp.concatenate(slots, axis=-1).astype(jnp.bfloat16)


def per_device(a_blocks, prolong, zagg, xlen):
    layers, depth, columns, block, coarse_width = prolong.shape
    width = a_blocks.shape[-1] // 7
    intervals = xlen.shape[1]
    halves = layers // 2
    layer_dev = lax.axis_index("dom")
    column_dev = lax.axis_index("grp")
    row_lengths = lax.dynamic_index_in_dim(xlen, column_dev, 0, keepdims=False)
    ends = jnp.cumsum(row_lengths)
    within = jnp.sum(
        (ends[:, None] <= jnp.arange(columns, dtype=jnp.int32)[None, :]).astype(jnp.int32), axis=0
    )
    column_pad = jnp.pad(within, 1, constant_values=-1)
    same_xm = (column_pad[:-2] == within).astype(jnp.float32).reshape(1, 1, columns, 1, 1)
    same_xp = (column_pad[2:] == within).astype(jnp.float32).reshape(1, 1, columns, 1, 1)
    layer_pad = jnp.pad(zagg, 1, constant_values=-1)
    layer_ids = lax.dynamic_slice_in_dim(layer_pad, layer_dev * layers, layers + 2, 0)
    same_zm = (layer_ids[:-2] == layer_ids[1:-1]).astype(jnp.float32).reshape(layers, 1, 1, 1, 1)
    same_zp = (layer_ids[2:] == layer_ids[1:-1]).astype(jnp.float32).reshape(layers, 1, 1, 1, 1)
    rimmed = with_halo(prolong, (("dom", 0), ("grp", 2)), 1)
    zeroed = jnp.pad(prolong, ((1, 1), (1, 1), (1, 1), (0, 0), (0, 0)))
    products = neighbour_products(a_blocks, zeroed)
    below = jnp.einsum(
        "yxrs,yxsc->yxrc",
        a_blocks[0, :, :, :, 5 * width : 6 * width],
        rimmed[0, :, 1:-1],
        preferred_element_type=jnp.float32,
    )
    above = jnp.einsum(
        "yxrs,yxsc->yxrc",
        a_blocks[-1, :, :, :, 6 * width : 7 * width],
        rimmed[-1, :, 1:-1],
        preferred_element_type=jnp.float32,
    )
    left_rim = jnp.einsum(
        "zyrs,zysc->zyrc",
        a_blocks[:, :, 0, :, width : 2 * width],
        rimmed[1:-1, :, 0],
        preferred_element_type=jnp.float32,
    )
    right_rim = jnp.einsum(
        "zyrs,zysc->zyrc",
        a_blocks[:, :, -1, :, 2 * width : 3 * width],
        rimmed[1:-1, :, -1],
        preferred_element_type=jnp.float32,
    )
    products[5] = products[5].at[0].add(below)
    products[6] = products[6].at[-1].add(above)
    products[1] = products[1].at[:, :, 0].add(left_rim)
    products[2] = products[2].at[:, :, -1].add(right_rim)
    routed = route_slots(products, same_xm, same_xp, same_zm, same_zp)
    member = (within[None, :] == jnp.arange(intervals, dtype=jnp.int32)[:, None]).astype(
        jnp.bfloat16
    )
    local_ids = layer_ids[1:-1] - layer_dev * halves + 1

    def accumulate(layer, running):
        piece = lax.dynamic_index_in_dim(prolong, layer, 0, keepdims=False)
        slots = lax.dynamic_index_in_dim(routed, layer, 0, keepdims=False)
        masked = piece[None] * member[:, None, :, None, None]
        coarse = jnp.einsum("eyxrc,yxrk->eck", masked, slots, preferred_element_type=jnp.float32)
        target = local_ids[layer]
        current = lax.dynamic_index_in_dim(running, target, 0, keepdims=True)
        return lax.dynamic_update_index_in_dim(running, current + coarse[None], target, 0)

    start = jnp.zeros((halves + 1, intervals, coarse_width, 5 * coarse_width), jnp.float32)
    running = lax.fori_loop(0, layers, accumulate, start)
    carried = passed_along(running[0], "dom", -1)
    owned = running[1:]
    finished = jnp.concatenate([owned[:-1], owned[-1:] + carried[None]], axis=0)
    return finished.astype(jnp.bfloat16)


def solution(mesh):
    in_specs = (P("dom", None, "grp", None, None), P("dom", None, "grp", None, None), P(), P())
    out_specs = P("dom", "grp", None, None)
    return jax.shard_map(
        per_device, mesh=mesh, in_specs=in_specs, out_specs=out_specs, check_vma=False
    )
```

profile of v0, /device:TPU:14, one launch (start us, length us, event | category | flops | bytes accessed | tf_op | source)
XLA Modules:
  0.0 275.0 jit_solution(11828233191571890794)
XLA Ops:
  10.9 8.4 %fusion.36 = f32[4,7,12,128,64]{3,4,2,1,0:T(8,128)} fusion(bf16[4,7,12,64,128]{4,3,2,1,0:T(8,128)(2,1)S(1)} %copy-done.2, bf16[4,7,12,64,448]{4,3,2,1,0:T(8,128)(2,1)} %param.14), kind=kOutput, calls=%fused_computation.39 | convolution fusion | flops 352321536 | bytes 22020096 | tf_op jit(solution)/shard_map/zyxrs,zyxsc->zyxrc/dot_general | solution.py:39
  19.2 8.5 %fusion.37 = f32[4,7,12,128,64]{3,4,2,1,0:T(8,128)} fusion(bf16[4,7,12,64,128]{4,3,2,1,0:T(8,128)(2,1)S(1)} %copy-done.2, bf16[4,7,12,64,448]{4,3,2,1,0:T(8,128)(2,1)} %param.14), kind=kOutput, calls=%fused_computation.40 | convolution fusion | flops 352321536 | bytes 22020096 | tf_op jit(solution)/shard_map/zyxrs,zyxsc->zyxrc/dot_general | solution.py:39
  27.7 8.4 %fusion.38 = f32[4,7,12,128,64]{3,4,2,1,0:T(8,128)} fusion(bf16[4,7,12,64,128]{4,3,2,1,0:T(8,128)(2,1)S(1)} %copy-done.2, bf16[4,7,12,64,448]{4,3,2,1,0:T(8,128)(2,1)} %param.14), kind=kOutput, calls=%fused_computation.41 | convolution fusion | flops 352321536 | bytes 22020096 | tf_op jit(solution)/shard_map/zyxrs,zyxsc->zyxrc/dot_general | solution.py:39
  36.1 8.3 %fusion.39 = f32[4,7,12,128,64]{3,4,2,1,0:T(8,128)} fusion(bf16[4,7,12,64,128]{4,3,2,1,0:T(8,128)(2,1)S(1)} %copy-done.2, bf16[4,7,12,64,448]{4,3,2,1,0:T(8,128)(2,1)} %param.14), kind=kOutput, calls=%fused_computation.42 | convolution fusion | flops 352321536 | bytes 22020096 | tf_op jit(solution)/shard_map/zyxrs,zyxsc->zyxrc/dot_general | solution.py:39
  44.4 8.4 %fusion.34 = f32[4,7,12,128,64]{3,4,2,1,0:T(8,128)} fusion(bf16[4,7,12,64,128]{4,3,2,1,0:T(8,128)(2,1)S(1)} %copy-done.2, bf16[4,7,12,64,448]{4,3,2,1,0:T(8,128)(2,1)} %param.14), kind=kOutput, calls=%fused_computation.37 | convolution fusion | flops 352321536 | bytes 22020096 | tf_op jit(solution)/shard_map/zyxrs,zyxsc->zyxrc/dot_general | solution.py:39
  53.2 10.6 %copy.58 = f32[4,7,12,64,128]{4,3,2,1,0:T(8,128)} copy(f32[4,7,12,64,128]{4,3,2,1,0:T(8,128)} %bitcast.148) | data formatting | bytes 22020096
  63.8 10.6 %copy.57 = f32[4,7,12,64,128]{4,3,2,1,0:T(8,128)} copy(f32[4,7,12,64,128]{4,3,2,1,0:T(8,128)} %bitcast.147) | data formatting | bytes 22020096
  74.5 4.1 %copy.54 = f32[4,7,12,64,128]{4,3,2,1,0:T(8,128)} copy(f32[4,7,12,64,128]{4,3,2,1,0:T(8,128)S(1)} %bitcast.146) | data formatting | bytes 22020096
  78.6 10.8 %copy.53 = f32[4,7,12,64,128]{4,3,2,1,0:T(8,128)} copy(f32[4,7,12,64,128]{4,3,2,1,0:T(8,128)} %bitcast.143) | data formatting | bytes 22020096
  89.6 9.8 %fusion.35 = f32[4,7,12,128,64]{3,4,2,1,0:T(8,128)} fusion(bf16[4,7,12,64,128]{4,3,2,1,0:T(8,128)(2,1)} %param.15, bf16[4,7,12,64,448]{4,3,2,1,0:T(8,128)(2,1)} %param.14), kind=kOutput, calls=%fused_computation.38 | convolution fusion | flops 352321536 | bytes 22020096 | tf_op jit(solution)/shard_map/zyxrs,zyxsc->zyxrc/dot_general | solution.py:39
  105.4 3.6 %collective-permute-start.3 = (bf16[6,7,1,64,128]{4,3,1,0,2:T(8,128)(2,1)S(1)}, bf16[6,7,1,64,128]{4,3,1,0,2:T(8,128)(2,1)S(1)}, u32[]{:S(2)}, u32[]{:S(2)}) collective-permute-start(bf16[6,7,1,64,128]{4,3,1,0,2:T(8,128)(2,1)S(1)} %get-tuple-element.211), channel_id=1, source_target_pairs={{1,0},{2,1},{3,2},{5,4},{6,5},{7,6},{9,8},{10,9},{11,10},{13,12},{... | collective-permute-start | bytes 2064392 | tf_op jit(solution)/shard_map/ppermute | solution.py:15
  109.0 4.4 %fusion.53 = f32[4,7,12,64,128]{4,3,2,1,0:T(8,128)} fusion(f32[4,7,12,64,128]{4,3,2,1,0:T(8,128)} %copy.54, f32[4,7,12,128,64]{3,4,2,1,0:T(8,128)} %fusion.38, bf16[4,7,12,64,448]{4,3,2,1,0:T(8,128)(2,1)} %param.14, bf16[1,7,12,64,128]{4,3,1,0,2:T(8,128)(2,1)S(1)} %collective-permute-done), kind=kOutput, calls=%fused_computation.56 | convolution fusion | flops 88768512 | bytes 8257536 | tf_op jit(solution)/shard_map/yxrs,yxsc->yxrc/dot_general | solution.py:91
  113.4 4.6 %fusion.51 = f32[4,7,12,64,128]{4,3,2,1,0:T(8,128)} fusion(f32[4,7,12,64,128]{4,3,2,1,0:T(8,128)} %copy.53, f32[4,7,12,128,64]{3,4,2,1,0:T(8,128)} %fusion.39, bf16[4,7,12,64,448]{4,3,2,1,0:T(8,128)(2,1)} %param.14, bf16[1,7,12,64,128]{4,3,1,0,2:T(8,128)(2,1)} %collective-permute-done.1), kind=kOutput, calls=%fused_computation.53 | convolution fusion | flops 88768512 | bytes 8257536 | tf_op jit(solution)/shard_map/yxrs,yxsc->yxrc/dot_general | solution.py:97
  123.3 27.5 %fusion.33 = bf16[4,7,12,64,640]{4,3,2,1,0:T(8,128)(2,1)} fusion(f32[4,7,12,64,128]{4,3,2,1,0:T(8,128)} %fusion.51, f32[4,7,12,64,128]{4,3,2,1,0:T(8,128)} %fusion.53, f32[4,7,12,64,128]{4,3,2,1,0:T(8,128)} %fusion.64, f32[4,7,12,64,128]{4,3,2,1,0:T(8,128)} %fusion.62, f32[4,7,12,128,64]{3,4,2,1,0:T(8,128)} %fusion.35, f32[4,7,12,128,64]{3,4,2,1,0:T(8,128)} %fusion.34, ...), kind=kOutput, calls=%fused_computation.36 | convolution fusion | flops 382599168 | bytes 82575488 | tf_op jit(solution)/shard_map/zyxrs,zyxsc->zyxrc/dot_general | solution.py:39
  150.8 8.3 %fusion.29 = bf16[4,7,12,64,640]{4,3,2,1,0:T(8,128)(2,1)} fusion(bf16[4,7,12,64,640]{4,3,2,1,0:T(8,128)(2,1)} %fusion.33, f32[4,7,12,64,128]{4,3,2,1,0:T(8,128)} %fusion.62, f32[12]{0:T(128)S(1)} %get-tuple-element.208), kind=kLoop, calls=%fused_computation.32 | loop fusion | flops 5505024 | bytes 16515120
  159.1 8.4 %fusion.30 = bf16[4,7,12,64,640]{4,3,2,1,0:T(8,128)(2,1)} fusion(bf16[4,7,12,64,640]{4,3,2,1,0:T(8,128)(2,1)} %fusion.29, f32[4,7,12,64,128]{4,3,2,1,0:T(8,128)} %fusion.64, f32[12]{0:T(128)S(1)} %get-tuple-element.214), kind=kLoop, calls=%fused_computation.33 | loop fusion | flops 5505024 | bytes 16515120
  167.5 8.4 %fusion.31 = bf16[4,7,12,64,640]{4,3,2,1,0:T(8,128)(2,1)} fusion(bf16[4,7,12,64,640]{4,3,2,1,0:T(8,128)(2,1)} %fusion.30, f32[4,7,12,64,128]{4,3,2,1,0:T(8,128)} %fusion.53, f32[4]{0:T(128)S(1)} %get-tuple-element.204), kind=kLoop, calls=%fused_computation.34 | loop fusion | flops 5505024 | bytes 16515088
  175.9 8.3 %fusion.32 = bf16[4,7,12,64,640]{4,3,2,1,0:T(8,128)(2,1)} fusion(bf16[4,7,12,64,640]{4,3,2,1,0:T(8,128)(2,1)} %fusion.31, f32[4,7,12,64,128]{4,3,2,1,0:T(8,128)} %fusion.51, f32[4]{0:T(128)S(1)} %get-tuple-element.216), kind=kLoop, calls=%fused_computation.35 | loop fusion | flops 5505024 | bytes 16515088 | tf_op jit(solution)/shard_map/concatenate | solution.py:66
  186.6 52.0 %while.18 = (s32[]{:T(128)}, f32[3,4,128,640]{3,2,1,0:T(8,128)}, s32[4]{0:T(128)S(1)}, bf16[4,7,12,64,128]{4,3,2,1,0:T(8,128)(2,1)}, bf16[4,7,12,64,640]{4,3,2,1...) while((s32[]{:T(128)}, f32[3,4,128,640]{3,2,1,0:T(8,128)}, ...), condition=%wide.region_3.4_spmd.clone, body=%wide.region_2.3_spmd.clone.sunk | while | flops 3526295552 | bytes 13632895 | solution.py:135
  190.6 8.9 %fusion.88 = f32[3,4,128,640]{3,2,1,0:T(8,128)} fusion(f32[3,4,128,640]{3,2,1,0:T(8,128)} %get-tuple-element.265, s32[]{:T(128)S(6)} %select_n.30, bf16[4,12]{1,0:T(4,128)(2,1)S(1)} %fusion.87, bf16[7,12,64,128]{3,2,0,1:T(8,128)(2,1)S(1)} %copy_bitcast_fusion.2, bf16[4,7,12,64,640]{4,3,2,1,0:T(8,128)(2,1)} %get-tuple-element.277, s32[]{:T(128)} %get-tuple-element.264), kind=kOutput, calls=%fused_computation.9.clone.1 | convolution fusion | flops 3526295552 | bytes 10879588 | tf_op jit(solution)/shard_map/while/body/eval_jaxpr/eyxrc,yxrk->eck/dot_general | solution.py:129
  203.6 9.0 %fusion.88 = f32[3,4,128,640]{3,2,1,0:T(8,128)} fusion(f32[3,4,128,640]{3,2,1,0:T(8,128)} %get-tuple-element.265, s32[]{:T(128)S(6)} %select_n.30, bf16[4,12]{1,0:T(4,128)(2,1)S(1)} %fusion.87, bf16[7,12,64,128]{3,2,0,1:T(8,128)(2,1)S(1)} %copy_bitcast_fusion.2, bf16[4,7,12,64,640]{4,3,2,1,0:T(8,128)(2,1)} %get-tuple-element.277, s32[]{:T(128)} %get-tuple-element.264), kind=kOutput, calls=%fused_computation.9.clone.1 | convolution fusion | flops 3526295552 | bytes 10879588 | tf_op jit(solution)/shard_map/while/body/eval_jaxpr/eyxrc,yxrk->eck/dot_general | solution.py:129
  216.6 9.0 %fusion.88 = f32[3,4,128,640]{3,2,1,0:T(8,128)} fusion(f32[3,4,128,640]{3,2,1,0:T(8,128)} %get-tuple-element.265, s32[]{:T(128)S(6)} %select_n.30, bf16[4,12]{1,0:T(4,128)(2,1)S(1)} %fusion.87, bf16[7,12,64,128]{3,2,0,1:T(8,128)(2,1)S(1)} %copy_bitcast_fusion.2, bf16[4,7,12,64,640]{4,3,2,1,0:T(8,128)(2,1)} %get-tuple-element.277, s32[]{:T(128)} %get-tuple-element.264), kind=kOutput, calls=%fused_computation.9.clone.1 | convolution fusion | flops 3526295552 | bytes 10879588 | tf_op jit(solution)/shard_map/while/body/eval_jaxpr/eyxrc,yxrk->eck/dot_general | solution.py:129
  229.7 8.9 %fusion.88 = f32[3,4,128,640]{3,2,1,0:T(8,128)} fusion(f32[3,4,128,640]{3,2,1,0:T(8,128)} %get-tuple-element.265, s32[]{:T(128)S(6)} %select_n.30, bf16[4,12]{1,0:T(4,128)(2,1)S(1)} %fusion.87, bf16[7,12,64,128]{3,2,0,1:T(8,128)(2,1)S(1)} %copy_bitcast_fusion.2, bf16[4,7,12,64,640]{4,3,2,1,0:T(8,128)(2,1)} %get-tuple-element.277, s32[]{:T(128)} %get-tuple-element.264), kind=kOutput, calls=%fused_computation.9.clone.1 | convolution fusion | flops 3526295552 | bytes 10879588 | tf_op jit(solution)/shard_map/while/body/eval_jaxpr/eyxrc,yxrk->eck/dot_general | solution.py:129
  244.7 27.7 %collective-permute-done.4 = f32[4,128,640]{2,1,0:T(8,128)S(1)} collective-permute-done((f32[4,128,640]{2,1,0:T(8,128)S(1)}, f32[4,128,640]{2,1,0:T(8,128)S(1)}, u32[]{:S(2)}, u32[]{:S(2)}) %collective-permute-start.4) | collective-permute-done | bytes 1310752 | tf_op jit(solution)/shard_map/ppermute | solution.py:23
  (61 shorter events, 42.0 us)
Async XLA Ops:
  0.0 53.0 %copy-start = (s32[4,4]{1,0:T(4,128)S(1)}, s32[4,4]{1,0:T(4,128)}, u32[]{:S(2)}) copy-start(s32[4,4]{1,0:T(4,128)} %param.17) | copy-start | bytes 196
  0.0 10.9 %copy-start.2 = (bf16[4,7,12,64,128]{4,3,2,1,0:T(8,128)(2,1)S(1)}, bf16[4,7,12,64,128]{4,3,2,1,0:T(8,128)(2,1)}, u32[]{:S(2)}) copy-start(bf16[4,7,12,64,128]{4,3,2,1,0:T(8,128)(2,1)} %param.15) | copy-start | bytes 16515076
  3.8 95.6 %collective-permute-start = (bf16[1,7,12,64,128]{4,3,1,0,2:T(8,128)(2,1)}, bf16[1,7,12,64,128]{4,3,1,0,2:T(8,128)(2,1)S(1)}, u32[]{:S(2)}, u32[]{:S(2)}) collective-permute-start(bf16[1,7,12,64,128]{4,3,1,0,2:T(8,128)(2,1)} %copy.47), channel_id=1, source_target_pairs={{0,4},{4,8},{8,12},{12,16},{16,20},{20,24},{24,28},{1,5},{5,9},{9,... | collective-permute-start | bytes 4128776 | tf_op jit(solution)/shard_map/ppermute | solution.py:12
  8.4 93.4 %collective-permute-start.1 = (bf16[1,7,12,64,128]{4,3,1,0,2:T(8,128)(2,1)}, bf16[1,7,12,64,128]{4,3,1,0,2:T(8,128)(2,1)}, u32[]{:S(2)}, u32[]{:S(2)}) collective-permute-start(bf16[1,7,12,64,128]{4,3,1,0,2:T(8,128)(2,1)} %copy.46), channel_id=1, source_target_pairs={{4,0},{8,4},{12,8},{16,12},{20,16},{24,20},{28,24},{5,1},{9,5},{13... | collective-permute-start | bytes 4128776 | tf_op jit(solution)/shard_map/ppermute | solution.py:15
  44.4 8.4 %copy-start.3 = (s32[32]{0:T(128)S(1)}, s32[32]{0:T(128)}, u32[]{:S(2)}) copy-start(s32[32]{0:T(128)} %param.16) | copy-start | bytes 388
  53.2 21.3 %slice-start.2 = ((s8[11010048]{0:T(1024)(128)(4,1)}), s8[4194304]{0:T(1024)(128)(4,1)S(1)}, s32[]{:S(2)}) async-start(s8[11010048]{0:T(1024)(128)(4,1)} %bitcast.144), calls=%async_computation.2 | async-start | bytes 8388608
  53.2 21.3 %slice-start.3 = ((s8[11010048]{0:T(1024)(128)(4,1)}), s8[4194304]{0:T(1024)(128)(4,1)S(1)}, s32[]{:S(2)}) async-start(s8[11010048]{0:T(1024)(128)(4,1)} %bitcast.144), calls=%async_computation.3 | async-start | bytes 8388608
  63.8 10.7 %slice-start.4 = ((s8[11010048]{0:T(1024)(128)(4,1)}), s8[2621440]{0:T(1024)(128)(4,1)S(1)}, s32[]{:S(2)}) async-start(s8[11010048]{0:T(1024)(128)(4,1)} %bitcast.144), calls=%async_computation.4 | async-start | bytes 5242880
  78.6 21.0 %slice-start = ((s8[5505024]{0:T(1024)(128)(4,1)}), s8[1310720]{0:T(1024)(128)(4,1)S(1)}, s32[]{:S(2)}) async-start(s8[5505024]{0:T(1024)(128)(4,1)} %bitcast.141), calls=%async_computation | async-start | bytes 2621440
  89.6 10.0 %slice-start.1 = ((s8[5505024]{0:T(1024)(128)(4,1)}), s8[4194304]{0:T(1024)(128)(4,1)S(1)}, s32[]{:S(2)}) async-start(s8[5505024]{0:T(1024)(128)(4,1)} %bitcast.141), calls=%async_computation.1 | async-start | bytes 8388608
  103.4 14.6 %collective-permute-start.2 = (bf16[6,7,1,64,128]{4,3,1,0,2:T(8,128)(2,1)S(1)}, bf16[6,7,1,64,128]{4,3,1,0,2:T(8,128)(2,1)S(1)}, u32[]{:S(2)}, u32[]{:S(2)}) collective-permute-start(bf16[6,7,1,64,128]{4,3,1,0,2:T(8,128)(2,1)S(1)} %get-tuple-element.210), channel_id=1, source_target_pairs={{0,1},{1,2},{2,3},{4,5},{5,6},{6,7},{8,9},{9,10},{10,11},{12,13},{... | collective-permute-start | bytes 2064392 | tf_op jit(solution)/shard_map/ppermute | solution.py:12
  105.4 15.3 %collective-permute-start.3 = (bf16[6,7,1,64,128]{4,3,1,0,2:T(8,128)(2,1)S(1)}, bf16[6,7,1,64,128]{4,3,1,0,2:T(8,128)(2,1)S(1)}, u32[]{:S(2)}, u32[]{:S(2)}) collective-permute-start(bf16[6,7,1,64,128]{4,3,1,0,2:T(8,128)(2,1)S(1)} %get-tuple-element.211), channel_id=1, source_target_pairs={{1,0},{2,1},{3,2},{5,4},{6,5},{7,6},{9,8},{10,9},{11,10},{13,12},{... | collective-permute-start | bytes 2064392 | tf_op jit(solution)/shard_map/ppermute | solution.py:15
  238.6 36.4 %copy-start.1 = (s32[4,4]{1,0:T(4,128)S(1)}, s32[4,4]{1,0:T(4,128)}, u32[]{:S(2)}) copy-start(s32[4,4]{1,0:T(4,128)} %param.17) | copy-start | bytes 196
  240.0 32.3 %collective-permute-start.4 = (f32[4,128,640]{2,1,0:T(8,128)S(1)}, f32[4,128,640]{2,1,0:T(8,128)S(1)}, u32[]{:S(2)}, u32[]{:S(2)}) collective-permute-start(f32[4,128,640]{2,1,0:T(8,128)S(1)} %slice_bitcast_fusion.2), channel_id=1, source_target_pairs={{4,0},{8,4},{12,8},{16,12},{20,16},{24,20},{28,24},{5,1},{9,5},{13... | collective-permute-start | bytes 3932168 | tf_op jit(solution)/shard_map/ppermute | solution.py:23
where the time goes:
time: 276 us; the launch traced here: 275 us
  matrix products  129 us (47%)
  local copies, waits for them, and re-layouts  58.8 us (21%)
  other arithmetic  36.6 us (13%)
  waiting for transfers between devices  27.7 us (10%)
  starting transfers between devices  14.6 us (5%)
  loops' own time  7.72 us (3%)
    dot_general x7, matrix products, neighbour_products(): jnp.einsum('zyxrs,zyxsc->zyxrc', a_blocks[..., k * width:(k + 1) * width]...  79.3 us
    unnamed x26, local copies, waits for them, and re-layouts  41 us
    dot_general x4, matrix products, accumulate(): jnp.einsum('eyxrc,yxrk->eck', masked, slots, preferred_element_type=jnp.f...  35.9 us
    ppermute x1, waiting for transfers between devices, passed_along(): return lax.ppermute(block, axis, route)  27.7 us
    unnamed x5, other arithmetic  25.1 us
    concatenate x1, other arithmetic, route_slots(): return jnp.concatenate(slots, axis=-1).astype(jnp.bfloat16)  8.33 us
    another operation x1, loops' own time, per_device(): running = lax.fori_loop(0, layers, accumulate, start)  7.72 us
    ppermute x2, starting transfers between devices, with_halo(): lax.ppermute(lax.slice_in_dim(block, 0, width, axis=dim), axis, backward)  6.05 us
  transfers between devices with their start and end apart: 5, of which 1 were waited for; matrix products, arithmetic and copies ran while one was open for 38% of the time, Pallas kernels for 0%

commit v1 on v0

v1 whole, which is shorter than its diff:
```python
import functools
import jax
import jax.numpy as jnp
from jax import lax
from jax.experimental import pallas as pl
from jax.experimental.pallas import tpu as pltpu
from jax.sharding import PartitionSpec as P

F32, BF16 = jnp.float32, jnp.bfloat16
LANES = 128
CHUNKS = 2
STEP = 4
LIMIT = 36 << 20


def vmem_block(shape, index):
    return pl.BlockSpec(shape, lambda *grid: index)


def scalars():
    return pl.BlockSpec(memory_space=pltpu.SMEM)


def shifted(block, axis, distance):
    devices = range(lax.axis_size(axis))
    route = [(i, i + distance) for i in devices if i + distance in devices]
    return lax.ppermute(block, axis, route)


def matmul(left, right):
    return jnp.dot(left, right, preferred_element_type=F32)


def transposed_matmul(left, right):
    return lax.dot_general(left, right, (((0,), (0,)), ((), ())), preferred_element_type=F32)


def interval_of(xlen_ref, group, column):
    end, found = 0, 0
    for i in range(xlen_ref.shape[1]):
        end = end + xlen_ref[group, i]
        found = found + jnp.where(column >= end, 1, 0)
    return found


def aligned(low, high, end):
    return low // LANES * LANES, min(-(-high // LANES) * LANES, end)


def factor(flag, shape):
    return jnp.full(shape, jnp.where(flag, 1.0, 0.0), F32).astype(BF16)


def diagonal(blocks, low, first, high):
    rows, columns = blocks[0].shape
    parts = []
    if first > low:
        parts.append(jnp.zeros((first - low, columns * len(blocks)), BF16))
    none = jnp.zeros((rows, columns), BF16)
    for i, block in enumerate(blocks):
        parts.append(jnp.concatenate([block if i == j else none for j in range(len(blocks))], axis=1))
    end = first + rows * len(blocks)
    if high > end:
        parts.append(jnp.zeros((high - end, columns * len(blocks)), BF16))
    return jnp.concatenate(parts, axis=0)


def pack_kernel(a_ref, top_ref, left_ref, right_ref, *outs):
    messages, (left_out, right_out) = outs[:-2], outs[-2:]
    depth, columns, block = top_ref.shape[1:4]
    each = columns // len(messages)
    for c, out in enumerate(messages):

        def body(i, _, c=c, out=out):
            at = c * each + 2 * i
            out[:, pl.ds(2 * i, 2)] = top_ref[0, :, pl.ds(at, 2)]
            for y in range(depth):
                pair = [a_ref[0, y, at + j, :, :block] for j in range(2)]
                out[y, each + i] = jnp.concatenate(pair, axis=-1)
            return 0

        lax.fori_loop(0, each // 2, body, 0)
    left_out[...] = left_ref[:, :, 0]
    right_out[...] = right_ref[:, :, 0]


def pack(a_blocks, prolong):
    layers, depth, columns, block, coarse = prolong.shape
    each = columns // CHUNKS
    low, _ = aligned(6 * block, 7 * block, 7 * block)
    message = jax.ShapeDtypeStruct((depth, each + each // 2, block, coarse), BF16)
    edge = jax.ShapeDtypeStruct((layers, depth, block, coarse), BF16)
    return pl.pallas_call(
        pack_kernel,
        grid=(1,),
        in_specs=[
            vmem_block((1, depth, columns, block, LANES), (layers - 1, 0, 0, 0, low // LANES)),
            vmem_block((1, depth, columns, block, coarse), (layers - 1, 0, 0, 0, 0)),
            vmem_block((layers, depth, 1, block, coarse), (0, 0, 0, 0, 0)),
            vmem_block((layers, depth, 1, block, coarse), (0, 0, columns - 1, 0, 0)),
        ],
        out_specs=[vmem_block(message.shape, (0,) * 4)] * CHUNKS + [vmem_block(edge.shape, (0,) * 4)] * 2,
        out_shape=[message] * CHUNKS + [edge] * 2,
        compiler_params=pltpu.CompilerParams(vmem_limit_bytes=LIMIT),
        name="pack",
    )(a_blocks, prolong, prolong, prolong)


def main_kernel(halves, zagg_ref, xlen_ref, a_ref, p_ref, left_ref, right_ref, sums_ref, early_ref):
    layers, depth, columns, block, coarse = p_ref.shape
    wide = a_ref.shape[-1]
    step = a_ref.shape[2]
    shape = (block, coarse)
    dom, grp = lax.axis_index("dom"), lax.axis_index("grp")
    layer = pl.program_id(0)

    @pl.when((pl.program_id(0) == 0) & (pl.program_id(1) == 0))
    def _():
        def clear(i, _):
            for target in range(sums_ref.shape[0]):
                sums_ref[target, i] = jnp.zeros(sums_ref.shape[2:], F32)
            return 0

        lax.fori_loop(0, sums_ref.shape[1], clear, 0)

    at = dom * layers + layer
    mine = zagg_ref[at]
    target = mine - dom * halves + 1
    has_zm, has_zp = layer > 0, layer < layers - 1
    below = jnp.where(has_zm, layer - 1, 0)
    above = jnp.where(has_zp, layer + 1, layer)
    same_zm = has_zm & (zagg_ref[jnp.where(has_zm, at - 1, at)] == mine)
    same_zp = has_zp & (zagg_ref[jnp.where(has_zp, at + 1, at)] == mine)
    apart_zm = has_zm & jnp.logical_not(same_zm)
    apart_zp = has_zp & jnp.logical_not(same_zp)
    none = jnp.zeros(shape, BF16)

    def beside(x):
        has_xm, has_xp = x > 0, x < columns - 1
        before, after = jnp.where(has_xm, x - 1, 0), jnp.where(has_xp, x + 1, x)
        interval = interval_of(xlen_ref, grp, x)
        same_xm = has_xm & (interval_of(xlen_ref, grp, before) == interval)
        same_xp = has_xp & (interval_of(xlen_ref, grp, after) == interval)
        return interval, has_xm, has_xp, before, after, same_xm, same_xp

    def own(x):
        return p_ref[layer, :, x].reshape(depth * block, coarse)

    def pair(q, _):
        first = pl.program_id(1) * step + 2 * q
        info = [beside(first + j) for j in range(2)]
        zm_factor, zp_factor = factor(same_zm, shape), factor(same_zp, shape)
        factors = [(factor(i[5], shape), factor(i[6], shape)) for i in info]
        rows = [[], []]
        for y in range(depth):
            stacks = []
            for j in range(2):
                x, (_, _, _, before, after, _, _) = first + j, info[j]
                stacks.append(
                    jnp.concatenate(
                        [
                            p_ref[layer, y, x],
                            p_ref[layer, y, before] * factors[j][0],
                            p_ref[layer, y, after] * factors[j][1],
                            p_ref[layer, y - 1, x] if y > 0 else none,
                            p_ref[layer, y + 1, x] if y < depth - 1 else none,
                            p_ref[below, y, x] * zm_factor,
                            p_ref[above, y, x] * zp_factor,
                        ],
                        axis=0,
                    )
                )
            left = a_ref[0, y, pl.ds(2 * q, 2)].reshape(2 * block, wide)
            both = matmul(left, jnp.concatenate(stacks, axis=1))
            for j in range(2):
                rows[j].append(
                    both[j * block : (j + 1) * block, j * coarse : (j + 1) * coarse].astype(BF16)
                )
        for j in range(2):
            sums_ref[target, info[j][0], :, :coarse] += transposed_matmul(
                own(first + j), jnp.concatenate(rows[j], axis=0)
            )
        return 0

    lax.fori_loop(0, step // 2, pair, 0)

    def split(i, x, interval, slot, k, blocks):
        low, high = aligned(k * block, (k + 2) * block, wide)
        rows = []
        for y in range(depth):
            right = diagonal(blocks(y), low, k * block, high)
            rows.append(matmul(a_ref[0, y, i, :, low:high], right).astype(BF16))
        lanes = slice(slot * coarse, (slot + 2) * coarse)
        sums_ref[target, interval, :, lanes] += transposed_matmul(own(x), jnp.concatenate(rows, axis=0))

    def along_x(i, _):
        x = pl.program_id(1) * step + i
        interval, has_xm, has_xp, before, after, same_xm, same_xp = beside(x)

        @pl.when(jnp.logical_not(same_xm & same_xp))
        def _():
            inner_xm = factor(has_xm & jnp.logical_not(same_xm), shape)
            inner_xp = factor(has_xp & jnp.logical_not(same_xp), shape)
            outer_xm, outer_xp = factor(jnp.logical_not(has_xm), shape), factor(jnp.logical_not(has_xp), shape)
            split(
                i,
                x,
                interval,
                1,
                1,
                lambda y: [
                    p_ref[layer, y, before] * inner_xm + left_ref[layer, y] * outer_xm,
                    p_ref[layer, y, after] * inner_xp + right_ref[layer, y] * outer_xp,
                ],
            )

        return 0

    lax.fori_loop(0, step, along_x, 0)

    @pl.when(apart_zm | apart_zp)
    def _():
        zm_factor, zp_factor = factor(apart_zm, shape), factor(apart_zp, shape)

        def along_z(i, _):
            x = pl.program_id(1) * step + i
            split(
                i,
                x,
                interval_of(xlen_ref, grp, x),
                3,
                5,
                lambda y: [p_ref[below, y, x] * zm_factor, p_ref[above, y, x] * zp_factor],
            )
            return 0

        lax.fori_loop(0, step, along_z, 0)

    @pl.when((layer == layers - 1) & (pl.program_id(1) == pl.num_programs(1) - 1))
    def _():
        def emit(i, _):
            early_ref[i, :, : 2 * coarse] = sums_ref[0, i, :, coarse : 3 * coarse].astype(BF16)
            early_ref[i, :, 2 * coarse :] = sums_ref[0, i, :, 4 * coarse :].astype(BF16)
            return 0

        lax.fori_loop(0, early_ref.shape[0], emit, 0)


def main(halves, zagg, xlen, a_blocks, prolong, left, right):
    layers, depth, columns, block, coarse = prolong.shape
    intervals = xlen.shape[1]
    sums = jax.ShapeDtypeStruct((halves + 1, intervals, coarse, 5 * coarse), F32)
    early = jax.ShapeDtypeStruct((intervals, coarse, 3 * coarse), BF16)
    step = STEP if columns % STEP == 0 else 2

    def whole(shape):
        return pl.BlockSpec(shape, lambda *grid: (0,) * len(shape), pipeline_mode=pl.Buffered(1))

    flops = layers * columns * depth * 2 * block * coarse * 12 * block
    return pl.pallas_call(
        functools.partial(main_kernel, halves),
        grid=(layers, columns // step),
        in_specs=[
            scalars(),
            scalars(),
            pl.BlockSpec((1, depth, step, block, a_blocks.shape[-1]), lambda i, j: (i, 0, j, 0, 0)),
            whole(prolong.shape),
            whole(left.shape),
            whole(right.shape),
        ],
        out_specs=[vmem_block(sums.shape, (0,) * 4), vmem_block(early.shape, (0,) * 3)],
        out_shape=[sums, early],
        cost_estimate=pl.CostEstimate(flops=flops * 4, bytes_accessed=40 << 20, transcendentals=0),
        compiler_params=pltpu.CompilerParams(vmem_limit_bytes=LIMIT),
        name="coarsen",
    )(zagg, xlen, a_blocks, prolong, left, right)


def boundary_kernel(chunk, last, zagg_ref, xlen_ref, message_ref, a_ref, p_ref, carried_ref, *rest):
    if chunk > 0:
        base_ref, rest = rest[0], rest[1:]
    depth, _, block, coarse = message_ref.shape
    each = p_ref.shape[2]
    dom, grp = lax.axis_index("dom"), lax.axis_index("grp")
    sums_ref = rest[-1]
    sums_ref[...] = base_ref[...] if chunk > 0 else jnp.zeros_like(sums_ref)
    low, high = aligned(5 * block, 6 * block, 7 * block)

    def interval(q, j):
        return interval_of(xlen_ref, grp, chunk * each + 2 * q + j)

    def upper(q, _):
        rows = [[], []]
        for y in range(depth):
            mine = [p_ref[0, y, 2 * q + j] for j in range(2)]
            both = matmul(message_ref[y, each + q], diagonal(mine, 0, 0, 2 * block))
            for j in range(2):
                rows[j].append(both[:, j * coarse : (j + 1) * coarse].astype(BF16))
        for j in range(2):
            theirs = message_ref[:, 2 * q + j].reshape(depth * block, coarse)
            sums_ref[0, interval(q, j)] += transposed_matmul(theirs, jnp.concatenate(rows[j], axis=0))
        return 0

    def lower(q, _):
        rows = [[], []]
        for y in range(depth):
            theirs = jnp.concatenate([message_ref[y, 2 * q + j] for j in range(2)], axis=1)
            left = a_ref[0, y, pl.ds(2 * q, 2)].reshape(2 * block, high - low)
            both = matmul(left, diagonal([theirs], low, 5 * block, high))
            for j in range(2):
                rows[j].append(both[j * block : (j + 1) * block, j * coarse : (j + 1) * coarse].astype(BF16))
        for j in range(2):
            own = p_ref[0, :, 2 * q + j].reshape(depth * block, coarse)
            sums_ref[1, interval(q, j)] += transposed_matmul(own, jnp.concatenate(rows[j], axis=0))
        return 0

    lax.fori_loop(0, each // 2, upper, 0)
    lax.fori_loop(0, each // 2, lower, 0)
    if last:
        late_ref, owned_ref = rest[:2]
        layers = zagg_ref.shape[0] // lax.axis_size("dom")
        at = dom * layers
        same = (at > 0) & (zagg_ref[jnp.where(at > 0, at - 1, 0)] == zagg_ref[at])
        joined = jnp.where(same, 1.0, 0.0)
        late_ref[...] = (carried_ref[0] + sums_ref[0] + joined * sums_ref[1]).astype(BF16)
        owned_ref[...] = (1.0 - joined) * sums_ref[1]


def boundary(chunk, zagg, xlen, message, a_blocks, prolong, carried, base=None):
    layers, depth, columns, block, coarse = prolong.shape
    intervals = xlen.shape[1]
    each = columns // CHUNKS
    last = chunk == CHUNKS - 1
    low, high = aligned(5 * block, 6 * block, 7 * block)
    sums = jax.ShapeDtypeStruct((2, intervals, coarse, coarse), F32)
    in_specs = [
        scalars(),
        scalars(),
        vmem_block(message.shape, (0,) * 4),
        vmem_block((1, depth, each, block, high - low), (0, 0, chunk, 0, low // LANES)),
        vmem_block((1, depth, each, block, coarse), (0, 0, chunk, 0, 0)),
        vmem_block((1, intervals, coarse, coarse), (0,) * 4),
    ]
    operands = [zagg, xlen, message, a_blocks, prolong, carried]
    if base is not None:
        in_specs.append(vmem_block(sums.shape, (0,) * 4))
        operands.append(base)
    out_specs, out_shape, scratch = [vmem_block(sums.shape, (0,) * 4)], [sums], []
    if last:
        late = jax.ShapeDtypeStruct((intervals, coarse, coarse), BF16)
        owned = jax.ShapeDtypeStruct((intervals, coarse, coarse), F32)
        out_specs, out_shape = [vmem_block(late.shape, (0,) * 3)] * 2, [late, owned]
        scratch = [pltpu.VMEM(sums.shape, F32)]
    return pl.pallas_call(
        functools.partial(boundary_kernel, chunk, last),
        grid=(1,),
        in_specs=in_specs,
        out_specs=out_specs,
        out_shape=out_shape,
        scratch_shapes=scratch,
        compiler_params=pltpu.CompilerParams(vmem_limit_bytes=LIMIT),
        name="boundary_" + str(chunk),
    )(*operands)


def final_kernel(zagg_ref, sums_ref, owned_ref, early_ref, late_ref, out_ref):
    coarse = sums_ref.shape[2]
    dom = lax.axis_index("dom")
    layers = zagg_ref.shape[0] // lax.axis_size("dom")
    half, halves = pl.program_id(0), pl.num_programs(0)
    first = jnp.where(half == 0, 1.0, 0.0)
    last = jnp.where(half == halves - 1, 1.0, 0.0)
    end = (dom + 1) * layers
    following = jnp.where(end < zagg_ref.shape[0], end, end - 1)
    joined = jnp.where(zagg_ref[following] == zagg_ref[end - 1], last, 0.0)

    def lanes(slot):
        return slice(slot * coarse, (slot + 1) * coarse)

    late = late_ref[...].astype(F32)

    def early(index):
        return last * early_ref[:, :, lanes(index)].astype(F32)

    out_ref[0, :, :, lanes(0)] = (sums_ref[0, :, :, lanes(0)] + joined * late).astype(BF16)
    out_ref[0, :, :, lanes(1)] = (sums_ref[0, :, :, lanes(1)] + early(0)).astype(BF16)
    out_ref[0, :, :, lanes(2)] = (sums_ref[0, :, :, lanes(2)] + early(1)).astype(BF16)
    out_ref[0, :, :, lanes(3)] = (sums_ref[0, :, :, lanes(3)] + first * owned_ref[...]).astype(BF16)
    out_ref[0, :, :, lanes(4)] = (
        sums_ref[0, :, :, lanes(4)] + early(2) + (last - joined) * late
    ).astype(BF16)


def final(halves, zagg, sums, owned, early, late):
    _, intervals, coarse, wide = sums.shape
    return pl.pallas_call(
        final_kernel,
        grid=(halves,),
        in_specs=[
            scalars(),
            pl.BlockSpec((1, intervals, coarse, wide), lambda h: (h + 1, 0, 0, 0)),
            vmem_block(owned.shape, (0,) * 3),
            vmem_block(early.shape, (0,) * 3),
            vmem_block(late.shape, (0,) * 3),
        ],
        out_specs=pl.BlockSpec((1, intervals, coarse, wide), lambda h: (h, 0, 0, 0)),
        out_shape=jax.ShapeDtypeStruct((halves, intervals, coarse, wide), BF16),
        name="finish",
    )(zagg, sums, owned, early, late)


def in_hbm(block):
    return pltpu.with_memory_space_constraint(block, pltpu.HBM)


def per_device(a_blocks, prolong, zagg, xlen):
    halves = prolong.shape[0] // 2
    *messages, left_edge, right_edge = pack(a_blocks, prolong)
    arrived = [in_hbm(shifted(message, "dom", 1)) for message in messages]
    left = in_hbm(shifted(right_edge, "grp", 1))
    right = in_hbm(shifted(left_edge, "grp", -1))
    sums, early = main(halves, zagg, xlen, a_blocks, prolong, left, right)
    early = in_hbm(shifted(early, "dom", -1))
    beyond = None
    for chunk, message in enumerate(arrived):
        outs = boundary(chunk, zagg, xlen, message, a_blocks, prolong, sums, beyond)
        beyond = outs[0]
    late, owned = outs
    late = in_hbm(shifted(late, "dom", -1))
    return final(halves, zagg, sums, owned, early, late)


def solution(mesh):
    in_specs = (P("dom", None, "grp", None, None), P("dom", None, "grp", None, None), P(), P())
    out_specs = P("dom", "grp", None, None)
    return jax.shard_map(per_device, mesh=mesh, in_specs=in_specs, out_specs=out_specs, check_vma=False)
```

time: 276 us -> 97 us (0.35)
  matrix products: 129 us -> 0 us
  Pallas kernels: 0 us -> 61.4 us
  local copies, waits for them, and re-layouts: 58.8 us -> 7.35 us
  other arithmetic: 36.6 us -> 0 us
  waiting for transfers between devices: 27.7 us -> 5.82 us
  loops' own time: 7.72 us -> 0 us
  starting transfers between devices: 14.6 us -> 21.9 us
    dot_general x15 -> x0, matrix products: 129 us -> none  [the longest x7 79.3 us: neighbour_products(): jnp.einsum('zyxrs,zyxsc->zyxrc', a_blocks[..., k * width:(k + 1) * width]...]
    pallas_call x0 -> x5, Pallas kernels: none -> 61.4 us  [the longest x1 48.2 us: main(): pl.pallas_call(functools.partial(main_kernel, halves), grid=(layers, colu...]
    unnamed x26 -> x22, local copies, waits for them, and re-layouts: 41 us -> 7.35 us
    unnamed x5 -> x0, other arithmetic: 25.1 us -> none
    ppermute x5 -> x6, waiting for transfers between devices: 27.7 us -> 5.82 us  [shifted(): return lax.ppermute(block, axis, route)]
    concatenate x2 -> x0, other arithmetic: 9.52 us -> none  [the longest x1 8.33 us: route_slots(): return jnp.concatenate(slots, axis=-1).astype(jnp.bfloat16)]
    another operation x1 -> x0, loops' own time: 7.72 us -> none  [per_device(): running = lax.fori_loop(0, layers, accumulate, start)]
    ppermute x5 -> x6, starting transfers between devices: 14.6 us -> 21.9 us  [shifted(): return lax.ppermute(block, axis, route)]
  transfers between devices with their start and end apart: 5 -> 6, of which waited for: 1 -> 1; matrix products, arithmetic and copies ran while one was open for 38% -> 0% of each run, Pallas kernels for 0% -> 58%
where the time goes in v1:
time: 97 us; the launch traced here: 96.6 us
  Pallas kernels  61.4 us (63%)
  starting transfers between devices  21.9 us (23%)
  local copies, waits for them, and re-layouts  7.35 us (8%)
  waiting for transfers between devices  5.82 us (6%)
    pallas_call x1, Pallas kernels, main(): pl.pallas_call(functools.partial(main_kernel, halves), grid=(layers, colu...  48.2 us
    ppermute x6, starting transfers between devices, shifted(): return lax.ppermute(block, axis, route)  21.9 us
    pallas_call x2, Pallas kernels, boundary(): pl.pallas_call(functools.partial(boundary_kernel, chunk, last), grid=(1,)...  8.14 us
    unnamed x22, local copies, waits for them, and re-layouts  7.35 us
    ppermute x6, waiting for transfers between devices, shifted(): return lax.ppermute(block, axis, route)  5.82 us
    pallas_call x1, Pallas kernels, final(): pl.pallas_call(final_kernel, grid=(halves,), in_specs=[scalars(), pl.Bloc...  3 us
    pallas_call x1, Pallas kernels, pack(): pl.pallas_call(pack_kernel, grid=(1,), in_specs=[vmem_block((1, depth, co...  2.08 us
  transfers between devices with their start and end apart: 6, of which 1 were waited for; matrix products, arithmetic and copies ran while one was open for 0% of the time, Pallas kernels for 58%

profile of v1, /device:TPU:14, one launch (start us, length us, event | category | flops | bytes accessed | tf_op | source)
XLA Modules:
  0.0 96.6 jit_solution(15509431144556326257)
XLA Ops:
  0.0 2.6 %copy-done = bf16[4,7,12,64,128]{4,3,2,1,0:T(8,128)(2,1)S(1)} copy-done((bf16[4,7,12,64,128]{4,3,2,1,0:T(8,128)(2,1)S(1)}, bf16[4,7,12,64,128]{4,3,2,1,0:T(8,128)(2,1)}, u32[]{:S(2)}) %copy-start) | copy-done | bytes 5505048
  2.6 2.1 %pack.1 = (bf16[7,9,64,128]{3,2,1,0:T(8,128)(2,1)S(1)}, bf16[7,9,64,128]{3,2,1,0:T(8,128)(2,1)S(1)}, bf16[4,7,64,128]{3,2,1,0:T(8,128)(2,1)S(1)}, bf16[4,7,64,128]{3,2,1,0:T(8,128)(2,1)S(1)}) custom-call(bf16[4,7,12,64,448]{4,3,2,1,0:T(8,128)(2,1)} %a_ref.7, bf16[4,7,12,64,128]{4,3,2,1,0:T(8,128)(2,1)S(1)} %copy-done, ...), custom_call_target="tpu_custom_call" | custom-call | tf_op jit(solution)/shard_map/pack/pallas_call | solution.py:93
  4.7 1.9 %collective-permute-start = (bf16[4,7,64,128]{3,2,1,0:T(8,128)(2,1)S(1)}, bf16[4,7,64,128]{3,2,1,0:T(8,128)(2,1)S(1)}, u32[]{:S(2)}, u32[]{:S(2)}) collective-permute-start(bf16[4,7,64,128]{3,2,1,0:T(8,128)(2,1)S(1)} %get-tuple-element.13), channel_id=1, source_target_pairs={{0,1},{1,2},{2,3},{4,5},{5,6},{6,7},{8,9},{9,10},{10,11},{12,13},{... | collective-permute-start | bytes 1376264 | tf_op jit(solution)/shard_map/ppermute | solution.py:27
  6.6 3.6 %collective-permute-start.1 = (bf16[4,7,64,128]{3,2,1,0:T(8,128)(2,1)S(1)}, bf16[4,7,64,128]{3,2,1,0:T(8,128)(2,1)S(1)}, u32[]{:S(2)}, u32[]{:S(2)}) collective-permute-start(bf16[4,7,64,128]{3,2,1,0:T(8,128)(2,1)S(1)} %get-tuple-element.14), channel_id=1, source_target_pairs={{1,0},{2,1},{3,2},{5,4},{6,5},{7,6},{9,8},{10,9},{11,10},{13,12},{... | collective-permute-start | bytes 1376264 | tf_op jit(solution)/shard_map/ppermute | solution.py:27
  10.2 3.4 %collective-permute-start.2 = (bf16[7,9,64,128]{3,2,1,0:T(8,128)(2,1)S(1)}, bf16[7,9,64,128]{3,2,1,0:T(8,128)(2,1)S(1)}, u32[]{:S(2)}, u32[]{:S(2)}) collective-permute-start(bf16[7,9,64,128]{3,2,1,0:T(8,128)(2,1)S(1)} %get-tuple-element.16), channel_id=1, source_target_pairs={{0,4},{4,8},{8,12},{12,16},{16,20},{20,24},{24,28},{1,5},{5,9},{9,... | collective-permute-start | bytes 3096584 | tf_op jit(solution)/shard_map/ppermute | solution.py:27
  13.7 3.4 %collective-permute-start.3 = (bf16[7,9,64,128]{3,2,1,0:T(8,128)(2,1)S(1)}, bf16[7,9,64,128]{3,2,1,0:T(8,128)(2,1)S(1)}, u32[]{:S(2)}, u32[]{:S(2)}) collective-permute-start(bf16[7,9,64,128]{3,2,1,0:T(8,128)(2,1)S(1)} %get-tuple-element.17), channel_id=1, source_target_pairs={{0,4},{4,8},{8,12},{12,16},{16,20},{20,24},{24,28},{1,5},{5,9},{9,... | collective-permute-start | bytes 3096584 | tf_op jit(solution)/shard_map/ppermute | solution.py:27
  17.1 0.0 collective-permute-done.left_ref
  17.1 0.0 copy-start.9
  17.1 0.0 collective-permute-done.1.right_ref
  17.1 0.7 copy-done.9
  17.9 0.8 copy-done.10
  18.7 48.2 %coarsen.1 = (f32[3,4,128,640]{3,2,1,0:T(8,128)S(1)}, bf16[4,128,384]{2,1,0:T(8,128)(2,1)S(1)}) custom-call(s32[32]{0:T(128)S(1)} %copy-done.4, s32[4,4]{1,0:T(4,128)S(1)} %copy-done.3, bf16[4,7,12,64,448]{4,3,2,1,0:T(8,128)(2,1)} %a_ref.7, bf16[4,7,12,64,128]{4,3,2,1,0:T(8,128)(2,1)S(1)} %copy-done, bf16[4,7,64,128]{3,2,1,0:T(8,128)(2,1)} %copy-done.9, ...), custom_call_target="tpu_custom_call" | custom-call | flops 16911433728 | bytes 41943040 | tf_op jit(solution)/shard_map/coarsen/pallas_call | solution.py:260
  66.9 7.5 %collective-permute-start.4 = (bf16[4,128,384]{2,1,0:T(8,128)(2,1)S(1)}, bf16[4,128,384]{2,1,0:T(8,128)(2,1)S(1)}, u32[]{:S(2)}, u32[]{:S(2)}) collective-permute-start(bf16[4,128,384]{2,1,0:T(8,128)(2,1)S(1)} %get-tuple-element.19), channel_id=1, source_target_pairs={{4,0},{8,4},{12,8},{16,12},{20,16},{24,20},{28,24},{5,1},{9,5},{13... | collective-permute-start | bytes 1179656 | tf_op jit(solution)/shard_map/ppermute | solution.py:27
  74.4 0.0 copy-start.6
  74.4 1.0 copy-done.6
  75.4 4.0 %boundary_0.1.rest_0_ = f32[2,4,128,128]{3,2,1,0:T(8,128)S(1)} custom-call(s32[32]{0:T(128)S(1)} %copy-done.4, s32[4,4]{1,0:T(4,128)S(1)} %copy-done.3, bf16[7,9,64,128]{3,2,1,0:T(8,128)(2,1)} %copy-done.6, bf16[4,7,12,64,448]{4,3,2,1,0:T(8,128)(2,1)} %a_ref.7, bf16[4,7,12,64,128]{4,3,2,1,0:T(8,128)(2,1)S(1)} %copy-done, ...), custom_call_target="tpu_custom_call" | custom-call | tf_op jit(solution)/shard_map/boundary_0/pallas_call | solution.py:354
  79.5 0.0 copy-start.5
  79.5 1.0 copy-done.5
  80.4 4.1 %boundary_1.1 = (bf16[4,128,128]{2,1,0:T(8,128)(2,1)S(1)}, f32[4,128,128]{2,1,0:T(8,128)S(1)}) custom-call(s32[32]{0:T(128)S(1)} %copy-done.4, s32[4,4]{1,0:T(4,128)S(1)} %copy-done.3, bf16[7,9,64,128]{3,2,1,0:T(8,128)(2,1)} %copy-done.5, bf16[4,7,12,64,448]{4,3,2,1,0:T(8,128)(2,1)} %a_ref.7, bf16[4,7,12,64,128]{4,3,2,1,0:T(8,128)(2,1)S(1)} %copy-done, ...), custom_call_target="tpu_custom_call" | custom-call | tf_op jit(solution)/shard_map/boundary_1/pallas_call | solution.py:354
  84.5 0.7 copy-done.2
  85.2 1.9 %collective-permute-start.5 = (bf16[4,128,128]{2,1,0:T(8,128)(2,1)S(1)}, bf16[4,128,128]{2,1,0:T(8,128)(2,1)S(1)}, u32[]{:S(2)}, u32[]{:S(2)}) collective-permute-start(bf16[4,128,128]{2,1,0:T(8,128)(2,1)S(1)} %get-tuple-element.20), channel_id=1, source_target_pairs={{4,0},{8,4},{12,8},{16,12},{20,16},{24,20},{28,24},{5,1},{9,5},{13... | collective-permute-start | bytes 393224 | tf_op jit(solution)/shard_map/ppermute | solution.py:27
  87.2 5.8 %collective-permute-done.5.late_ref = bf16[4,128,128]{2,1,0:T(8,128)(2,1)S(1)} collective-permute-done((bf16[4,128,128]{2,1,0:T(8,128)(2,1)S(1)}, bf16[4,128,128]{2,1,0:T(8,128)(2,1)S(1)}, u32[]{:S(2)}, u32[]{:S(2)}) %collective-permute-start.5) | collective-permute-done | bytes 131104 | tf_op jit(solution)/shard_map/ppermute | solution.py:27
  93.0 0.6 copy-done.8
  93.6 3.0 %finish.1 = bf16[2,4,128,640]{3,2,1,0:T(8,128)(2,1)} custom-call(s32[32]{0:T(128)} %zagg_ref.7, f32[3,4,128,640]{3,2,1,0:T(8,128)} %copy-done.1, f32[4,128,128]{2,1,0:T(8,128)} %copy-done.2, bf16[4,128,384]{2,1,0:T(8,128)(2,1)} %copy-done.7, bf16[4,128,128]{2,1,0:T(8,128)(2,1)} %copy-done.8), custom_call_target="tpu_custom_call" | custom-call | tf_op jit(solution)/shard_map/finish/pallas_call | solution.py:396
  (15 shorter events, 0.0 us)
Async XLA Ops:
  0.0 2.6 %copy-start = (bf16[4,7,12,64,128]{4,3,2,1,0:T(8,128)(2,1)S(1)}, bf16[4,7,12,64,128]{4,3,2,1,0:T(8,128)(2,1)}, u32[]{:S(2)}) copy-start(bf16[4,7,12,64,128]{4,3,2,1,0:T(8,128)(2,1)} %p_ref.5) | copy-start | bytes 16515076
  2.6 16.1 %copy-start.3 = (s32[4,4]{1,0:T(4,128)S(1)}, s32[4,4]{1,0:T(4,128)}, u32[]{:S(2)}) copy-start(s32[4,4]{1,0:T(4,128)} %xlen_ref.5) | copy-start | bytes 196
  2.6 16.1 %copy-start.4 = (s32[32]{0:T(128)S(1)}, s32[32]{0:T(128)}, u32[]{:S(2)}) copy-start(s32[32]{0:T(128)} %zagg_ref.7) | copy-start | bytes 388
  4.7 12.5 %collective-permute-start = (bf16[4,7,64,128]{3,2,1,0:T(8,128)(2,1)S(1)}, bf16[4,7,64,128]{3,2,1,0:T(8,128)(2,1)S(1)}, u32[]{:S(2)}, u32[]{:S(2)}) collective-permute-start(bf16[4,7,64,128]{3,2,1,0:T(8,128)(2,1)S(1)} %get-tuple-element.13), channel_id=1, source_target_pairs={{0,1},{1,2},{2,3},{4,5},{5,6},{6,7},{8,9},{9,10},{10,11},{12,13},{... | collective-permute-start | bytes 1376264 | tf_op jit(solution)/shard_map/ppermute | solution.py:27
  6.6 10.5 %collective-permute-start.1 = (bf16[4,7,64,128]{3,2,1,0:T(8,128)(2,1)S(1)}, bf16[4,7,64,128]{3,2,1,0:T(8,128)(2,1)S(1)}, u32[]{:S(2)}, u32[]{:S(2)}) collective-permute-start(bf16[4,7,64,128]{3,2,1,0:T(8,128)(2,1)S(1)} %get-tuple-element.14), channel_id=1, source_target_pairs={{1,0},{2,1},{3,2},{5,4},{6,5},{7,6},{9,8},{10,9},{11,10},{13,12},{... | collective-permute-start | bytes 1376264 | tf_op jit(solution)/shard_map/ppermute | solution.py:27
  10.2 69.2 %collective-permute-start.2 = (bf16[7,9,64,128]{3,2,1,0:T(8,128)(2,1)S(1)}, bf16[7,9,64,128]{3,2,1,0:T(8,128)(2,1)S(1)}, u32[]{:S(2)}, u32[]{:S(2)}) collective-permute-start(bf16[7,9,64,128]{3,2,1,0:T(8,128)(2,1)S(1)} %get-tuple-element.16), channel_id=1, source_target_pairs={{0,4},{4,8},{8,12},{12,16},{16,20},{20,24},{24,28},{1,5},{5,9},{9,... | collective-permute-start | bytes 3096584 | tf_op jit(solution)/shard_map/ppermute | solution.py:27
  13.7 60.7 %collective-permute-start.3 = (bf16[7,9,64,128]{3,2,1,0:T(8,128)(2,1)S(1)}, bf16[7,9,64,128]{3,2,1,0:T(8,128)(2,1)S(1)}, u32[]{:S(2)}, u32[]{:S(2)}) collective-permute-start(bf16[7,9,64,128]{3,2,1,0:T(8,128)(2,1)S(1)} %get-tuple-element.17), channel_id=1, source_target_pairs={{0,4},{4,8},{8,12},{12,16},{16,20},{20,24},{24,28},{1,5},{5,9},{9,... | collective-permute-start | bytes 3096584 | tf_op jit(solution)/shard_map/ppermute | solution.py:27
  17.1 0.8 copy-start.9
  17.9 0.8 copy-start.10
  66.9 12.6 %copy-start.1 = (f32[3,4,128,640]{3,2,1,0:T(8,128)}, f32[3,4,128,640]{3,2,1,0:T(8,128)S(1)}, u32[]{:S(2)}) copy-start(f32[3,4,128,640]{3,2,1,0:T(8,128)S(1)} %get-tuple-element.15.carried_ref.sums_ref) | copy-start | bytes 11796484
  66.9 20.3 %collective-permute-start.4 = (bf16[4,128,384]{2,1,0:T(8,128)(2,1)S(1)}, bf16[4,128,384]{2,1,0:T(8,128)(2,1)S(1)}, u32[]{:S(2)}, u32[]{:S(2)}) collective-permute-start(bf16[4,128,384]{2,1,0:T(8,128)(2,1)S(1)} %get-tuple-element.19), channel_id=1, source_target_pairs={{4,0},{8,4},{12,8},{16,12},{20,16},{24,20},{28,24},{5,1},{9,5},{13... | collective-permute-start | bytes 1179656 | tf_op jit(solution)/shard_map/ppermute | solution.py:27
  74.4 1.0 copy-start.6
  79.5 1.0 copy-start.5
  84.5 0.7 copy-start.2
  85.2 7.7 %collective-permute-start.5 = (bf16[4,128,128]{2,1,0:T(8,128)(2,1)S(1)}, bf16[4,128,128]{2,1,0:T(8,128)(2,1)S(1)}, u32[]{:S(2)}, u32[]{:S(2)}) collective-permute-start(bf16[4,128,128]{2,1,0:T(8,128)(2,1)S(1)} %get-tuple-element.20), channel_id=1, source_target_pairs={{4,0},{8,4},{12,8},{16,12},{20,16},{24,20},{28,24},{5,1},{9,5},{13... | collective-permute-start | bytes 393224 | tf_op jit(solution)/shard_map/ppermute | solution.py:27
  87.2 5.8 %copy-start.7 = (bf16[4,128,384]{2,1,0:T(8,128)(2,1)}, bf16[4,128,384]{2,1,0:T(8,128)(2,1)S(1)}, u32[]{:S(2)}) copy-start(bf16[4,128,384]{2,1,0:T(8,128)(2,1)S(1)} %collective-permute-done.4.early_ref) | copy-start | bytes 1179652
  93.0 0.7 copy-start.8

commit v2 on v1

v2 whole, which is shorter than its diff:
```python
import functools
import jax
import jax.numpy as jnp
from jax import lax
from jax.experimental import pallas as pl
from jax.experimental.pallas import tpu as pltpu
from jax.sharding import PartitionSpec as P


F32, BF16 = jnp.float32, jnp.bfloat16
LANES = 128
CHUNKS = 2
LIMIT = 36 << 20


def vmem_block(shape, index):
    return pl.BlockSpec(shape, lambda *grid: index)


def scalars():
    return pl.BlockSpec(memory_space=pltpu.SMEM)


def in_vmem():
    return pl.BlockSpec(memory_space=pltpu.VMEM)


def shifted(block, axis, distance):
    devices = range(lax.axis_size(axis))
    route = [(i, i + distance) for i in devices if i + distance in devices]
    return lax.ppermute(block, axis, route)


def matmul(left, right):
    return jnp.dot(left, right, preferred_element_type=F32)


def transposed_matmul(left, right):
    return lax.dot_general(left, right, (((0,), (0,)), ((), ())), preferred_element_type=F32)


def interval_of(xlen_ref, group, column):
    end, found = 0, 0
    for i in range(xlen_ref.shape[1]):
        end = end + xlen_ref[group, i]
        found = found + jnp.where(column >= end, 1, 0)
    return found


def aligned(low, high, end):
    return low // LANES * LANES, min(-(-high // LANES) * LANES, end)


def factor(flag, shape):
    return jnp.full(shape, jnp.where(flag, 1.0, 0.0), F32).astype(BF16)


def diagonal(blocks, low, first, high):
    rows, columns = blocks[0].shape
    parts = []
    if first > low:
        parts.append(jnp.zeros((first - low, columns * len(blocks)), BF16))
    none = jnp.zeros((rows, columns), BF16)
    for i, block in enumerate(blocks):
        parts.append(jnp.concatenate([block if i == j else none for j in range(len(blocks))], axis=1))
    end = first + rows * len(blocks)
    if high > end:
        parts.append(jnp.zeros((high - end, columns * len(blocks)), BF16))
    return jnp.concatenate(parts, axis=0)


def pack_kernel(a_ref, top_ref, left_ref, right_ref, *outs):
    messages, (left_out, right_out) = outs[:-2], outs[-2:]
    depth, columns, block = top_ref.shape[1:4]
    each = columns // len(messages)
    for c, out in enumerate(messages):

        def body(i, _, c=c, out=out):
            at = c * each + 2 * i
            out[:, pl.ds(2 * i, 2)] = top_ref[0, :, pl.ds(at, 2)]
            for y in range(depth):
                pair = [a_ref[0, y, at + j, :, :block] for j in range(2)]
                out[y, each + i] = jnp.concatenate(pair, axis=-1)
            return 0

        lax.fori_loop(0, each // 2, body, 0)
    left_out[...] = left_ref[:, :, 0]
    right_out[...] = right_ref[:, :, 0]


def pack(a_blocks, prolong):
    layers, depth, columns, block, coarse = prolong.shape
    each = columns // CHUNKS
    low, _ = aligned(6 * block, 7 * block, 7 * block)
    message = jax.ShapeDtypeStruct((depth, each + each // 2, block, coarse), BF16)
    edge = jax.ShapeDtypeStruct((layers, depth, block, coarse), BF16)
    return pl.pallas_call(
        pack_kernel,
        grid=(1,),
        in_specs=[
            vmem_block((1, depth, columns, block, LANES), (layers - 1, 0, 0, 0, low // LANES)),
            vmem_block((1, depth, columns, block, coarse), (layers - 1, 0, 0, 0, 0)),
            vmem_block((layers, depth, 1, block, coarse), (0, 0, 0, 0, 0)),
            vmem_block((layers, depth, 1, block, coarse), (0, 0, columns - 1, 0, 0)),
        ],
        out_specs=[vmem_block(message.shape, (0,) * 4)] * CHUNKS + [vmem_block(edge.shape, (0,) * 4)] * 2,
        out_shape=[message] * CHUNKS + [edge] * 2,
        compiler_params=pltpu.CompilerParams(vmem_limit_bytes=LIMIT),
        name="pack",
    )(a_blocks, prolong, prolong, prolong)


def main_kernel(halves, zagg_ref, xlen_ref, a_ref, p_ref, left_ref, right_ref, sums_ref, early_ref, rows_ref):
    layers, depth, columns, block, coarse = p_ref.shape
    intervals = sums_ref.shape[1]
    wide = a_ref.shape[-1]
    shape = (block, coarse)
    dom, grp = lax.axis_index("dom"), lax.axis_index("grp")
    layer = pl.program_id(0)

    @pl.when(layer == 0)
    def _():
        def clear(i, _):
            for target in range(sums_ref.shape[0]):
                sums_ref[target, i] = jnp.zeros(sums_ref.shape[2:], F32)
            return 0

        lax.fori_loop(0, intervals, clear, 0)

    rows_ref[...] = jnp.zeros_like(rows_ref)

    at = dom * layers + layer
    mine = zagg_ref[at]
    target = mine - dom * halves + 1
    has_zm, has_zp = layer > 0, layer < layers - 1
    below = jnp.where(has_zm, layer - 1, 0)
    above = jnp.where(has_zp, layer + 1, layer)
    same_zm = has_zm & (zagg_ref[jnp.where(has_zm, at - 1, at)] == mine)
    same_zp = has_zp & (zagg_ref[jnp.where(has_zp, at + 1, at)] == mine)
    none = jnp.zeros(shape, BF16)

    def settle(pending):
        for j in range(2):
            x, interval, slot = pending[j]
            own = p_ref[layer, :, x].reshape(depth * block, coarse)
            sums_ref[target, interval, slot] += transposed_matmul(own, rows_ref[j])

    def keep(products):
        for y, both in enumerate(products):
            for j in range(2):
                part = both[j * block : (j + 1) * block, j * coarse : (j + 1) * coarse]
                rows_ref[j, y * block : (y + 1) * block] = part.astype(BF16)

    def inner(q, pending):
        settle(pending)
        zm_factor, zp_factor = factor(same_zm, shape), factor(same_zp, shape)
        info = []
        for j in range(2):
            x = 2 * q + j
            has_xm, has_xp = x > 0, x < columns - 1
            before, after = jnp.where(has_xm, x - 1, 0), jnp.where(has_xp, x + 1, x)
            interval = interval_of(xlen_ref, grp, x)
            same_xm = has_xm & (interval_of(xlen_ref, grp, before) == interval)
            same_xp = has_xp & (interval_of(xlen_ref, grp, after) == interval)
            info.append((x, interval, before, after, factor(same_xm, shape), factor(same_xp, shape)))
        products = []
        for y in range(depth):
            stacks = []
            for x, _, before, after, xm_factor, xp_factor in info:
                stacks.append(
                    jnp.concatenate(
                        [
                            p_ref[layer, y, x],
                            p_ref[layer, y, before] * xm_factor,
                            p_ref[layer, y, after] * xp_factor,
                            p_ref[layer, y - 1, x] if y > 0 else none,
                            p_ref[layer, y + 1, x] if y < depth - 1 else none,
                            p_ref[below, y, x] * zm_factor,
                            p_ref[above, y, x] * zp_factor,
                        ],
                        axis=0,
                    )
                )
            left = a_ref[0, y, pl.ds(2 * q, 2)].reshape(2 * block, wide)
            products.append(matmul(left, jnp.concatenate(stacks, axis=1)))
        keep(products)
        return tuple((i[0], i[1], jnp.int32(0)) for i in info)

    def across_x(i, pending):
        settle(pending)
        low, high = aligned(block, 3 * block, wide)
        end = 0
        for n in range(intervals):
            end = end + jnp.where(n <= i, xlen_ref[grp, n], 0)
        inside = end < columns
        x0, x1 = end - 1, jnp.where(inside, end, 0)
        within, beyond = factor(inside, shape), factor(jnp.logical_not(inside), shape)
        products = []
        for y in range(depth):
            before = p_ref[layer, y, x0] * within + left_ref[layer, y] * beyond
            after = p_ref[layer, y, x1] * within + right_ref[layer, y] * beyond
            stack = jnp.concatenate(
                [
                    jnp.zeros((block - low, 2 * coarse), BF16),
                    jnp.concatenate([none, before], axis=1),
                    jnp.concatenate([after, none], axis=1),
                    jnp.zeros((high - 3 * block, 2 * coarse), BF16),
                ],
                axis=0,
            )
            left = jnp.concatenate([a_ref[0, y, x0, :, low:high], a_ref[0, y, x1, :, low:high]], axis=0)
            products.append(matmul(left, stack))
        keep(products)
        return ((x0, i, jnp.int32(2)), (x1, jnp.where(i < intervals - 1, i + 1, 0), jnp.int32(1)))

    def across_z(k, slot, other):
        low, high = aligned(k * block, (k + 1) * block, wide)

        def body(q, pending):
            settle(pending)
            products = []
            for y in range(depth):
                beside = jnp.concatenate([p_ref[other, y, 2 * q + j] for j in range(2)], axis=1)
                left = a_ref[0, y, pl.ds(2 * q, 2), :, low:high].reshape(2 * block, high - low)
                products.append(matmul(left, diagonal([beside], low, k * block, high)))
            keep(products)
            return tuple((2 * q + j, interval_of(xlen_ref, grp, 2 * q + j), jnp.int32(slot)) for j in range(2))

        return body

    zero = jnp.int32(0)
    pending = ((zero, zero, zero), (zero, zero, zero))
    pairs = columns // 2
    pending = lax.fori_loop(0, pairs, inner, pending)
    pending = lax.fori_loop(0, intervals, across_x, pending)
    pairs_zm = jnp.where(has_zm & jnp.logical_not(same_zm), pairs, 0)
    pairs_zp = jnp.where(has_zp & jnp.logical_not(same_zp), pairs, 0)
    pending = lax.fori_loop(0, pairs_zm, across_z(5, 3, below), pending)
    pending = lax.fori_loop(0, pairs_zp, across_z(6, 4, above), pending)
    settle(pending)

    @pl.when(layer == layers - 1)
    def _():
        def emit(i, _):
            for n, slot in enumerate((1, 2, 4)):
                early_ref[n, i] = sums_ref[0, i, slot].astype(BF16)
            return 0

        lax.fori_loop(0, intervals, emit, 0)


def main(halves, zagg, xlen, a_blocks, prolong, left, right):
    layers, depth, columns, block, coarse = prolong.shape
    intervals = xlen.shape[1]
    sums = jax.ShapeDtypeStruct((halves + 1, intervals, 5, coarse, coarse), F32)
    early = jax.ShapeDtypeStruct((3, intervals, coarse, coarse), BF16)

    def whole(shape):
        return pl.BlockSpec(shape, lambda *grid: (0,) * len(shape), pipeline_mode=pl.Buffered(1))

    flops = layers * columns * depth * 2 * block * coarse * 12 * block
    return pl.pallas_call(
        functools.partial(main_kernel, halves),
        grid=(layers,),
        in_specs=[
            scalars(),
            scalars(),
            pl.BlockSpec((1, depth, columns, block, a_blocks.shape[-1]), lambda i: (i, 0, 0, 0, 0)),
            whole(prolong.shape),
            in_vmem(),
            in_vmem(),
        ],
        out_specs=[vmem_block(sums.shape, (0,) * 5), vmem_block(early.shape, (0,) * 4)],
        out_shape=[sums, early],
        scratch_shapes=[pltpu.VMEM((2, depth * block, coarse), BF16)],
        cost_estimate=pl.CostEstimate(flops=flops * 4, bytes_accessed=40 << 20, transcendentals=0),
        compiler_params=pltpu.CompilerParams(vmem_limit_bytes=LIMIT),
        name="coarsen",
    )(zagg, xlen, a_blocks, prolong, left, right)


def boundary_kernel(chunk, last, zagg_ref, xlen_ref, message_ref, a_ref, p_ref, carried_ref, *rest):
    if chunk > 0:
        base_ref, rest = rest[0], rest[1:]
    depth, _, block, coarse = message_ref.shape
    each = p_ref.shape[2]
    dom, grp = lax.axis_index("dom"), lax.axis_index("grp")
    sums_ref = rest[-1]
    sums_ref[...] = base_ref[...] if chunk > 0 else jnp.zeros_like(sums_ref)
    low, high = aligned(5 * block, 6 * block, 7 * block)

    def interval(q, j):
        return interval_of(xlen_ref, grp, chunk * each + 2 * q + j)

    def upper(q, _):
        rows = [[], []]
        for y in range(depth):
            mine = [p_ref[0, y, 2 * q + j] for j in range(2)]
            both = matmul(message_ref[y, each + q], diagonal(mine, 0, 0, 2 * block))
            for j in range(2):
                rows[j].append(both[:, j * coarse : (j + 1) * coarse].astype(BF16))
        for j in range(2):
            theirs = message_ref[:, 2 * q + j].reshape(depth * block, coarse)
            sums_ref[0, interval(q, j)] += transposed_matmul(theirs, jnp.concatenate(rows[j], axis=0))
        return 0

    def lower(q, _):
        rows = [[], []]
        for y in range(depth):
            theirs = jnp.concatenate([message_ref[y, 2 * q + j] for j in range(2)], axis=1)
            left = a_ref[0, y, pl.ds(2 * q, 2)].reshape(2 * block, high - low)
            both = matmul(left, diagonal([theirs], low, 5 * block, high))
            for j in range(2):
                rows[j].append(both[j * block : (j + 1) * block, j * coarse : (j + 1) * coarse].astype(BF16))
        for j in range(2):
            own = p_ref[0, :, 2 * q + j].reshape(depth * block, coarse)
            sums_ref[1, interval(q, j)] += transposed_matmul(own, jnp.concatenate(rows[j], axis=0))
        return 0

    lax.fori_loop(0, each // 2, upper, 0)
    lax.fori_loop(0, each // 2, lower, 0)
    if last:
        late_ref, owned_ref = rest[:2]
        layers = zagg_ref.shape[0] // lax.axis_size("dom")
        at = dom * layers
        same = (at > 0) & (zagg_ref[jnp.where(at > 0, at - 1, 0)] == zagg_ref[at])
        joined = jnp.where(same, 1.0, 0.0)
        late_ref[...] = (carried_ref[0, :, 0] + sums_ref[0] + joined * sums_ref[1]).astype(BF16)
        owned_ref[...] = (1.0 - joined) * sums_ref[1]


def boundary(chunk, zagg, xlen, message, a_blocks, prolong, carried, base=None):
    _, depth, columns, block, coarse = prolong.shape
    intervals = xlen.shape[1]
    each = columns // CHUNKS
    last = chunk == CHUNKS - 1
    low, high = aligned(5 * block, 6 * block, 7 * block)
    sums = jax.ShapeDtypeStruct((2, intervals, coarse, coarse), F32)
    in_specs = [
        scalars(),
        scalars(),
        in_vmem(),
        vmem_block((1, depth, each, block, high - low), (0, 0, chunk, 0, low // LANES)),
        vmem_block((1, depth, each, block, coarse), (0, 0, chunk, 0, 0)),
        vmem_block((1, intervals, 1, coarse, coarse), (0,) * 5),
    ]
    operands = [zagg, xlen, message, a_blocks, prolong, carried]
    if base is not None:
        in_specs.append(vmem_block(sums.shape, (0,) * 4))
        operands.append(base)
    out_specs, out_shape, scratch = [vmem_block(sums.shape, (0,) * 4)], [sums], []
    if last:
        late = jax.ShapeDtypeStruct((intervals, coarse, coarse), BF16)
        owned = jax.ShapeDtypeStruct((intervals, coarse, coarse), F32)
        out_specs, out_shape = [vmem_block(late.shape, (0,) * 3)] * 2, [late, owned]
        scratch = [pltpu.VMEM(sums.shape, F32)]
    return pl.pallas_call(
        functools.partial(boundary_kernel, chunk, last),
        grid=(1,),
        in_specs=in_specs,
        out_specs=out_specs,
        out_shape=out_shape,
        scratch_shapes=scratch,
        compiler_params=pltpu.CompilerParams(vmem_limit_bytes=LIMIT),
    )(*operands)


def final_kernel(zagg_ref, sums_ref, owned_ref, early_ref, late_ref, out_ref):
    coarse = sums_ref.shape[-1]
    dom = lax.axis_index("dom")
    layers = zagg_ref.shape[0] // lax.axis_size("dom")
    half, halves = pl.program_id(0), pl.num_programs(0)
    first = jnp.where(half == 0, 1.0, 0.0)
    last = jnp.where(half == halves - 1, 1.0, 0.0)
    end = (dom + 1) * layers
    following = jnp.where(end < zagg_ref.shape[0], end, end - 1)
    joined = jnp.where(zagg_ref[following] == zagg_ref[end - 1], last, 0.0)

    def put(slot, value):
        out_ref[0, :, :, slot * coarse : (slot + 1) * coarse] = value.astype(BF16)

    late = late_ref[...].astype(F32)

    def early(n):
        return last * early_ref[n].astype(F32)

    put(0, sums_ref[0, :, 0] + joined * late)
    put(1, sums_ref[0, :, 1] + early(0))
    put(2, sums_ref[0, :, 2] + early(1))
    put(3, sums_ref[0, :, 3] + first * owned_ref[...])
    put(4, sums_ref[0, :, 4] + early(2) + (last - joined) * late)


def final(halves, zagg, sums, owned, early, late):
    _, intervals, slots, coarse, _ = sums.shape
    return pl.pallas_call(
        final_kernel,
        grid=(halves,),
        in_specs=[
            scalars(),
            pl.BlockSpec((1, intervals, slots, coarse, coarse), lambda h: (h + 1, 0, 0, 0, 0)),
            vmem_block(owned.shape, (0,) * 3),
            in_vmem(),
            in_vmem(),
        ],
        out_specs=pl.BlockSpec((1, intervals, coarse, slots * coarse), lambda h: (h, 0, 0, 0)),
        out_shape=jax.ShapeDtypeStruct((halves, intervals, coarse, slots * coarse), BF16),
        compiler_params=pltpu.CompilerParams(vmem_limit_bytes=LIMIT),
        name="finish",
    )(zagg, sums, owned, early, late)


def per_device(a_blocks, prolong, zagg, xlen):
    halves = prolong.shape[0] // 2
    prolong = pltpu.with_memory_space_constraint(prolong, pltpu.HBM)
    *messages, left_edge, right_edge = pack(a_blocks, prolong)
    arrived = []
    for message in messages:
        arrived.append(shifted(message, "dom", 1))
    left = shifted(right_edge, "grp", 1)
    right = shifted(left_edge, "grp", -1)
    sums, early = main(halves, zagg, xlen, a_blocks, prolong, left, right)
    early = shifted(early, "dom", -1)
    beyond = None
    for chunk, message in enumerate(arrived):
        outs = boundary(chunk, zagg, xlen, message, a_blocks, prolong, sums, beyond)
        beyond = outs[0]
    late, owned = outs
    late = shifted(late, "dom", -1)
    return final(halves, zagg, sums, owned, early, late)


def solution(mesh):
    in_specs = (P("dom", None, "grp", None, None), P("dom", None, "grp", None, None), P(), P())
    out_specs = P("dom", "grp", None, None)
    return jax.shard_map(per_device, mesh=mesh, in_specs=in_specs, out_specs=out_specs, check_vma=False)
```

time: 97 us -> 82.2 us (0.85)
  Pallas kernels: 61.4 us -> 46.8 us
  waiting for transfers between devices: 5.82 us -> 18.6 us
  local copies, waits for them, and re-layouts: 7.35 us -> 0.01 us
  starting transfers between devices: 21.9 us -> 16.3 us
    pallas_call x1, Pallas kernels: 48.2 us -> 34.3 us  [main(): pl.pallas_call(functools.partial(main_kernel, halves), grid=(layers,), in...]
    ppermute x6, waiting for transfers between devices: 5.82 us -> 18.6 us  [shifted(): return lax.ppermute(block, axis, route)]
    unnamed x22 -> x4, local copies, waits for them, and re-layouts: 7.35 us -> 0.01 us
    ppermute x6, starting transfers between devices: 21.9 us -> 16.3 us  [shifted(): return lax.ppermute(block, axis, route)]
    pallas_call x1, Pallas kernels: 3 us -> 1.81 us  [final(): pl.pallas_call(final_kernel, grid=(halves,), in_specs=[scalars(), pl.Bloc...]
  transfers between devices with their start and end apart: 6 -> 6, of which waited for: 1 -> 2; matrix products, arithmetic and copies ran while one was open for 0% -> 0% of each run, Pallas kernels for 58% -> 52%
where the time goes in v2:
time: 82.2 us; the launch traced here: 81.9 us
  Pallas kernels  46.8 us (57%)
  waiting for transfers between devices  18.6 us (23%)
  starting transfers between devices  16.3 us (20%)
    pallas_call x1, Pallas kernels, main(): pl.pallas_call(functools.partial(main_kernel, halves), grid=(layers,), in...  34.3 us
    ppermute x6, waiting for transfers between devices, shifted(): return lax.ppermute(block, axis, route)  18.6 us
    ppermute x6, starting transfers between devices, shifted(): return lax.ppermute(block, axis, route)  16.3 us
    pallas_call x2, Pallas kernels, boundary(): pl.pallas_call(functools.partial(boundary_kernel, chunk, last), grid=(1,)...  7.97 us
    pallas_call x1, Pallas kernels, pack(): pl.pallas_call(pack_kernel, grid=(1,), in_specs=[vmem_block((1, depth, co...  2.75 us
    pallas_call x1, Pallas kernels, final(): pl.pallas_call(final_kernel, grid=(halves,), in_specs=[scalars(), pl.Bloc...  1.81 us
  transfers between devices with their start and end apart: 6, of which 2 were waited for; matrix products, arithmetic and copies ran while one was open for 0% of the time, Pallas kernels for 52%

profile of v2, /device:TPU:14, one launch (start us, length us, event | category | flops | bytes accessed | tf_op | source)
XLA Modules:
  0.0 81.9 jit_solution(12887767866806478107)
XLA Ops:
  0.0 0.0 copy-start.1
  0.0 0.0 copy-start
  0.0 2.8 %pack.1 = (bf16[7,9,64,128]{3,2,1,0:T(8,128)(2,1)S(1)}, bf16[7,9,64,128]{3,2,1,0:T(8,128)(2,1)S(1)}, bf16[4,7,64,128]{3,2,1,0:T(8,128)(2,1)S(1)}, bf16[4,7,64,128]{3,2,1,0:T(8,128)(2,1)S(1)}) custom-call(bf16[4,7,12,64,448]{4,3,2,1,0:T(8,128)(2,1)} %a_ref.7, bf16[4,7,12,64,128]{4,3,2,1,0:T(8,128)(2,1)} %p_ref.5, bf16[4,7,12,64,128]{4,3,2,1,0:T(8,128)(2,1)} %p_ref.5, ...), custom_call_target="tpu_custom_call" | custom-call | tf_op jit(solution)/shard_map/pack/pallas_call | solution.py:97
  2.8 1.9 %collective-permute-start = (bf16[4,7,64,128]{3,2,1,0:T(8,128)(2,1)S(1)}, bf16[4,7,64,128]{3,2,1,0:T(8,128)(2,1)S(1)}, u32[]{:S(2)}, u32[]{:S(2)}) collective-permute-start(bf16[4,7,64,128]{3,2,1,0:T(8,128)(2,1)S(1)} %get-tuple-element.13), channel_id=1, source_target_pairs={{0,1},{1,2},{2,3},{4,5},{5,6},{6,7},{8,9},{9,10},{10,11},{12,13},{... | collective-permute-start | bytes 1376264 | tf_op jit(solution)/shard_map/ppermute | solution.py:31
  4.7 3.6 %collective-permute-start.1 = (bf16[4,7,64,128]{3,2,1,0:T(8,128)(2,1)S(1)}, bf16[4,7,64,128]{3,2,1,0:T(8,128)(2,1)S(1)}, u32[]{:S(2)}, u32[]{:S(2)}) collective-permute-start(bf16[4,7,64,128]{3,2,1,0:T(8,128)(2,1)S(1)} %get-tuple-element.14), channel_id=1, source_target_pairs={{1,0},{2,1},{3,2},{5,4},{6,5},{7,6},{9,8},{10,9},{11,10},{13,12},{... | collective-permute-start | bytes 1376264 | tf_op jit(solution)/shard_map/ppermute | solution.py:31
  8.3 3.4 %collective-permute-start.2 = (bf16[7,9,64,128]{3,2,1,0:T(8,128)(2,1)S(1)}, bf16[7,9,64,128]{3,2,1,0:T(8,128)(2,1)S(1)}, u32[]{:S(2)}, u32[]{:S(2)}) collective-permute-start(bf16[7,9,64,128]{3,2,1,0:T(8,128)(2,1)S(1)} %get-tuple-element.16), channel_id=1, source_target_pairs={{0,4},{4,8},{8,12},{12,16},{16,20},{20,24},{24,28},{1,5},{5,9},{9,... | collective-permute-start | bytes 3096584 | tf_op jit(solution)/shard_map/ppermute | solution.py:31
  11.8 3.4 %collective-permute-start.3 = (bf16[7,9,64,128]{3,2,1,0:T(8,128)(2,1)S(1)}, bf16[7,9,64,128]{3,2,1,0:T(8,128)(2,1)S(1)}, u32[]{:S(2)}, u32[]{:S(2)}) collective-permute-start(bf16[7,9,64,128]{3,2,1,0:T(8,128)(2,1)S(1)} %get-tuple-element.17), channel_id=1, source_target_pairs={{0,4},{4,8},{8,12},{12,16},{16,20},{20,24},{24,28},{1,5},{5,9},{9,... | collective-permute-start | bytes 3096584 | tf_op jit(solution)/shard_map/ppermute | solution.py:31
  15.2 0.0 collective-permute-done.left_ref
  15.2 0.0 collective-permute-done.1.right_ref
  15.2 0.0 copy-done.1
  15.2 0.0 copy-done
  15.3 34.3 %coarsen.1 = (f32[3,4,5,128,128]{4,3,2,1,0:T(8,128)S(1)}, bf16[3,4,128,128]{3,2,1,0:T(8,128)(2,1)S(1)}) custom-call(s32[32]{0:T(128)S(1)} %copy-done.1, s32[4,4]{1,0:T(4,128)S(1)} %copy-done, bf16[4,7,12,64,448]{4,3,2,1,0:T(8,128)(2,1)} %a_ref.7, bf16[4,7,12,64,128]{4,3,2,1,0:T(8,128)(2,1)} %p_ref.5, ...), custom_call_target="tpu_custom_call" | custom-call | flops 16911433728 | bytes 41943040 | tf_op jit(solution)/shard_map/coarsen/pallas_call | solution.py:262
  49.6 1.9 %collective-permute-start.4 = (bf16[3,4,128,128]{3,2,1,0:T(8,128)(2,1)S(1)}, bf16[3,4,128,128]{3,2,1,0:T(8,128)(2,1)S(1)}, u32[]{:S(2)}, u32[]{:S(2)}) collective-permute-start(bf16[3,4,128,128]{3,2,1,0:T(8,128)(2,1)S(1)} %get-tuple-element.19), channel_id=1, source_target_pairs={{4,0},{8,4},{12,8},{16,12},{20,16},{24,20},{28,24},{5,1},{9,5},{13... | collective-permute-start | bytes 1179656 | tf_op jit(solution)/shard_map/ppermute | solution.py:31
  51.5 12.8 %collective-permute-done.3.message_ref = bf16[7,9,64,128]{3,2,1,0:T(8,128)(2,1)S(1)} collective-permute-done((bf16[7,9,64,128]{3,2,1,0:T(8,128)(2,1)S(1)}, bf16[7,9,64,128]{3,2,1,0:T(8,128)(2,1)S(1)}, u32[]{:S(2)}, u32[]{:S(2)}) %collective-permute-start.3) | collective-permute-done | bytes 1032224 | tf_op jit(solution)/shard_map/ppermute | solution.py:31
  64.3 4.0 %shard_map.46.rest_0_ = f32[2,4,128,128]{3,2,1,0:T(8,128)S(1)} custom-call(s32[32]{0:T(128)S(1)} %copy-done.1, s32[4,4]{1,0:T(4,128)S(1)} %copy-done, bf16[7,9,64,128]{3,2,1,0:T(8,128)(2,1)S(1)} %collective-permute-done.3.message_ref, bf16[4,7,12,64,448]{4,3,2,1,0:T(8,128)(2,1)} %a_ref.7, bf16[4,7,12,64,128]{4,3,2,1,0:T(8,128)(2,1)} %p_ref.5, ...), custom_call_target="tpu_custom_call" | custom-call | tf_op jit(solution)/shard_map/pallas_call | solution.py:357
  68.3 0.0 collective-permute-done.2.message_ref
  68.3 4.0 %shard_map.47 = (bf16[4,128,128]{2,1,0:T(8,128)(2,1)S(1)}, f32[4,128,128]{2,1,0:T(8,128)S(1)}) custom-call(s32[32]{0:T(128)S(1)} %copy-done.1, s32[4,4]{1,0:T(4,128)S(1)} %copy-done, bf16[7,9,64,128]{3,2,1,0:T(8,128)(2,1)S(1)} %collective-permute-done.2.message_ref, bf16[4,7,12,64,448]{4,3,2,1,0:T(8,128)(2,1)} %a_ref.7, bf16[4,7,12,64,128]{4,3,2,1,0:T(8,128)(2,1)} %p_ref.5, ...), custom_call_target="tpu_custom_call" | custom-call | tf_op jit(solution)/shard_map/pallas_call | solution.py:357
  72.3 1.9 %collective-permute-start.5 = (bf16[4,128,128]{2,1,0:T(8,128)(2,1)S(1)}, bf16[4,128,128]{2,1,0:T(8,128)(2,1)S(1)}, u32[]{:S(2)}, u32[]{:S(2)}) collective-permute-start(bf16[4,128,128]{2,1,0:T(8,128)(2,1)S(1)} %get-tuple-element.20), channel_id=1, source_target_pairs={{4,0},{8,4},{12,8},{16,12},{20,16},{24,20},{28,24},{5,1},{9,5},{13... | collective-permute-start | bytes 393224 | tf_op jit(solution)/shard_map/ppermute | solution.py:31
  74.2 0.0 collective-permute-done.4.early_ref
  74.2 5.8 %collective-permute-done.5.late_ref = bf16[4,128,128]{2,1,0:T(8,128)(2,1)S(1)} collective-permute-done((bf16[4,128,128]{2,1,0:T(8,128)(2,1)S(1)}, bf16[4,128,128]{2,1,0:T(8,128)(2,1)S(1)}, u32[]{:S(2)}, u32[]{:S(2)}) %collective-permute-start.5) | collective-permute-done | bytes 131104 | tf_op jit(solution)/shard_map/ppermute | solution.py:31
  80.1 1.8 %finish.1 = bf16[2,4,128,640]{3,2,1,0:T(8,128)(2,1)} custom-call(s32[32]{0:T(128)S(1)} %copy-done.1, f32[3,4,5,128,128]{4,3,2,1,0:T(8,128)S(1)} %get-tuple-element.15.carried_ref.sums_ref, f32[4,128,128]{2,1,0:T(8,128)S(1)} %get-tuple-element.18.owned_ref, bf16[3,4,128,128]{3,2,1,0:T(8,128)(2,1)S(1)} %collective-permute-done.4.early_ref, ...), custom_call_target="tpu_custom_call" | custom-call | tf_op jit(solution)/shard_map/finish/pallas_call | solution.py:396
Async XLA Ops:
  0.0 15.2 %copy-start.1 = (s32[32]{0:T(128)S(1)}, s32[32]{0:T(128)}, u32[]{:S(2)}) copy-start(s32[32]{0:T(128)} %zagg_ref.7) | copy-start | bytes 388
  0.0 15.2 %copy-start = (s32[4,4]{1,0:T(4,128)S(1)}, s32[4,4]{1,0:T(4,128)}, u32[]{:S(2)}) copy-start(s32[4,4]{1,0:T(4,128)} %xlen_ref.5) | copy-start | bytes 196
  2.8 12.5 %collective-permute-start = (bf16[4,7,64,128]{3,2,1,0:T(8,128)(2,1)S(1)}, bf16[4,7,64,128]{3,2,1,0:T(8,128)(2,1)S(1)}, u32[]{:S(2)}, u32[]{:S(2)}) collective-permute-start(bf16[4,7,64,128]{3,2,1,0:T(8,128)(2,1)S(1)} %get-tuple-element.13), channel_id=1, source_target_pairs={{0,1},{1,2},{2,3},{4,5},{5,6},{6,7},{8,9},{9,10},{10,11},{12,13},{... | collective-permute-start | bytes 1376264 | tf_op jit(solution)/shard_map/ppermute | solution.py:31
  4.7 10.5 %collective-permute-start.1 = (bf16[4,7,64,128]{3,2,1,0:T(8,128)(2,1)S(1)}, bf16[4,7,64,128]{3,2,1,0:T(8,128)(2,1)S(1)}, u32[]{:S(2)}, u32[]{:S(2)}) collective-permute-start(bf16[4,7,64,128]{3,2,1,0:T(8,128)(2,1)S(1)} %get-tuple-element.14), channel_id=1, source_target_pairs={{1,0},{2,1},{3,2},{5,4},{6,5},{7,6},{9,8},{10,9},{11,10},{13,12},{... | collective-permute-start | bytes 1376264 | tf_op jit(solution)/shard_map/ppermute | solution.py:31
  8.3 59.9 %collective-permute-start.2 = (bf16[7,9,64,128]{3,2,1,0:T(8,128)(2,1)S(1)}, bf16[7,9,64,128]{3,2,1,0:T(8,128)(2,1)S(1)}, u32[]{:S(2)}, u32[]{:S(2)}) collective-permute-start(bf16[7,9,64,128]{3,2,1,0:T(8,128)(2,1)S(1)} %get-tuple-element.16), channel_id=1, source_target_pairs={{0,4},{4,8},{8,12},{12,16},{16,20},{20,24},{24,28},{1,5},{5,9},{9,... | collective-permute-start | bytes 3096584 | tf_op jit(solution)/shard_map/ppermute | solution.py:31
  11.8 52.5 %collective-permute-start.3 = (bf16[7,9,64,128]{3,2,1,0:T(8,128)(2,1)S(1)}, bf16[7,9,64,128]{3,2,1,0:T(8,128)(2,1)S(1)}, u32[]{:S(2)}, u32[]{:S(2)}) collective-permute-start(bf16[7,9,64,128]{3,2,1,0:T(8,128)(2,1)S(1)} %get-tuple-element.17), channel_id=1, source_target_pairs={{0,4},{4,8},{8,12},{12,16},{16,20},{20,24},{24,28},{1,5},{5,9},{9,... | collective-permute-start | bytes 3096584 | tf_op jit(solution)/shard_map/ppermute | solution.py:31
  49.6 24.7 %collective-permute-start.4 = (bf16[3,4,128,128]{3,2,1,0:T(8,128)(2,1)S(1)}, bf16[3,4,128,128]{3,2,1,0:T(8,128)(2,1)S(1)}, u32[]{:S(2)}, u32[]{:S(2)}) collective-permute-start(bf16[3,4,128,128]{3,2,1,0:T(8,128)(2,1)S(1)} %get-tuple-element.19), channel_id=1, source_target_pairs={{4,0},{8,4},{12,8},{16,12},{20,16},{24,20},{28,24},{5,1},{9,5},{13... | collective-permute-start | bytes 1179656 | tf_op jit(solution)/shard_map/ppermute | solution.py:31
  72.3 7.8 %collective-permute-start.5 = (bf16[4,128,128]{2,1,0:T(8,128)(2,1)S(1)}, bf16[4,128,128]{2,1,0:T(8,128)(2,1)S(1)}, u32[]{:S(2)}, u32[]{:S(2)}) collective-permute-start(bf16[4,128,128]{2,1,0:T(8,128)(2,1)S(1)} %get-tuple-element.20), channel_id=1, source_target_pairs={{4,0},{8,4},{12,8},{16,12},{20,16},{24,20},{28,24},{5,1},{9,5},{13... | collective-permute-start | bytes 393224 | tf_op jit(solution)/shard_map/ppermute | solution.py:31

commit v3 on v2

v3 whole, which is shorter than its diff:
```python
import functools
import jax
import jax.numpy as jnp
from jax import lax
from jax.experimental import pallas as pl
from jax.experimental.pallas import tpu as pltpu
from jax.sharding import PartitionSpec as P


F32, BF16 = jnp.float32, jnp.bfloat16
LANES = 128
LIMIT = 36 << 20


def vmem_block(shape, index):
    return pl.BlockSpec(shape, lambda *grid: index)


def scalars():
    return pl.BlockSpec(memory_space=pltpu.SMEM)


def in_vmem():
    return pl.BlockSpec(memory_space=pltpu.VMEM)


def shifted(block, axis, distance):
    devices = range(lax.axis_size(axis))
    route = [(i, i + distance) for i in devices if i + distance in devices]
    return lax.ppermute(block, axis, route)


def matmul(left, right):
    return jnp.dot(left, right, preferred_element_type=F32)


def transposed_matmul(left, right):
    return lax.dot_general(left, right, (((0,), (0,)), ((), ())), preferred_element_type=F32)


def interval_of(xlen_ref, group, column):
    end, found = 0, 0
    for i in range(xlen_ref.shape[1]):
        end = end + xlen_ref[group, i]
        found = found + jnp.where(column >= end, 1, 0)
    return found


def aligned(low, high, end):
    return low // LANES * LANES, min(-(-high // LANES) * LANES, end)


def factor(flag, shape):
    return jnp.full(shape, jnp.where(flag, 1.0, 0.0), F32).astype(BF16)


def diagonal(blocks, low, first, high):
    rows, columns = blocks[0].shape
    parts = []
    if first > low:
        parts.append(jnp.zeros((first - low, columns * len(blocks)), BF16))
    none = jnp.zeros((rows, columns), BF16)
    for i, block in enumerate(blocks):
        parts.append(jnp.concatenate([block if i == j else none for j in range(len(blocks))], axis=1))
    end = first + rows * len(blocks)
    if high > end:
        parts.append(jnp.zeros((high - end, columns * len(blocks)), BF16))
    return jnp.concatenate(parts, axis=0)


def top_kernel(p_ref, out_ref, sem):
    copy = pltpu.make_async_copy(p_ref.at[p_ref.shape[0] - 1], out_ref, sem)
    copy.start()
    copy.wait()


def top(prolong):
    return pl.pallas_call(
        top_kernel,
        in_specs=[pl.BlockSpec(memory_space=pltpu.HBM)],
        out_specs=in_vmem(),
        out_shape=jax.ShapeDtypeStruct(prolong.shape[1:], BF16),
        scratch_shapes=[pltpu.SemaphoreType.DMA],
        compiler_params=pltpu.CompilerParams(vmem_limit_bytes=LIMIT),
        name="top",
    )(prolong)


def pack_kernel(a_ref, p_ref, after_ref, pairs_ref, left_ref, right_ref, sems):
    _, depth, block, _ = left_ref.shape
    copies = [
        pltpu.make_async_copy(p_ref.at[:, :, 0], left_ref, sems.at[0]),
        pltpu.make_async_copy(p_ref.at[:, :, p_ref.shape[2] - 1], right_ref, sems.at[1]),
    ]
    for copy in copies:
        copy.start()

    def body(i, _):
        for y in range(depth):
            pair = [a_ref[0, y, 2 * i + j, :, :block] for j in range(2)]
            pairs_ref[y, i] = jnp.concatenate(pair, axis=-1)
        return 0

    lax.fori_loop(0, pairs_ref.shape[1], body, 0)
    for copy in copies:
        copy.wait()


def pack(a_blocks, prolong, after):
    layers, depth, columns, block, coarse = prolong.shape
    low, _ = aligned(6 * block, 7 * block, 7 * block)
    pairs = jax.ShapeDtypeStruct((depth, columns // 2, block, 2 * block), BF16)
    edge = jax.ShapeDtypeStruct((layers, depth, block, coarse), BF16)
    return pl.pallas_call(
        pack_kernel,
        grid=(1,),
        in_specs=[
            vmem_block((1, depth, columns, block, LANES), (layers - 1, 0, 0, 0, low // LANES)),
            pl.BlockSpec(memory_space=pltpu.HBM),
            pl.BlockSpec(memory_space=pl.ANY),
        ],
        out_specs=[in_vmem()] * 3,
        out_shape=[pairs, edge, edge],
        scratch_shapes=[pltpu.SemaphoreType.DMA((2,))],
        compiler_params=pltpu.CompilerParams(vmem_limit_bytes=LIMIT),
        name="pack",
    )(a_blocks, prolong, after)


def main_kernel(halves, zagg_ref, xlen_ref, a_ref, p_ref, sums_ref, rows_ref):
    layers, depth, columns, block, coarse = p_ref.shape
    intervals = sums_ref.shape[1]
    wide = a_ref.shape[-1]
    shape = (block, coarse)
    dom, grp = lax.axis_index("dom"), lax.axis_index("grp")
    layer = pl.program_id(0)

    @pl.when(layer == 0)
    def _():
        def clear(i, _):
            for target in range(sums_ref.shape[0]):
                sums_ref[target, i] = jnp.zeros(sums_ref.shape[2:], F32)
            return 0

        lax.fori_loop(0, intervals, clear, 0)

    rows_ref[...] = jnp.zeros_like(rows_ref)

    at = dom * layers + layer
    mine = zagg_ref[at]
    target = mine - dom * halves + 1
    has_zm, has_zp = layer > 0, layer < layers - 1
    below = jnp.where(has_zm, layer - 1, 0)
    above = jnp.where(has_zp, layer + 1, layer)
    same_zm = has_zm & (zagg_ref[jnp.where(has_zm, at - 1, at)] == mine)
    same_zp = has_zp & (zagg_ref[jnp.where(has_zp, at + 1, at)] == mine)
    none = jnp.zeros(shape, BF16)

    def settle(pending):
        for j in range(2):
            x, interval, slot = pending[j]
            own = p_ref[layer, :, x].reshape(depth * block, coarse)
            sums_ref[target, interval, slot] += transposed_matmul(own, rows_ref[j])

    def keep(products):
        for y, both in enumerate(products):
            for j in range(2):
                part = both[j * block : (j + 1) * block, j * coarse : (j + 1) * coarse]
                rows_ref[j, y * block : (y + 1) * block] = part.astype(BF16)

    def inner(q, pending):
        settle(pending)
        zm_factor, zp_factor = factor(same_zm, shape), factor(same_zp, shape)
        info = []
        for j in range(2):
            x = 2 * q + j
            has_xm, has_xp = x > 0, x < columns - 1
            before, after = jnp.where(has_xm, x - 1, 0), jnp.where(has_xp, x + 1, x)
            interval = interval_of(xlen_ref, grp, x)
            same_xm = has_xm & (interval_of(xlen_ref, grp, before) == interval)
            same_xp = has_xp & (interval_of(xlen_ref, grp, after) == interval)
            info.append((x, interval, before, after, factor(same_xm, shape), factor(same_xp, shape)))
        products = []
        for y in range(depth):
            stacks = []
            for x, _, before, after, xm_factor, xp_factor in info:
                stacks.append(
                    jnp.concatenate(
                        [
                            p_ref[layer, y, x],
                            p_ref[layer, y, before] * xm_factor,
                            p_ref[layer, y, after] * xp_factor,
                            p_ref[layer, y - 1, x] if y > 0 else none,
                            p_ref[layer, y + 1, x] if y < depth - 1 else none,
                            p_ref[below, y, x] * zm_factor,
                            p_ref[above, y, x] * zp_factor,
                        ],
                        axis=0,
                    )
                )
            left = a_ref[0, y, pl.ds(2 * q, 2)].reshape(2 * block, wide)
            products.append(matmul(left, jnp.concatenate(stacks, axis=1)))
        keep(products)
        return tuple((i[0], i[1], jnp.int32(0)) for i in info)

    def across_x(i, pending):
        settle(pending)
        low, high = aligned(block, 3 * block, wide)
        end = 0
        for n in range(intervals):
            end = end + jnp.where(n <= i, xlen_ref[grp, n], 0)
        x0, x1 = end - 1, end
        products = []
        for y in range(depth):
            stack = jnp.concatenate(
                [
                    jnp.zeros((block - low, 2 * coarse), BF16),
                    jnp.concatenate([none, p_ref[layer, y, x0]], axis=1),
                    jnp.concatenate([p_ref[layer, y, x1], none], axis=1),
                    jnp.zeros((high - 3 * block, 2 * coarse), BF16),
                ],
                axis=0,
            )
            left = jnp.concatenate([a_ref[0, y, x0, :, low:high], a_ref[0, y, x1, :, low:high]], axis=0)
            products.append(matmul(left, stack))
        keep(products)
        return ((x0, i, jnp.int32(2)), (x1, i + 1, jnp.int32(1)))

    def across_z(k, slot, other):
        low, high = aligned(k * block, (k + 1) * block, wide)

        def body(q, pending):
            settle(pending)
            products = []
            for y in range(depth):
                beside = jnp.concatenate([p_ref[other, y, 2 * q + j] for j in range(2)], axis=1)
                left = a_ref[0, y, pl.ds(2 * q, 2), :, low:high].reshape(2 * block, high - low)
                products.append(matmul(left, diagonal([beside], low, k * block, high)))
            keep(products)
            return tuple((2 * q + j, interval_of(xlen_ref, grp, 2 * q + j), jnp.int32(slot)) for j in range(2))

        return body

    zero = jnp.int32(0)
    pending = ((zero, zero, zero), (zero, zero, zero))
    pairs = columns // 2
    pending = lax.fori_loop(0, pairs, inner, pending)
    pending = lax.fori_loop(0, intervals - 1, across_x, pending)
    pairs_zm = jnp.where(has_zm & jnp.logical_not(same_zm), pairs, 0)
    pairs_zp = jnp.where(has_zp & jnp.logical_not(same_zp), pairs, 0)
    pending = lax.fori_loop(0, pairs_zm, across_z(5, 3, below), pending)
    pending = lax.fori_loop(0, pairs_zp, across_z(6, 4, above), pending)
    settle(pending)


def sums_shape(halves, intervals, coarse):
    return jax.ShapeDtypeStruct((halves + 1, intervals, 5, coarse, coarse), F32)


def main(halves, zagg, xlen, a_blocks, prolong):
    layers, depth, columns, block, coarse = prolong.shape
    flops = layers * columns * depth * 2 * block * coarse * 12 * block
    return pl.pallas_call(
        functools.partial(main_kernel, halves),
        grid=(layers,),
        in_specs=[
            scalars(),
            scalars(),
            pl.BlockSpec((1, depth, columns, block, a_blocks.shape[-1]), lambda i: (i, 0, 0, 0, 0)),
            pl.BlockSpec(prolong.shape, lambda i: (0,) * 5, pipeline_mode=pl.Buffered(1)),
        ],
        out_specs=in_vmem(),
        out_shape=sums_shape(halves, xlen.shape[1], coarse),
        scratch_shapes=[pltpu.VMEM((2, depth * block, coarse), BF16)],
        cost_estimate=pl.CostEstimate(flops=flops * 4, bytes_accessed=40 << 20, transcendentals=0),
        compiler_params=pltpu.CompilerParams(vmem_limit_bytes=LIMIT),
        name="coarsen",
    )(zagg, xlen, a_blocks, prolong)


def edge_kernel(halves, zagg_ref, first_ref, last_ref, low_edge_ref, high_edge_ref, left_ref, right_ref, old_ref, sums_ref, early_ref):
    layers, depth, block, coarse = left_ref.shape
    intervals = sums_ref.shape[1]
    dom = lax.axis_index("dom")
    low_first, high_first = aligned(block, 2 * block, 7 * block)
    low_last, high_last = aligned(2 * block, 3 * block, 7 * block)
    none = jnp.zeros((block, coarse), BF16)

    def body(layer, _):
        target = zagg_ref[dom * layers + layer] - dom * halves + 1
        rows = [[], []]
        for y in range(depth):
            first = diagonal([left_ref[layer, y]], low_first, block, high_first)
            last = diagonal([right_ref[layer, y]], low_last, 2 * block, high_last)
            rows[0].append(matmul(first_ref[layer, y, 0], first).astype(BF16))
            rows[1].append(matmul(last_ref[layer, y, 0], last).astype(BF16))
        own = [low_edge_ref[layer].reshape(depth * block, coarse), high_edge_ref[layer].reshape(depth * block, coarse)]
        sums_ref[target, 0, 1] += transposed_matmul(own[0], jnp.concatenate(rows[0], axis=0))
        sums_ref[target, intervals - 1, 2] += transposed_matmul(own[1], jnp.concatenate(rows[1], axis=0))
        return 0

    lax.fori_loop(0, layers, body, 0)

    def emit(i, _):
        for n, slot in enumerate((1, 2, 4)):
            early_ref[n, i] = sums_ref[0, i, slot].astype(BF16)
        return 0

    lax.fori_loop(0, intervals, emit, 0)


def edges(halves, zagg, a_blocks, low_edge, high_edge, left, right, sums):
    layers, depth, columns, block, _ = a_blocks.shape
    intervals, coarse = sums.shape[1], sums.shape[-1]
    lanes = [aligned(k * block, (k + 1) * block, 7 * block)[0] // LANES for k in (1, 2)]
    shape = (layers, depth, 1, block, LANES)
    return pl.pallas_call(
        functools.partial(edge_kernel, halves),
        grid=(1,),
        in_specs=[
            scalars(),
            vmem_block(shape, (0, 0, 0, 0, lanes[0])),
            vmem_block(shape, (0, 0, columns - 1, 0, lanes[1])),
        ]
        + [in_vmem()] * 5,
        out_specs=[in_vmem()] * 2,
        out_shape=[sums, jax.ShapeDtypeStruct((3, intervals, coarse, coarse), BF16)],
        input_output_aliases={7: 0},
        compiler_params=pltpu.CompilerParams(vmem_limit_bytes=LIMIT),
        name="edges",
    )(zagg, a_blocks, a_blocks, low_edge, high_edge, left, right, sums)


def boundary_kernel(zagg_ref, xlen_ref, theirs_ref, pairs_ref, a_ref, p_ref, old_ref, sums_ref, late_ref, upper_ref, lower_ref):
    depth, columns, block, coarse = theirs_ref.shape
    dom, grp = lax.axis_index("dom"), lax.axis_index("grp")
    upper_ref[...] = jnp.zeros_like(upper_ref)
    lower_ref[...] = jnp.zeros_like(lower_ref)
    low, high = aligned(5 * block, 6 * block, 7 * block)

    def upper(q, _):
        rows = [[], []]
        for y in range(depth):
            mine = [p_ref[0, y, 2 * q + j] for j in range(2)]
            both = matmul(pairs_ref[y, q], diagonal(mine, 0, 0, 2 * block))
            for j in range(2):
                rows[j].append(both[:, j * coarse : (j + 1) * coarse].astype(BF16))
        for j in range(2):
            theirs = theirs_ref[:, 2 * q + j].reshape(depth * block, coarse)
            at = interval_of(xlen_ref, grp, 2 * q + j)
            upper_ref[at] += transposed_matmul(theirs, jnp.concatenate(rows[j], axis=0))
        return 0

    def lower(q, _):
        rows = [[], []]
        for y in range(depth):
            theirs = jnp.concatenate([theirs_ref[y, 2 * q + j] for j in range(2)], axis=1)
            left = a_ref[0, y, pl.ds(2 * q, 2)].reshape(2 * block, high - low)
            both = matmul(left, diagonal([theirs], low, 5 * block, high))
            for j in range(2):
                rows[j].append(both[j * block : (j + 1) * block, j * coarse : (j + 1) * coarse].astype(BF16))
        for j in range(2):
            own = p_ref[0, :, 2 * q + j].reshape(depth * block, coarse)
            at = interval_of(xlen_ref, grp, 2 * q + j)
            lower_ref[at] += transposed_matmul(own, jnp.concatenate(rows[j], axis=0))
        return 0

    lax.fori_loop(0, columns // 2, upper, 0)
    lax.fori_loop(0, columns // 2, lower, 0)
    layers = zagg_ref.shape[0] // lax.axis_size("dom")
    at = dom * layers
    same = (at > 0) & (zagg_ref[jnp.where(at > 0, at - 1, 0)] == zagg_ref[at])
    joined = jnp.where(same, 1.0, 0.0)

    def emit(i, _):
        late_ref[i] = (sums_ref[0, i, 0] + upper_ref[i] + joined * lower_ref[i]).astype(BF16)
        sums_ref[1, i, 3] += (1.0 - joined) * lower_ref[i]
        return 0

    lax.fori_loop(0, late_ref.shape[0], emit, 0)


def boundary(zagg, xlen, theirs, pairs, a_blocks, prolong, sums):
    _, depth, columns, block, coarse = prolong.shape
    low, high = aligned(5 * block, 6 * block, 7 * block)
    late = jax.ShapeDtypeStruct((xlen.shape[1], coarse, coarse), BF16)
    return pl.pallas_call(
        boundary_kernel,
        grid=(1,),
        in_specs=[
            scalars(),
            scalars(),
            in_vmem(),
            in_vmem(),
            vmem_block((1, depth, columns, block, high - low), (0, 0, 0, 0, low // LANES)),
            vmem_block((1, depth, columns, block, coarse), (0, 0, 0, 0, 0)),
            in_vmem(),
        ],
        out_specs=[in_vmem()] * 2,
        out_shape=[sums, late],
        scratch_shapes=[pltpu.VMEM(late.shape, F32)] * 2,
        input_output_aliases={6: 0},
        compiler_params=pltpu.CompilerParams(vmem_limit_bytes=LIMIT),
        name="boundary",
    )(zagg, xlen, theirs, pairs, a_blocks, prolong, sums)


def final_kernel(zagg_ref, sums_ref, early_ref, late_ref, out_ref):
    coarse = sums_ref.shape[-1]
    dom = lax.axis_index("dom")
    layers = zagg_ref.shape[0] // lax.axis_size("dom")
    half, halves = pl.program_id(0), pl.num_programs(0)
    last = half == halves - 1
    end = (dom + 1) * layers
    following = jnp.where(end < zagg_ref.shape[0], end, end - 1)
    same = zagg_ref[following] == zagg_ref[end - 1]
    early_factor = jnp.where(last, 1.0, 0.0)
    self_factor = jnp.where(last & same, 1.0, 0.0)
    above_factor = jnp.where(last & jnp.logical_not(same), 1.0, 0.0)

    def body(i, _):
        def put(slot, value):
            out_ref[0, i, :, slot * coarse : (slot + 1) * coarse] = value.astype(BF16)

        late = late_ref[i].astype(F32)
        early = [early_factor * early_ref[n, i].astype(F32) for n in range(3)]
        put(0, sums_ref[half + 1, i, 0] + self_factor * late)
        put(1, sums_ref[half + 1, i, 1] + early[0])
        put(2, sums_ref[half + 1, i, 2] + early[1])
        put(3, sums_ref[half + 1, i, 3])
        put(4, sums_ref[half + 1, i, 4] + early[2] + above_factor * late)
        return 0

    lax.fori_loop(0, out_ref.shape[1], body, 0)


def final(halves, zagg, sums, early, late):
    _, intervals, slots, coarse, _ = sums.shape
    return pl.pallas_call(
        final_kernel,
        grid=(halves,),
        in_specs=[scalars(), in_vmem(), in_vmem(), in_vmem()],
        out_specs=pl.BlockSpec((1, intervals, coarse, slots * coarse), lambda h: (h, 0, 0, 0)),
        out_shape=jax.ShapeDtypeStruct((halves, intervals, coarse, slots * coarse), BF16),
        compiler_params=pltpu.CompilerParams(vmem_limit_bytes=LIMIT),
        name="finish",
    )(zagg, sums, early, late)


def per_device(a_blocks, prolong, zagg, xlen):
    halves = prolong.shape[0] // 2
    prolong = pltpu.with_memory_space_constraint(prolong, pltpu.HBM)
    rows = top(prolong)
    theirs = shifted(rows, "dom", 1)
    pairs, low_edge, high_edge = pack(a_blocks, prolong, rows)
    pairs = shifted(pairs, "dom", 1)
    left = shifted(high_edge, "grp", 1)
    right = shifted(low_edge, "grp", -1)
    sums = main(halves, zagg, xlen, a_blocks, prolong)
    sums, early = edges(halves, zagg, a_blocks, low_edge, high_edge, left, right, sums)
    early = shifted(early, "dom", -1)
    sums, late = boundary(zagg, xlen, theirs, pairs, a_blocks, prolong, sums)
    late = shifted(late, "dom", -1)
    return final(halves, zagg, sums, early, late)


def solution(mesh):
    in_specs = (P("dom", None, "grp", None, None), P("dom", None, "grp", None, None), P(), P())
    out_specs = P("dom", "grp", None, None)
    return jax.shard_map(per_device, mesh=mesh, in_specs=in_specs, out_specs=out_specs, check_vma=False)
```

time: 82.2 us -> 71.3 us (0.87)
  the two profiles are of different devices: /device:TPU:14 before, /device:TPU:16 now
where the time goes in v3:
time: 71.3 us; the launch traced here: 70.9 us
  Pallas kernels  48.4 us (68%)
  starting transfers between devices  16.4 us (23%)
  waiting for transfers between devices  5.91 us (8%)
    pallas_call x1, Pallas kernels, main(): pl.pallas_call(functools.partial(main_kernel, halves), grid=(layers,), in...  32.7 us
    ppermute x6, starting transfers between devices, shifted(): return lax.ppermute(block, axis, route)  16.4 us
    pallas_call x1, Pallas kernels, boundary(): pl.pallas_call(boundary_kernel, grid=(1,), in_specs=[scalars(), scalars()...  7.05 us
    ppermute x6, waiting for transfers between devices, shifted(): return lax.ppermute(block, axis, route)  5.91 us
    pallas_call x1, Pallas kernels, edges(): pl.pallas_call(functools.partial(edge_kernel, halves), grid=(1,), in_spec...  2.98 us
    pallas_call x1, Pallas kernels, pack(): pl.pallas_call(pack_kernel, grid=(1,), in_specs=[vmem_block((1, depth, co...  2.52 us
    pallas_call x1, Pallas kernels, final(): pl.pallas_call(final_kernel, grid=(halves,), in_specs=[scalars(), in_vmem...  1.81 us
  transfers between devices with their start and end apart: 6, of which 2 were waited for; matrix products, arithmetic and copies ran while one was open for 0% of the time, Pallas kernels for 64%

profile of v3, /device:TPU:16, one launch (start us, length us, event | category | flops | bytes accessed | tf_op | source)
XLA Modules:
  0.0 70.9 jit_solution(12609324565580011710)
XLA Ops:
  0.0 1.3 %top.1.after_ref = bf16[7,12,64,128]{3,2,1,0:T(8,128)(2,1)S(1)} custom-call(bf16[4,7,12,64,128]{4,3,2,1,0:T(8,128)(2,1)} %p_ref.7), custom_call_target="tpu_custom_call" | custom-call | tf_op jit(solution)/shard_map/top/pallas_call | solution.py:78
  1.4 0.0 copy-start
  1.4 0.0 copy-start.1
  1.4 3.4 %collective-permute-start = (bf16[7,12,64,128]{3,2,1,0:T(8,128)(2,1)S(1)}, bf16[7,12,64,128]{3,2,1,0:T(8,128)(2,1)S(1)}, u32[]{:S(2)}, u32[]{:S(2)}) collective-permute-start(bf16[7,12,64,128]{3,2,1,0:T(8,128)(2,1)S(1)} %top.1.after_ref), channel_id=1, source_target_pairs={{0,4},{4,8},{8,12},{12,16},{16,20},{20,24},{24,28},{1,5},{5,9},{9,... | collective-permute-start | bytes 4128776 | tf_op jit(solution)/shard_map/ppermute | solution.py:30
  4.8 2.5 %pack.1 = (bf16[7,6,64,128]{3,2,1,0:T(8,128)(2,1)S(1)}, bf16[4,7,64,128]{3,2,1,0:T(8,128)(2,1)S(1)}, bf16[4,7,64,128]{3,2,1,0:T(8,128)(2,1)S(1)}) custom-call(bf16[4,7,12,64,448]{4,3,2,1,0:T(8,128)(2,1)} %a_ref.5, bf16[4,7,12,64,128]{4,3,2,1,0:T(8,128)(2,1)} %p_ref.7, bf16[7,12,64,128]{3,2,1,0:T(8,128)(2,1)S(1)} %top.1.after_ref), custom_call_target="tpu_custom_call" | custom-call | tf_op jit(solution)/shard_map/pack/pallas_call | solution.py:114
  7.3 1.3 %collective-permute-start.3 = (bf16[4,7,64,128]{3,2,1,0:T(8,128)(2,1)S(1)}, bf16[4,7,64,128]{3,2,1,0:T(8,128)(2,1)S(1)}, u32[]{:S(2)}, u32[]{:S(2)}) collective-permute-start(bf16[4,7,64,128]{3,2,1,0:T(8,128)(2,1)S(1)} %get-tuple-element.13.low_edge_ref), channel_id=1, source_target_pairs={{1,0},{2,1},{3,2},{5,4},{6,5},{7,6},{9,8},{10,9},{11,10},{13,12},{... | collective-permute-start | bytes 1376264 | tf_op jit(solution)/shard_map/ppermute | solution.py:30
  8.6 3.1 %collective-permute-start.2 = (bf16[4,7,64,128]{3,2,1,0:T(8,128)(2,1)S(1)}, bf16[4,7,64,128]{3,2,1,0:T(8,128)(2,1)S(1)}, u32[]{:S(2)}, u32[]{:S(2)}) collective-permute-start(bf16[4,7,64,128]{3,2,1,0:T(8,128)(2,1)S(1)} %get-tuple-element.14.high_edge_ref), channel_id=1, source_target_pairs={{0,1},{1,2},{2,3},{4,5},{5,6},{6,7},{8,9},{9,10},{10,11},{12,13},{... | collective-permute-start | bytes 1376264 | tf_op jit(solution)/shard_map/ppermute | solution.py:30
  11.7 3.4 %collective-permute-start.1 = (bf16[7,6,64,128]{3,2,1,0:T(8,128)(2,1)S(1)}, bf16[7,6,64,128]{3,2,1,0:T(8,128)(2,1)S(1)}, u32[]{:S(2)}, u32[]{:S(2)}) collective-permute-start(bf16[7,6,64,128]{3,2,1,0:T(8,128)(2,1)S(1)} %get-tuple-element.12), channel_id=1, source_target_pairs={{0,4},{4,8},{8,12},{12,16},{16,20},{20,24},{24,28},{1,5},{5,9},{9,... | collective-permute-start | bytes 2064392 | tf_op jit(solution)/shard_map/ppermute | solution.py:30
  15.1 0.0 copy-done
  15.2 0.0 copy-done.1
  15.2 32.7 %coarsen.1.old_ref = f32[3,4,5,128,128]{4,3,2,1,0:T(8,128)S(1)} custom-call(s32[32]{0:T(128)S(1)} %copy-done, s32[4,4]{1,0:T(4,128)S(1)} %copy-done.1, bf16[4,7,12,64,448]{4,3,2,1,0:T(8,128)(2,1)} %a_ref.5, bf16[4,7,12,64,128]{4,3,2,1,0:T(8,128)(2,1)} %p_ref.7), custom_call_target="tpu_custom_call" | custom-call | flops 16911433728 | bytes 41943040 | tf_op jit(solution)/shard_map/coarsen/pallas_call | solution.py:263
  47.9 0.0 collective-permute-done.3.right_ref
  47.9 0.0 collective-permute-done.2.left_ref
  47.9 3.0 %edges.1 = (f32[3,4,5,128,128]{4,3,2,1,0:T(8,128)S(1)}, bf16[3,4,128,128]{3,2,1,0:T(8,128)(2,1)S(1)}) custom-call(s32[32]{0:T(128)S(1)} %copy-done, bf16[4,7,12,64,448]{4,3,2,1,0:T(8,128)(2,1)} %a_ref.5, bf16[4,7,12,64,448]{4,3,2,1,0:T(8,128)(2,1)} %a_ref.5, ...), custom_call_target="tpu_custom_call", output_to_operand_aliasing={{0}: (7, {})} | custom-call | tf_op jit(solution)/shard_map/edges/pallas_call | solution.py:317
  50.9 3.3 %collective-permute-start.4 = (bf16[3,4,128,128]{3,2,1,0:T(8,128)(2,1)S(1)}, bf16[3,4,128,128]{3,2,1,0:T(8,128)(2,1)S(1)}, u32[]{:S(2)}, u32[]{:S(2)}) collective-permute-start(bf16[3,4,128,128]{3,2,1,0:T(8,128)(2,1)S(1)} %get-tuple-element.17), channel_id=1, source_target_pairs={{4,0},{8,4},{12,8},{16,12},{20,16},{24,20},{28,24},{5,1},{9,5},{13... | collective-permute-start | bytes 1179656 | tf_op jit(solution)/shard_map/ppermute | solution.py:30
  54.2 0.0 collective-permute-done.1.pairs_ref
  54.2 0.0 collective-permute-done.theirs_ref
  54.2 7.1 %boundary.1 = (f32[3,4,5,128,128]{4,3,2,1,0:T(8,128)S(1)}, bf16[4,128,128]{2,1,0:T(8,128)(2,1)S(1)}) custom-call(s32[32]{0:T(128)S(1)} %copy-done, s32[4,4]{1,0:T(4,128)S(1)} %copy-done.1, bf16[7,12,64,128]{3,2,1,0:T(8,128)(2,1)S(1)} %collective-permute-done.theirs_ref, ...), custom_call_target="tpu_custom_call", output_to_operand_aliasing={{0}: (6, {})} | custom-call | tf_op jit(solution)/shard_map/boundary/pallas_call | solution.py:387
  61.3 1.9 %collective-permute-start.5 = (bf16[4,128,128]{2,1,0:T(8,128)(2,1)S(1)}, bf16[4,128,128]{2,1,0:T(8,128)(2,1)S(1)}, u32[]{:S(2)}, u32[]{:S(2)}) collective-permute-start(bf16[4,128,128]{2,1,0:T(8,128)(2,1)S(1)} %get-tuple-element.18), channel_id=1, source_target_pairs={{4,0},{8,4},{12,8},{16,12},{20,16},{24,20},{28,24},{5,1},{9,5},{13... | collective-permute-start | bytes 393224 | tf_op jit(solution)/shard_map/ppermute | solution.py:30
  63.2 1.4 %collective-permute-done.4.early_ref = bf16[3,4,128,128]{3,2,1,0:T(8,128)(2,1)S(1)} collective-permute-done((bf16[3,4,128,128]{3,2,1,0:T(8,128)(2,1)S(1)}, bf16[3,4,128,128]{3,2,1,0:T(8,128)(2,1)S(1)}, u32[]{:S(2)}, u32[]{:S(2)}) %collective-permute-start.4) | collective-permute-done | bytes 393248 | tf_op jit(solution)/shard_map/ppermute | solution.py:30
  64.6 4.5 %collective-permute-done.5.late_ref = bf16[4,128,128]{2,1,0:T(8,128)(2,1)S(1)} collective-permute-done((bf16[4,128,128]{2,1,0:T(8,128)(2,1)S(1)}, bf16[4,128,128]{2,1,0:T(8,128)(2,1)S(1)}, u32[]{:S(2)}, u32[]{:S(2)}) %collective-permute-start.5) | collective-permute-done | bytes 131104 | tf_op jit(solution)/shard_map/ppermute | solution.py:30
  69.1 1.8 %finish.1 = bf16[2,4,128,640]{3,2,1,0:T(8,128)(2,1)} custom-call(s32[32]{0:T(128)S(1)} %copy-done, f32[3,4,5,128,128]{4,3,2,1,0:T(8,128)S(1)} %get-tuple-element.16.sums_ref, bf16[3,4,128,128]{3,2,1,0:T(8,128)(2,1)S(1)} %collective-permute-done.4.early_ref, bf16[4,128,128]{2,1,0:T(8,128)(2,1)S(1)} %collective-permute-done.5.late_ref), custom_call_target="tpu_custom_call" | custom-call | tf_op jit(solution)/shard_map/finish/pallas_call | solution.py:439
Async XLA Ops:
  1.4 13.8 %copy-start = (s32[32]{0:T(128)S(1)}, s32[32]{0:T(128)}, u32[]{:S(2)}) copy-start(s32[32]{0:T(128)} %zagg_ref.7) | copy-start | bytes 388
  1.4 13.8 %copy-start.1 = (s32[4,4]{1,0:T(4,128)S(1)}, s32[4,4]{1,0:T(4,128)}, u32[]{:S(2)}) copy-start(s32[4,4]{1,0:T(4,128)} %xlen_ref.3) | copy-start | bytes 196
  1.4 52.8 %collective-permute-start = (bf16[7,12,64,128]{3,2,1,0:T(8,128)(2,1)S(1)}, bf16[7,12,64,128]{3,2,1,0:T(8,128)(2,1)S(1)}, u32[]{:S(2)}, u32[]{:S(2)}) collective-permute-start(bf16[7,12,64,128]{3,2,1,0:T(8,128)(2,1)S(1)} %top.1.after_ref), channel_id=1, source_target_pairs={{0,4},{4,8},{8,12},{12,16},{16,20},{20,24},{24,28},{1,5},{5,9},{9,... | collective-permute-start | bytes 4128776 | tf_op jit(solution)/shard_map/ppermute | solution.py:30
  7.3 40.5 %collective-permute-start.3 = (bf16[4,7,64,128]{3,2,1,0:T(8,128)(2,1)S(1)}, bf16[4,7,64,128]{3,2,1,0:T(8,128)(2,1)S(1)}, u32[]{:S(2)}, u32[]{:S(2)}) collective-permute-start(bf16[4,7,64,128]{3,2,1,0:T(8,128)(2,1)S(1)} %get-tuple-element.13.low_edge_ref), channel_id=1, source_target_pairs={{1,0},{2,1},{3,2},{5,4},{6,5},{7,6},{9,8},{10,9},{11,10},{13,12},{... | collective-permute-start | bytes 1376264 | tf_op jit(solution)/shard_map/ppermute | solution.py:30
  8.6 39.2 %collective-permute-start.2 = (bf16[4,7,64,128]{3,2,1,0:T(8,128)(2,1)S(1)}, bf16[4,7,64,128]{3,2,1,0:T(8,128)(2,1)S(1)}, u32[]{:S(2)}, u32[]{:S(2)}) collective-permute-start(bf16[4,7,64,128]{3,2,1,0:T(8,128)(2,1)S(1)} %get-tuple-element.14.high_edge_ref), channel_id=1, source_target_pairs={{0,1},{1,2},{2,3},{4,5},{5,6},{6,7},{8,9},{9,10},{10,11},{12,13},{... | collective-permute-start | bytes 1376264 | tf_op jit(solution)/shard_map/ppermute | solution.py:30
  11.7 42.5 %collective-permute-start.1 = (bf16[7,6,64,128]{3,2,1,0:T(8,128)(2,1)S(1)}, bf16[7,6,64,128]{3,2,1,0:T(8,128)(2,1)S(1)}, u32[]{:S(2)}, u32[]{:S(2)}) collective-permute-start(bf16[7,6,64,128]{3,2,1,0:T(8,128)(2,1)S(1)} %get-tuple-element.12), channel_id=1, source_target_pairs={{0,4},{4,8},{8,12},{12,16},{16,20},{20,24},{24,28},{1,5},{5,9},{9,... | collective-permute-start | bytes 2064392 | tf_op jit(solution)/shard_map/ppermute | solution.py:30
  50.9 13.7 %collective-permute-start.4 = (bf16[3,4,128,128]{3,2,1,0:T(8,128)(2,1)S(1)}, bf16[3,4,128,128]{3,2,1,0:T(8,128)(2,1)S(1)}, u32[]{:S(2)}, u32[]{:S(2)}) collective-permute-start(bf16[3,4,128,128]{3,2,1,0:T(8,128)(2,1)S(1)} %get-tuple-element.17), channel_id=1, source_target_pairs={{4,0},{8,4},{12,8},{16,12},{20,16},{24,20},{28,24},{5,1},{9,5},{13... | collective-permute-start | bytes 1179656 | tf_op jit(solution)/shard_map/ppermute | solution.py:30
  61.3 7.8 %collective-permute-start.5 = (bf16[4,128,128]{2,1,0:T(8,128)(2,1)S(1)}, bf16[4,128,128]{2,1,0:T(8,128)(2,1)S(1)}, u32[]{:S(2)}, u32[]{:S(2)}) collective-permute-start(bf16[4,128,128]{2,1,0:T(8,128)(2,1)S(1)} %get-tuple-element.18), channel_id=1, source_target_pairs={{4,0},{8,4},{12,8},{16,12},{20,16},{24,20},{28,24},{5,1},{9,5},{13... | collective-permute-start | bytes 393224 | tf_op jit(solution)/shard_map/ppermute | solution.py:30

commit v4 on v3

--- a/solution.py
+++ b/solution.py
@@ -127,7 +127,7 @@
     )(a_blocks, prolong, after)
 
 
-def main_kernel(halves, zagg_ref, xlen_ref, a_ref, p_ref, sums_ref, rows_ref):
+def main_kernel(halves, zagg_ref, xlen_ref, a_ref, p_ref, sums_ref, bottom_ref, first_ref, last_ref, rows_ref):
     layers, depth, columns, block, coarse = p_ref.shape
     intervals = sums_ref.shape[1]
     wide = a_ref.shape[-1]
@@ -144,6 +144,17 @@
 
         lax.fori_loop(0, intervals, clear, 0)
 
+        def bottom(x, _):
+            low, high = aligned(5 * block, 6 * block, wide)
+            bottom_ref[:, x] = a_ref[0, :, x, :, low:high]
+            return 0
+
+        lax.fori_loop(0, columns, bottom, 0)
+
+    low, high = aligned(block, 2 * block, wide)
+    first_ref[layer] = a_ref[0, :, 0, :, low:high]
+    low, high = aligned(2 * block, 3 * block, wide)
+    last_ref[layer] = a_ref[0, :, columns - 1, :, low:high]
     rows_ref[...] = jnp.zeros_like(rows_ref)
 
     at = dom * layers + layer
@@ -156,21 +167,30 @@
     same_zp = has_zp & (zagg_ref[jnp.where(has_zp, at + 1, at)] == mine)
     none = jnp.zeros(shape, BF16)
 
+    apart_zm = has_zm & jnp.logical_not(same_zm)
+    apart_zp = has_zp & jnp.logical_not(same_zp)
+    side = jnp.where(apart_zm, 3, 4)
+
     def settle(pending):
         for j in range(2):
             x, interval, slot = pending[j]
             own = p_ref[layer, :, x].reshape(depth * block, coarse)
-            sums_ref[target, interval, slot] += transposed_matmul(own, rows_ref[j])
+            both = transposed_matmul(own, rows_ref[j])
+            sums_ref[target, interval, slot] += both[:, :coarse]
+            sums_ref[target, interval, side] += both[:, coarse:]
 
     def keep(products):
         for y, both in enumerate(products):
             for j in range(2):
                 part = both[j * block : (j + 1) * block, j * coarse : (j + 1) * coarse]
-                rows_ref[j, y * block : (y + 1) * block] = part.astype(BF16)
+                rows_ref[j, y * block : (y + 1) * block, :coarse] = part.astype(BF16)
+                rows_ref[j, y * block : (y + 1) * block, coarse:] = none
 
     def inner(q, pending):
         settle(pending)
         zm_factor, zp_factor = factor(same_zm, shape), factor(same_zp, shape)
+        zm_aside = factor(apart_zm, shape)
+        zp_aside = factor(apart_zp & jnp.logical_not(apart_zm), shape)
         info = []
         for j in range(2):
             x = 2 * q + j
@@ -181,26 +201,22 @@
             same_xp = has_xp & (interval_of(xlen_ref, grp, after) == interval)
             info.append((x, interval, before, after, factor(same_xm, shape), factor(same_xp, shape)))
         products = []
-        for y in range(depth):
-            stacks = []
-            for x, _, before, after, xm_factor, xp_factor in info:
-                stacks.append(
-                    jnp.concatenate(
-                        [
-                            p_ref[layer, y, x],
-                            p_ref[layer, y, before] * xm_factor,
-                            p_ref[layer, y, after] * xp_factor,
-                            p_ref[layer, y - 1, x] if y > 0 else none,
-                            p_ref[layer, y + 1, x] if y < depth - 1 else none,
-                            p_ref[below, y, x] * zm_factor,
-                            p_ref[above, y, x] * zp_factor,
-                        ],
-                        axis=0,
-                    )
-                )
-            left = a_ref[0, y, pl.ds(2 * q, 2)].reshape(2 * block, wide)
-            products.append(matmul(left, jnp.concatenate(stacks, axis=1)))
-        keep(products)
+        for j, (x, _, before, after, xm_factor, xp_factor) in enumerate(info):
+            for y in range(depth):
+                lower, upper = p_ref[below, y, x], p_ref[above, y, x]
+                stack = [
+                    (p_ref[layer, y, x], none),
+                    (p_ref[layer, y, before] * xm_factor, none),
+                    (p_ref[layer, y, after] * xp_factor, none),
+                    (p_ref[layer, y - 1, x] if y > 0 else none, none),
+                    (p_ref[layer, y + 1, x] if y < depth - 1 else none, none),
+                    (lower * zm_factor, lower * zm_aside),
+                    (upper * zp_factor, upper * zp_aside),
+                ]
+                stack = jnp.concatenate([jnp.concatenate(row, axis=1) for row in stack], axis=0)
+                products.append((j, y, matmul(a_ref[0, y, 2 * q + j], stack)))
+        for j, y, both in products:
+            rows_ref[j, y * block : (y + 1) * block] = both.astype(BF16)
         return tuple((i[0], i[1], jnp.int32(0)) for i in info)
 
     def across_x(i, pending):
@@ -246,9 +262,7 @@
     pairs = columns // 2
     pending = lax.fori_loop(0, pairs, inner, pending)
     pending = lax.fori_loop(0, intervals - 1, across_x, pending)
-    pairs_zm = jnp.where(has_zm & jnp.logical_not(same_zm), pairs, 0)
-    pairs_zp = jnp.where(has_zp & jnp.logical_not(same_zp), pairs, 0)
-    pending = lax.fori_loop(0, pairs_zm, across_z(5, 3, below), pending)
+    pairs_zp = jnp.where(apart_zm & apart_zp, pairs, 0)
     pending = lax.fori_loop(0, pairs_zp, across_z(6, 4, above), pending)
     settle(pending)
 
@@ -267,11 +281,16 @@
             scalars(),
             scalars(),
             pl.BlockSpec((1, depth, columns, block, a_blocks.shape[-1]), lambda i: (i, 0, 0, 0, 0)),
-            pl.BlockSpec(prolong.shape, lambda i: (0,) * 5, pipeline_mode=pl.Buffered(1)),
+            in_vmem(),
         ],
-        out_specs=in_vmem(),
-        out_shape=sums_shape(halves, xlen.shape[1], coarse),
-        scratch_shapes=[pltpu.VMEM((2, depth * block, coarse), BF16)],
+        out_specs=[in_vmem()] * 4,
+        out_shape=[
+            sums_shape(halves, xlen.shape[1], coarse),
+            jax.ShapeDtypeStruct((depth, columns, block, LANES), BF16),
+            jax.ShapeDtypeStruct((layers, depth, block, LANES), BF16),
+            jax.ShapeDtypeStruct((layers, depth, block, LANES), BF16),
+        ],
+        scratch_shapes=[pltpu.VMEM((2, depth * block, 2 * coarse), BF16)],
         cost_estimate=pl.CostEstimate(flops=flops * 4, bytes_accessed=40 << 20, transcendentals=0),
         compiler_params=pltpu.CompilerParams(vmem_limit_bytes=LIMIT),
         name="coarsen",
@@ -292,8 +311,8 @@
         for y in range(depth):
             first = diagonal([left_ref[layer, y]], low_first, block, high_first)
             last = diagonal([right_ref[layer, y]], low_last, 2 * block, high_last)
-            rows[0].append(matmul(first_ref[layer, y, 0], first).astype(BF16))
-            rows[1].append(matmul(last_ref[layer, y, 0], last).astype(BF16))
+            rows[0].append(matmul(first_ref[layer, y], first).astype(BF16))
+            rows[1].append(matmul(last_ref[layer, y], last).astype(BF16))
         own = [low_edge_ref[layer].reshape(depth * block, coarse), high_edge_ref[layer].reshape(depth * block, coarse)]
         sums_ref[target, 0, 1] += transposed_matmul(own[0], jnp.concatenate(rows[0], axis=0))
         sums_ref[target, intervals - 1, 2] += transposed_matmul(own[1], jnp.concatenate(rows[1], axis=0))
@@ -309,64 +328,85 @@
     lax.fori_loop(0, intervals, emit, 0)
 
 
-def edges(halves, zagg, a_blocks, low_edge, high_edge, left, right, sums):
-    layers, depth, columns, block, _ = a_blocks.shape
+def edges(halves, zagg, pieces, low_edge, high_edge, left, right, sums):
     intervals, coarse = sums.shape[1], sums.shape[-1]
-    lanes = [aligned(k * block, (k + 1) * block, 7 * block)[0] // LANES for k in (1, 2)]
-    shape = (layers, depth, 1, block, LANES)
     return pl.pallas_call(
         functools.partial(edge_kernel, halves),
-        grid=(1,),
-        in_specs=[
-            scalars(),
-            vmem_block(shape, (0, 0, 0, 0, lanes[0])),
-            vmem_block(shape, (0, 0, columns - 1, 0, lanes[1])),
-        ]
-        + [in_vmem()] * 5,
+        in_specs=[scalars()] + [in_vmem()] * 7,
         out_specs=[in_vmem()] * 2,
         out_shape=[sums, jax.ShapeDtypeStruct((3, intervals, coarse, coarse), BF16)],
         input_output_aliases={7: 0},
         compiler_params=pltpu.CompilerParams(vmem_limit_bytes=LIMIT),
         name="edges",
-    )(zagg, a_blocks, a_blocks, low_edge, high_edge, left, right, sums)
-
-
-def boundary_kernel(zagg_ref, xlen_ref, theirs_ref, pairs_ref, a_ref, p_ref, old_ref, sums_ref, late_ref, upper_ref, lower_ref):
+    )(zagg, *pieces, low_edge, high_edge, left, right, sums)
+
+
+def lower_kernel(xlen_ref, theirs_ref, a_ref, own_ref, lower_ref):
+    depth, columns, block, coarse = theirs_ref.shape
+    grp = lax.axis_index("grp")
+    lower_ref[...] = jnp.zeros_like(lower_ref)
+    low, high = aligned(5 * block, 6 * block, 7 * block)
+
+    group = 2 if columns % 4 == 0 else 1
+
+    def body(step, _):
+        rows = []
+        for n in range(group):
+            q = group * step + n
+            parts = [[], []]
+            for y in range(depth):
+                theirs = jnp.concatenate([theirs_ref[y, 2 * q + j] for j in range(2)], axis=1)
+                left = a_ref[y, pl.ds(2 * q, 2)].reshape(2 * block, high - low)
+                both = matmul(left, diagonal([theirs], low, 5 * block, high))
+                for j in range(2):
+                    part = both[j * block : (j + 1) * block, j * coarse : (j + 1) * coarse]
+                    parts[j].append(part.astype(BF16))
+            rows.extend(jnp.concatenate(part, axis=0) for part in parts)
+        for n, right in enumerate(rows):
+            x = 2 * group * step + n
+            own = own_ref[0, :, x].reshape(depth * block, coarse)
+            lower_ref[interval_of(xlen_ref, grp, x)] += transposed_matmul(own, right)
+        return 0
+
+    lax.fori_loop(0, columns // (2 * group), body, 0)
+
+
+def lower_sums(xlen, theirs, bottom, prolong):
+    coarse = prolong.shape[-1]
+    return pl.pallas_call(
+        lower_kernel,
+        in_specs=[scalars()] + [in_vmem()] * 3,
+        out_specs=in_vmem(),
+        out_shape=jax.ShapeDtypeStruct((xlen.shape[1], coarse, coarse), F32),
+        compiler_params=pltpu.CompilerParams(vmem_limit_bytes=LIMIT),
+        name="lower",
+    )(xlen, theirs, bottom, prolong)
+
+
+def upper_kernel(zagg_ref, xlen_ref, theirs_ref, pairs_ref, own_ref, lower_ref, old_ref, sums_ref, late_ref, upper_ref):
     depth, columns, block, coarse = theirs_ref.shape
     dom, grp = lax.axis_index("dom"), lax.axis_index("grp")
     upper_ref[...] = jnp.zeros_like(upper_ref)
-    lower_ref[...] = jnp.zeros_like(lower_ref)
-    low, high = aligned(5 * block, 6 * block, 7 * block)
-
-    def upper(q, _):
-        rows = [[], []]
-        for y in range(depth):
-            mine = [p_ref[0, y, 2 * q + j] for j in range(2)]
-            both = matmul(pairs_ref[y, q], diagonal(mine, 0, 0, 2 * block))
-            for j in range(2):
-                rows[j].append(both[:, j * coarse : (j + 1) * coarse].astype(BF16))
-        for j in range(2):
-            theirs = theirs_ref[:, 2 * q + j].reshape(depth * block, coarse)
-            at = interval_of(xlen_ref, grp, 2 * q + j)
-            upper_ref[at] += transposed_matmul(theirs, jnp.concatenate(rows[j], axis=0))
+    group = 2 if columns % 4 == 0 else 1
+
+    def body(step, _):
+        rows = []
+        for n in range(group):
+            q = group * step + n
+            halves = [[], []]
+            for y in range(depth):
+                mine = [own_ref[0, y, 2 * q + j] for j in range(2)]
+                both = matmul(pairs_ref[y, q], diagonal(mine, 0, 0, 2 * block))
+                for j in range(2):
+                    halves[j].append(both[:, j * coarse : (j + 1) * coarse].astype(BF16))
+            rows.extend(jnp.concatenate(half, axis=0) for half in halves)
+        for n, right in enumerate(rows):
+            x = 2 * group * step + n
+            theirs = theirs_ref[:, x].reshape(depth * block, coarse)
+            upper_ref[interval_of(xlen_ref, grp, x)] += transposed_matmul(theirs, right)
         return 0
 
-    def lower(q, _):
-        rows = [[], []]
-        for y in range(depth):
-            theirs = jnp.concatenate([theirs_ref[y, 2 * q + j] for j in range(2)], axis=1)
-            left = a_ref[0, y, pl.ds(2 * q, 2)].reshape(2 * block, high - low)
-            both = matmul(left, diagonal([theirs], low, 5 * block, high))
-            for j in range(2):
-                rows[j].append(both[j * block : (j + 1) * block, j * coarse : (j + 1) * coarse].astype(BF16))
-        for j in range(2):
-            own = p_ref[0, :, 2 * q + j].reshape(depth * block, coarse)
-            at = interval_of(xlen_ref, grp, 2 * q + j)
-            lower_ref[at] += transposed_matmul(own, jnp.concatenate(rows[j], axis=0))
-        return 0
-
-    lax.fori_loop(0, columns // 2, upper, 0)
-    lax.fori_loop(0, columns // 2, lower, 0)
+    lax.fori_loop(0, columns // (2 * group), body, 0)
     layers = zagg_ref.shape[0] // lax.axis_size("dom")
     at = dom * layers
     same = (at > 0) & (zagg_ref[jnp.where(at > 0, at - 1, 0)] == zagg_ref[at])
@@ -380,88 +420,90 @@
     lax.fori_loop(0, late_ref.shape[0], emit, 0)
 
 
-def boundary(zagg, xlen, theirs, pairs, a_blocks, prolong, sums):
-    _, depth, columns, block, coarse = prolong.shape
-    low, high = aligned(5 * block, 6 * block, 7 * block)
-    late = jax.ShapeDtypeStruct((xlen.shape[1], coarse, coarse), BF16)
-    return pl.pallas_call(
-        boundary_kernel,
-        grid=(1,),
-        in_specs=[
-            scalars(),
-            scalars(),
-            in_vmem(),
-            in_vmem(),
-            vmem_block((1, depth, columns, block, high - low), (0, 0, 0, 0, low // LANES)),
-            vmem_block((1, depth, columns, block, coarse), (0, 0, 0, 0, 0)),
-            in_vmem(),
-        ],
+def upper_sums(zagg, xlen, theirs, pairs, own, lower, sums):
+    late = jax.ShapeDtypeStruct(lower.shape, BF16)
+    return pl.pallas_call(
+        upper_kernel,
+        in_specs=[scalars(), scalars()] + [in_vmem()] * 5,
         out_specs=[in_vmem()] * 2,
         out_shape=[sums, late],
-        scratch_shapes=[pltpu.VMEM(late.shape, F32)] * 2,
+        scratch_shapes=[pltpu.VMEM(late.shape, F32)],
         input_output_aliases={6: 0},
         compiler_params=pltpu.CompilerParams(vmem_limit_bytes=LIMIT),
-        name="boundary",
-    )(zagg, xlen, theirs, pairs, a_blocks, prolong, sums)
-
-
-def final_kernel(zagg_ref, sums_ref, early_ref, late_ref, out_ref):
+        name="upper",
+    )(zagg, xlen, theirs, pairs, own, lower, sums)
+
+
+def owned_kernel(sums_ref, out_ref):
     coarse = sums_ref.shape[-1]
+    half, i = pl.program_id(0), pl.program_id(1)
+    for slot in range(sums_ref.shape[2]):
+        out_ref[0, 0, :, slot * coarse : (slot + 1) * coarse] = sums_ref[half + 1, i, slot].astype(BF16)
+
+
+def last_kernel(zagg_ref, sums_ref, early_ref, late_ref, old_ref, out_ref):
+    halves, coarse = sums_ref.shape[0] - 1, sums_ref.shape[-1]
     dom = lax.axis_index("dom")
-    layers = zagg_ref.shape[0] // lax.axis_size("dom")
-    half, halves = pl.program_id(0), pl.num_programs(0)
-    last = half == halves - 1
-    end = (dom + 1) * layers
+    end = (dom + 1) * (zagg_ref.shape[0] // lax.axis_size("dom"))
     following = jnp.where(end < zagg_ref.shape[0], end, end - 1)
-    same = zagg_ref[following] == zagg_ref[end - 1]
-    early_factor = jnp.where(last, 1.0, 0.0)
-    self_factor = jnp.where(last & same, 1.0, 0.0)
-    above_factor = jnp.where(last & jnp.logical_not(same), 1.0, 0.0)
-
-    def body(i, _):
-        def put(slot, value):
-            out_ref[0, i, :, slot * coarse : (slot + 1) * coarse] = value.astype(BF16)
-
-        late = late_ref[i].astype(F32)
-        early = [early_factor * early_ref[n, i].astype(F32) for n in range(3)]
-        put(0, sums_ref[half + 1, i, 0] + self_factor * late)
-        put(1, sums_ref[half + 1, i, 1] + early[0])
-        put(2, sums_ref[half + 1, i, 2] + early[1])
-        put(3, sums_ref[half + 1, i, 3])
-        put(4, sums_ref[half + 1, i, 4] + early[2] + above_factor * late)
-        return 0
-
-    lax.fori_loop(0, out_ref.shape[1], body, 0)
-
-
-def final(halves, zagg, sums, early, late):
+    self_factor = jnp.where(zagg_ref[following] == zagg_ref[end - 1], 1.0, 0.0)
+    i = pl.program_id(0)
+    late = late_ref[i].astype(F32)
+    more = {
+        0: self_factor * late,
+        1: early_ref[0, i].astype(F32),
+        2: early_ref[1, i].astype(F32),
+        4: early_ref[2, i].astype(F32) + (1.0 - self_factor) * late,
+    }
+    for slot in range(sums_ref.shape[2]):
+        value = sums_ref[halves, i, slot]
+        value = value + more[slot] if slot in more else value
+        out_ref[0, 0, :, slot * coarse : (slot + 1) * coarse] = value.astype(BF16)
+
+
+def owned(halves, sums):
     _, intervals, slots, coarse, _ = sums.shape
     return pl.pallas_call(
-        final_kernel,
-        grid=(halves,),
-        in_specs=[scalars(), in_vmem(), in_vmem(), in_vmem()],
-        out_specs=pl.BlockSpec((1, intervals, coarse, slots * coarse), lambda h: (h, 0, 0, 0)),
+        owned_kernel,
+        grid=(halves - 1, intervals),
+        in_specs=[in_vmem()],
+        out_specs=pl.BlockSpec((1, 1, coarse, slots * coarse), lambda h, i: (h, i, 0, 0)),
         out_shape=jax.ShapeDtypeStruct((halves, intervals, coarse, slots * coarse), BF16),
         compiler_params=pltpu.CompilerParams(vmem_limit_bytes=LIMIT),
+        name="owned",
+    )(sums)
+
+
+def last(halves, zagg, sums, early, late, out):
+    _, intervals, slots, coarse, _ = sums.shape
+    return pl.pallas_call(
+        last_kernel,
+        grid=(intervals,),
+        in_specs=[scalars(), in_vmem(), in_vmem(), in_vmem(), pl.BlockSpec(memory_space=pl.ANY)],
+        out_specs=pl.BlockSpec((1, 1, coarse, slots * coarse), lambda i: (halves - 1, i, 0, 0)),
+        out_shape=out,
+        input_output_aliases={4: 0},
+        compiler_params=pltpu.CompilerParams(vmem_limit_bytes=LIMIT),
         name="finish",
-    )(zagg, sums, early, late)
+    )(zagg, sums, early, late, out)
 
 
 def per_device(a_blocks, prolong, zagg, xlen):
     halves = prolong.shape[0] // 2
-    prolong = pltpu.with_memory_space_constraint(prolong, pltpu.HBM)
-    rows = top(prolong)
+    outside = pltpu.with_memory_space_constraint(prolong, pltpu.HBM)
+    rows = top(outside)
     theirs = shifted(rows, "dom", 1)
-    pairs, low_edge, high_edge = pack(a_blocks, prolong, rows)
+    pairs, low_edge, high_edge = pack(a_blocks, outside, rows)
     pairs = shifted(pairs, "dom", 1)
     left = shifted(high_edge, "grp", 1)
     right = shifted(low_edge, "grp", -1)
-    sums = main(halves, zagg, xlen, a_blocks, prolong)
-    sums, early = edges(halves, zagg, a_blocks, low_edge, high_edge, left, right, sums)
+    sums, bottom, *pieces = main(halves, zagg, xlen, a_blocks, prolong)
+    sums, early = edges(halves, zagg, pieces, low_edge, high_edge, left, right, sums)
+    lower = lower_sums(xlen, theirs, bottom, prolong)
     early = shifted(early, "dom", -1)
-    sums, late = boundary(zagg, xlen, theirs, pairs, a_blocks, prolong, sums)
+    sums, late = upper_sums(zagg, xlen, theirs, pairs, prolong, lower, sums)
     late = shifted(late, "dom", -1)
-    return final(halves, zagg, sums, early, late)
+    return last(halves, zagg, sums, early, late, owned(halves, sums))
 
 
 def solution(mesh):

time: 71.3 us -> 71 us (level)
  the two profiles are of different devices: /device:TPU:16 before, /device:TPU:14 now
where the time goes in v4:
time: 71 us; the launch traced here: 70.6 us
  Pallas kernels  40.9 us (58%)
  starting transfers between devices  15.2 us (21%)
  waiting for transfers between devices  14.4 us (20%)
    pallas_call x1, Pallas kernels, main(): pl.pallas_call(functools.partial(main_kernel, halves), grid=(layers,), in...  26.6 us
    ppermute x6, starting transfers between devices, shifted(): return lax.ppermute(block, axis, route)  15.2 us
    ppermute x6, waiting for transfers between devices, shifted(): return lax.ppermute(block, axis, route)  14.4 us
    pallas_call x1, Pallas kernels, pack(): pl.pallas_call(pack_kernel, grid=(1,), in_specs=[vmem_block((1, depth, co...  2.52 us
    pallas_call x1, Pallas kernels, lower_sums(): pl.pallas_call(lower_kernel, in_specs=[scalars()] + [in_vmem()] * 3, out_...  2.31 us
    pallas_call x1, Pallas kernels, edges(): pl.pallas_call(functools.partial(edge_kernel, halves), in_specs=[scalars(...  2.3 us
    pallas_call x1, Pallas kernels, upper_sums(): pl.pallas_call(upper_kernel, in_specs=[scalars(), scalars()] + [in_vmem()...  2.17 us
    pallas_call x1, Pallas kernels, last(): pl.pallas_call(last_kernel, grid=(intervals,), in_specs=[scalars(), in_vm...  2.04 us
  transfers between devices with their start and end apart: 6, of which 2 were waited for; matrix products, arithmetic and copies ran while one was open for 0% of the time, Pallas kernels for 53%

profile of v4, /device:TPU:14, one launch (start us, length us, event | category | flops | bytes accessed | tf_op | source)
XLA Modules:
  0.0 70.6 jit_solution(16831167319956209076)
XLA Ops:
  0.0 1.5 %top.1.after_ref = bf16[7,12,64,128]{3,2,1,0:T(8,128)(2,1)S(1)} custom-call(bf16[4,7,12,64,128]{4,3,2,1,0:T(8,128)(2,1)} %own_ref.3), custom_call_target="tpu_custom_call" | custom-call | tf_op jit(solution)/shard_map/top/pallas_call | solution.py:78
  1.5 0.0 slice-start.1
  1.5 0.0 copy-start
  1.5 0.0 copy-start.1
  1.5 3.6 %collective-permute-start = (bf16[7,12,64,128]{3,2,1,0:T(8,128)(2,1)S(1)}, bf16[7,12,64,128]{3,2,1,0:T(8,128)(2,1)S(1)}, u32[]{:S(2)}, u32[]{:S(2)}) collective-permute-start(bf16[7,12,64,128]{3,2,1,0:T(8,128)(2,1)S(1)} %top.1.after_ref), channel_id=1, source_target_pairs={{0,4},{4,8},{8,12},{12,16},{16,20},{20,24},{24,28},{1,5},{5,9},{9,... | collective-permute-start | bytes 4128776 | tf_op jit(solution)/shard_map/ppermute | solution.py:30
  5.1 2.5 %pack.1 = (bf16[7,6,64,128]{3,2,1,0:T(8,128)(2,1)S(1)}, bf16[4,7,64,128]{3,2,1,0:T(8,128)(2,1)S(1)}, bf16[4,7,64,128]{3,2,1,0:T(8,128)(2,1)S(1)}) custom-call(bf16[4,7,12,64,448]{4,3,2,1,0:T(8,128)(2,1)} %a_ref.3, bf16[4,7,12,64,128]{4,3,2,1,0:T(8,128)(2,1)} %own_ref.3, bf16[7,12,64,128]{3,2,1,0:T(8,128)(2,1)S(1)} %top.1.after_ref), custom_call_target="tpu_custom_call" | custom-call | tf_op jit(solution)/shard_map/pack/pallas_call | solution.py:114
  7.6 1.9 %collective-permute-start.3 = (bf16[4,7,64,128]{3,2,1,0:T(8,128)(2,1)S(1)}, bf16[4,7,64,128]{3,2,1,0:T(8,128)(2,1)S(1)}, u32[]{:S(2)}, u32[]{:S(2)}) collective-permute-start(bf16[4,7,64,128]{3,2,1,0:T(8,128)(2,1)S(1)} %get-tuple-element.20.low_edge_ref), channel_id=1, source_target_pairs={{1,0},{2,1},{3,2},{5,4},{6,5},{7,6},{9,8},{10,9},{11,10},{13,12},{... | collective-permute-start | bytes 1376264 | tf_op jit(solution)/shard_map/ppermute | solution.py:30
  9.6 2.4 %collective-permute-start.2 = (bf16[4,7,64,128]{3,2,1,0:T(8,128)(2,1)S(1)}, bf16[4,7,64,128]{3,2,1,0:T(8,128)(2,1)S(1)}, u32[]{:S(2)}, u32[]{:S(2)}) collective-permute-start(bf16[4,7,64,128]{3,2,1,0:T(8,128)(2,1)S(1)} %get-tuple-element.21.high_edge_ref), channel_id=1, source_target_pairs={{0,1},{1,2},{2,3},{4,5},{5,6},{6,7},{8,9},{9,10},{10,11},{12,13},{... | collective-permute-start | bytes 1376264 | tf_op jit(solution)/shard_map/ppermute | solution.py:30
  12.0 3.4 %collective-permute-start.1 = (bf16[7,6,64,128]{3,2,1,0:T(8,128)(2,1)S(1)}, bf16[7,6,64,128]{3,2,1,0:T(8,128)(2,1)S(1)}, u32[]{:S(2)}, u32[]{:S(2)}) collective-permute-start(bf16[7,6,64,128]{3,2,1,0:T(8,128)(2,1)S(1)} %get-tuple-element.16), channel_id=1, source_target_pairs={{0,4},{4,8},{8,12},{12,16},{16,20},{20,24},{24,28},{1,5},{5,9},{9,... | collective-permute-start | bytes 2064392 | tf_op jit(solution)/shard_map/ppermute | solution.py:30
  15.4 0.0 slice-done
  15.5 26.6 %coarsen.1 = (f32[3,4,5,128,128]{4,3,2,1,0:T(8,128)S(1)}, bf16[7,12,64,128]{3,2,1,0:T(8,128)(2,1)S(1)}, bf16[4,7,64,128]{3,2,1,0:T(8,128)(2,1)S(1)}, bf16[4,7,64,128]{3,2,1,0:T(8,128)(2,1)S(1)}) custom-call(s32[32]{0:T(128)S(1)} %copy-done.1, s32[4,4]{1,0:T(4,128)S(1)} %copy-done, bf16[4,7,12,64,448]{4,3,2,1,0:T(8,128)(2,1)} %a_ref.3, ...), custom_call_target="tpu_custom_call" | custom-call | flops 16911433728 | bytes 41943040 | tf_op jit(solution)/shard_map/coarsen/pallas_call | solution.py:277
  42.1 0.0 collective-permute-done.3.right_ref
  42.1 0.0 collective-permute-done.2.left_ref
  42.1 2.3 %edges.1 = (f32[3,4,5,128,128]{4,3,2,1,0:T(8,128)S(1)}, bf16[3,4,128,128]{3,2,1,0:T(8,128)(2,1)S(1)}) custom-call(s32[32]{0:T(128)S(1)} %copy-done.1, bf16[4,7,64,128]{3,2,1,0:T(8,128)(2,1)S(1)} %get-tuple-element.18.first_ref, bf16[4,7,64,128]{3,2,1,0:T(8,128)(2,1)S(1)} %get-tuple-element.19.last_ref, ...), custom_call_target="tpu_custom_call", output_to_operand_aliasing={{0}: (7, {})} | custom-call | tf_op jit(solution)/shard_map/edges/pallas_call | solution.py:333
  44.4 1.9 %collective-permute-start.4 = (bf16[3,4,128,128]{3,2,1,0:T(8,128)(2,1)S(1)}, bf16[3,4,128,128]{3,2,1,0:T(8,128)(2,1)S(1)}, u32[]{:S(2)}, u32[]{:S(2)}) collective-permute-start(bf16[3,4,128,128]{3,2,1,0:T(8,128)(2,1)S(1)} %get-tuple-element.25), channel_id=1, source_target_pairs={{4,0},{8,4},{12,8},{16,12},{20,16},{24,20},{28,24},{5,1},{9,5},{13... | collective-permute-start | bytes 1179656 | tf_op jit(solution)/shard_map/ppermute | solution.py:30
  46.4 0.0 collective-permute-done.theirs_ref
  46.4 2.3 %lower.1.lower_ref = f32[4,128,128]{2,1,0:T(8,128)S(1)} custom-call(s32[4,4]{1,0:T(4,128)S(1)} %copy-done, bf16[7,12,64,128]{3,2,1,0:T(8,128)(2,1)S(1)} %collective-permute-done.theirs_ref, bf16[7,12,64,128]{3,2,1,0:T(8,128)(2,1)S(1)} %get-tuple-element.17.a_ref, bf16[4,7,12,64,128]{4,3,2,1,0:T(8,128)(2,1)S(1)} %bitcast.1), custom_call_target="tpu_custom_call" | custom-call | tf_op jit(solution)/shard_map/lower/pallas_call | solution.py:376
  48.7 10.0 %collective-permute-done.1.pairs_ref = bf16[7,6,64,128]{3,2,1,0:T(8,128)(2,1)S(1)} collective-permute-done((bf16[7,6,64,128]{3,2,1,0:T(8,128)(2,1)S(1)}, bf16[7,6,64,128]{3,2,1,0:T(8,128)(2,1)S(1)}, u32[]{:S(2)}, u32[]{:S(2)}) %collective-permute-start.1) | collective-permute-done | bytes 688160 | tf_op jit(solution)/shard_map/ppermute | solution.py:30
  58.7 2.2 %upper.1 = (f32[3,4,5,128,128]{4,3,2,1,0:T(8,128)S(1)}, bf16[4,128,128]{2,1,0:T(8,128)(2,1)S(1)}) custom-call(s32[32]{0:T(128)S(1)} %copy-done.1, s32[4,4]{1,0:T(4,128)S(1)} %copy-done, bf16[7,12,64,128]{3,2,1,0:T(8,128)(2,1)S(1)} %collective-permute-done.theirs_ref, ...), custom_call_target="tpu_custom_call", output_to_operand_aliasing={{0}: (6, {})} | custom-call | tf_op jit(solution)/shard_map/upper/pallas_call | solution.py:425
  60.8 1.9 %collective-permute-start.5 = (bf16[4,128,128]{2,1,0:T(8,128)(2,1)S(1)}, bf16[4,128,128]{2,1,0:T(8,128)(2,1)S(1)}, u32[]{:S(2)}, u32[]{:S(2)}) collective-permute-start(bf16[4,128,128]{2,1,0:T(8,128)(2,1)S(1)} %get-tuple-element.26), channel_id=1, source_target_pairs={{4,0},{8,4},{12,8},{16,12},{20,16},{24,20},{28,24},{5,1},{9,5},{13... | collective-permute-start | bytes 393224 | tf_op jit(solution)/shard_map/ppermute | solution.py:30
  62.8 1.5 %owned.1.old_ref = bf16[2,4,128,640]{3,2,1,0:T(8,128)(2,1)} custom-call(f32[3,4,5,128,128]{4,3,2,1,0:T(8,128)S(1)} %get-tuple-element.24.sums_ref), custom_call_target="tpu_custom_call" | custom-call | tf_op jit(solution)/shard_map/owned/pallas_call | solution.py:466
  64.2 0.0 collective-permute-done.4.early_ref
  64.2 4.4 %collective-permute-done.5.late_ref = bf16[4,128,128]{2,1,0:T(8,128)(2,1)S(1)} collective-permute-done((bf16[4,128,128]{2,1,0:T(8,128)(2,1)S(1)}, bf16[4,128,128]{2,1,0:T(8,128)(2,1)S(1)}, u32[]{:S(2)}, u32[]{:S(2)}) %collective-permute-start.5) | collective-permute-done | bytes 131104 | tf_op jit(solution)/shard_map/ppermute | solution.py:30
  68.6 2.0 %finish.1 = bf16[2,4,128,640]{3,2,1,0:T(8,128)(2,1)} custom-call(s32[32]{0:T(128)S(1)} %copy-done.1, f32[3,4,5,128,128]{4,3,2,1,0:T(8,128)S(1)} %get-tuple-element.24.sums_ref, bf16[3,4,128,128]{3,2,1,0:T(8,128)(2,1)S(1)} %collective-permute-done.4.early_ref, ...), custom_call_target="tpu_custom_call", output_to_operand_aliasing={{}: (4, {})} | custom-call | tf_op jit(solution)/shard_map/finish/pallas_call | solution.py:479
  (5 shorter events, 0.0 us)
Async XLA Ops:
  0.0 15.4 %slice-start = ((s8[5505024]{0:T(1024)(128)(4,1)}), s8[4194304]{0:T(1024)(128)(4,1)S(1)}, s32[]{:S(2)}) async-start(s8[5505024]{0:T(1024)(128)(4,1)} %bitcast), calls=%async_computation | async-start | bytes 8388608
  1.5 13.9 %slice-start.1 = ((s8[5505024]{0:T(1024)(128)(4,1)}), s8[1310720]{0:T(1024)(128)(4,1)S(1)}, s32[]{:S(2)}) async-start(s8[5505024]{0:T(1024)(128)(4,1)} %bitcast), calls=%async_computation.1 | async-start | bytes 2621440
  1.5 13.9 %copy-start = (s32[4,4]{1,0:T(4,128)S(1)}, s32[4,4]{1,0:T(4,128)}, u32[]{:S(2)}) copy-start(s32[4,4]{1,0:T(4,128)} %xlen_ref.5) | copy-start | bytes 196
  1.5 13.9 %copy-start.1 = (s32[32]{0:T(128)S(1)}, s32[32]{0:T(128)}, u32[]{:S(2)}) copy-start(s32[32]{0:T(128)} %zagg_ref.7) | copy-start | bytes 388
  1.5 44.8 %collective-permute-start = (bf16[7,12,64,128]{3,2,1,0:T(8,128)(2,1)S(1)}, bf16[7,12,64,128]{3,2,1,0:T(8,128)(2,1)S(1)}, u32[]{:S(2)}, u32[]{:S(2)}) collective-permute-start(bf16[7,12,64,128]{3,2,1,0:T(8,128)(2,1)S(1)} %top.1.after_ref), channel_id=1, source_target_pairs={{0,4},{4,8},{8,12},{12,16},{16,20},{20,24},{24,28},{1,5},{5,9},{9,... | collective-permute-start | bytes 4128776 | tf_op jit(solution)/shard_map/ppermute | solution.py:30
  7.6 34.5 %collective-permute-start.3 = (bf16[4,7,64,128]{3,2,1,0:T(8,128)(2,1)S(1)}, bf16[4,7,64,128]{3,2,1,0:T(8,128)(2,1)S(1)}, u32[]{:S(2)}, u32[]{:S(2)}) collective-permute-start(bf16[4,7,64,128]{3,2,1,0:T(8,128)(2,1)S(1)} %get-tuple-element.20.low_edge_ref), channel_id=1, source_target_pairs={{1,0},{2,1},{3,2},{5,4},{6,5},{7,6},{9,8},{10,9},{11,10},{13,12},{... | collective-permute-start | bytes 1376264 | tf_op jit(solution)/shard_map/ppermute | solution.py:30
  9.6 32.5 %collective-permute-start.2 = (bf16[4,7,64,128]{3,2,1,0:T(8,128)(2,1)S(1)}, bf16[4,7,64,128]{3,2,1,0:T(8,128)(2,1)S(1)}, u32[]{:S(2)}, u32[]{:S(2)}) collective-permute-start(bf16[4,7,64,128]{3,2,1,0:T(8,128)(2,1)S(1)} %get-tuple-element.21.high_edge_ref), channel_id=1, source_target_pairs={{0,1},{1,2},{2,3},{4,5},{5,6},{6,7},{8,9},{9,10},{10,11},{12,13},{... | collective-permute-start | bytes 1376264 | tf_op jit(solution)/shard_map/ppermute | solution.py:30
  12.0 46.7 %collective-permute-start.1 = (bf16[7,6,64,128]{3,2,1,0:T(8,128)(2,1)S(1)}, bf16[7,6,64,128]{3,2,1,0:T(8,128)(2,1)S(1)}, u32[]{:S(2)}, u32[]{:S(2)}) collective-permute-start(bf16[7,6,64,128]{3,2,1,0:T(8,128)(2,1)S(1)} %get-tuple-element.16), channel_id=1, source_target_pairs={{0,4},{4,8},{8,12},{12,16},{16,20},{20,24},{24,28},{1,5},{5,9},{9,... | collective-permute-start | bytes 2064392 | tf_op jit(solution)/shard_map/ppermute | solution.py:30
  44.4 19.8 %collective-permute-start.4 = (bf16[3,4,128,128]{3,2,1,0:T(8,128)(2,1)S(1)}, bf16[3,4,128,128]{3,2,1,0:T(8,128)(2,1)S(1)}, u32[]{:S(2)}, u32[]{:S(2)}) collective-permute-start(bf16[3,4,128,128]{3,2,1,0:T(8,128)(2,1)S(1)} %get-tuple-element.25), channel_id=1, source_target_pairs={{4,0},{8,4},{12,8},{16,12},{20,16},{24,20},{28,24},{5,1},{9,5},{13... | collective-permute-start | bytes 1179656 | tf_op jit(solution)/shard_map/ppermute | solution.py:30
  60.8 7.8 %collective-permute-start.5 = (bf16[4,128,128]{2,1,0:T(8,128)(2,1)S(1)}, bf16[4,128,128]{2,1,0:T(8,128)(2,1)S(1)}, u32[]{:S(2)}, u32[]{:S(2)}) collective-permute-start(bf16[4,128,128]{2,1,0:T(8,128)(2,1)S(1)} %get-tuple-element.26), channel_id=1, source_target_pairs={{4,0},{8,4},{12,8},{16,12},{20,16},{24,20},{28,24},{5,1},{9,5},{13... | collective-permute-start | bytes 393224 | tf_op jit(solution)/shard_map/ppermute | solution.py:30

commit v5 on v4

--- a/solution.py
+++ b/solution.py
@@ -441,24 +441,30 @@
         out_ref[0, 0, :, slot * coarse : (slot + 1) * coarse] = sums_ref[half + 1, i, slot].astype(BF16)
 
 
-def last_kernel(zagg_ref, sums_ref, early_ref, late_ref, old_ref, out_ref):
-    halves, coarse = sums_ref.shape[0] - 1, sums_ref.shape[-1]
+def last_kernel(zagg_ref, sums_ref, early_ref, late_ref, old_ref, out_ref, rows_ref, sems):
+    halves, intervals, slots, coarse, _ = sums_ref.shape
+    halves = halves - 1
     dom = lax.axis_index("dom")
     end = (dom + 1) * (zagg_ref.shape[0] // lax.axis_size("dom"))
     following = jnp.where(end < zagg_ref.shape[0], end, end - 1)
     self_factor = jnp.where(zagg_ref[following] == zagg_ref[end - 1], 1.0, 0.0)
-    i = pl.program_id(0)
-    late = late_ref[i].astype(F32)
-    more = {
-        0: self_factor * late,
-        1: early_ref[0, i].astype(F32),
-        2: early_ref[1, i].astype(F32),
-        4: early_ref[2, i].astype(F32) + (1.0 - self_factor) * late,
-    }
-    for slot in range(sums_ref.shape[2]):
-        value = sums_ref[halves, i, slot]
-        value = value + more[slot] if slot in more else value
-        out_ref[0, 0, :, slot * coarse : (slot + 1) * coarse] = value.astype(BF16)
+    copies = []
+    for i in range(intervals):
+        late = late_ref[i].astype(F32)
+        more = {
+            0: self_factor * late,
+            1: early_ref[0, i].astype(F32),
+            2: early_ref[1, i].astype(F32),
+            4: early_ref[2, i].astype(F32) + (1.0 - self_factor) * late,
+        }
+        for slot in range(slots):
+            value = sums_ref[halves, i, slot]
+            value = value + more[slot] if slot in more else value
+            rows_ref[i, :, slot * coarse : (slot + 1) * coarse] = value.astype(BF16)
+        copies.append(pltpu.make_async_copy(rows_ref.at[i], out_ref.at[halves - 1, i], sems.at[i]))
+        copies[-1].start()
+    for copy in copies:
+        copy.wait()
 
 
 def owned(halves, sums):
@@ -474,14 +480,17 @@
     )(sums)
 
 
-def last(halves, zagg, sums, early, late, out):
+def last(zagg, sums, early, late, out):
     _, intervals, slots, coarse, _ = sums.shape
     return pl.pallas_call(
         last_kernel,
-        grid=(intervals,),
-        in_specs=[scalars(), in_vmem(), in_vmem(), in_vmem(), pl.BlockSpec(memory_space=pl.ANY)],
-        out_specs=pl.BlockSpec((1, 1, coarse, slots * coarse), lambda i: (halves - 1, i, 0, 0)),
+        in_specs=[scalars(), in_vmem(), in_vmem(), in_vmem(), pl.BlockSpec(memory_space=pltpu.HBM)],
+        out_specs=pl.BlockSpec(memory_space=pltpu.HBM),
         out_shape=out,
+        scratch_shapes=[
+            pltpu.VMEM((intervals, coarse, slots * coarse), BF16),
+            pltpu.SemaphoreType.DMA((intervals,)),
+        ],
         input_output_aliases={4: 0},
         compiler_params=pltpu.CompilerParams(vmem_limit_bytes=LIMIT),
         name="finish",
@@ -503,7 +512,7 @@
     early = shifted(early, "dom", -1)
     sums, late = upper_sums(zagg, xlen, theirs, pairs, prolong, lower, sums)
     late = shifted(late, "dom", -1)
-    return last(halves, zagg, sums, early, late, owned(halves, sums))
+    return last(zagg, sums, early, late, owned(halves, sums))
 
 
 def solution(mesh):

time: 71 us -> 70.4 us (level)
  no operation moved by 1% of the time
where the time goes in v5:
time: 70.4 us; the launch traced here: 70 us
  Pallas kernels  40.3 us (57%)
  starting transfers between devices  15.2 us (22%)
  waiting for transfers between devices  14.4 us (20%)
    pallas_call x1, Pallas kernels, main(): pl.pallas_call(functools.partial(main_kernel, halves), grid=(layers,), in...  26.6 us
    ppermute x6, starting transfers between devices, shifted(): return lax.ppermute(block, axis, route)  15.2 us
    ppermute x6, waiting for transfers between devices, shifted(): return lax.ppermute(block, axis, route)  14.4 us
    pallas_call x1, Pallas kernels, pack(): pl.pallas_call(pack_kernel, grid=(1,), in_specs=[vmem_block((1, depth, co...  2.52 us
    pallas_call x1, Pallas kernels, lower_sums(): pl.pallas_call(lower_kernel, in_specs=[scalars()] + [in_vmem()] * 3, out_...  2.31 us
    pallas_call x1, Pallas kernels, edges(): pl.pallas_call(functools.partial(edge_kernel, halves), in_specs=[scalars(...  2.3 us
    pallas_call x1, Pallas kernels, upper_sums(): pl.pallas_call(upper_kernel, in_specs=[scalars(), scalars()] + [in_vmem()...  2.17 us
    pallas_call x1, Pallas kernels, top(): pl.pallas_call(top_kernel, in_specs=[pl.BlockSpec(memory_space=pltpu.HBM)...  1.5 us
  transfers between devices with their start and end apart: 6, of which 2 were waited for; matrix products, arithmetic and copies ran while one was open for 0% of the time, Pallas kernels for 53%

profile of v5, /device:TPU:14, one launch (start us, length us, event | category | flops | bytes accessed | tf_op | source)
XLA Modules:
  0.0 70.0 jit_solution(17443787717964763989)
XLA Ops:
  0.0 1.5 %top.1.after_ref = bf16[7,12,64,128]{3,2,1,0:T(8,128)(2,1)S(1)} custom-call(bf16[4,7,12,64,128]{4,3,2,1,0:T(8,128)(2,1)} %own_ref.3), custom_call_target="tpu_custom_call" | custom-call | tf_op jit(solution)/shard_map/top/pallas_call | solution.py:78
  1.5 0.0 slice-start.1
  1.5 0.0 copy-start
  1.5 0.0 copy-start.1
  1.5 3.6 %collective-permute-start = (bf16[7,12,64,128]{3,2,1,0:T(8,128)(2,1)S(1)}, bf16[7,12,64,128]{3,2,1,0:T(8,128)(2,1)S(1)}, u32[]{:S(2)}, u32[]{:S(2)}) collective-permute-start(bf16[7,12,64,128]{3,2,1,0:T(8,128)(2,1)S(1)} %top.1.after_ref), channel_id=1, source_target_pairs={{0,4},{4,8},{8,12},{12,16},{16,20},{20,24},{24,28},{1,5},{5,9},{9,... | collective-permute-start | bytes 4128776 | tf_op jit(solution)/shard_map/ppermute | solution.py:30
  5.1 2.5 %pack.1 = (bf16[7,6,64,128]{3,2,1,0:T(8,128)(2,1)S(1)}, bf16[4,7,64,128]{3,2,1,0:T(8,128)(2,1)S(1)}, bf16[4,7,64,128]{3,2,1,0:T(8,128)(2,1)S(1)}) custom-call(bf16[4,7,12,64,448]{4,3,2,1,0:T(8,128)(2,1)} %a_ref.3, bf16[4,7,12,64,128]{4,3,2,1,0:T(8,128)(2,1)} %own_ref.3, bf16[7,12,64,128]{3,2,1,0:T(8,128)(2,1)S(1)} %top.1.after_ref), custom_call_target="tpu_custom_call" | custom-call | tf_op jit(solution)/shard_map/pack/pallas_call | solution.py:114
  7.6 1.9 %collective-permute-start.3 = (bf16[4,7,64,128]{3,2,1,0:T(8,128)(2,1)S(1)}, bf16[4,7,64,128]{3,2,1,0:T(8,128)(2,1)S(1)}, u32[]{:S(2)}, u32[]{:S(2)}) collective-permute-start(bf16[4,7,64,128]{3,2,1,0:T(8,128)(2,1)S(1)} %get-tuple-element.20.low_edge_ref), channel_id=1, source_target_pairs={{1,0},{2,1},{3,2},{5,4},{6,5},{7,6},{9,8},{10,9},{11,10},{13,12},{... | collective-permute-start | bytes 1376264 | tf_op jit(solution)/shard_map/ppermute | solution.py:30
  9.6 2.4 %collective-permute-start.2 = (bf16[4,7,64,128]{3,2,1,0:T(8,128)(2,1)S(1)}, bf16[4,7,64,128]{3,2,1,0:T(8,128)(2,1)S(1)}, u32[]{:S(2)}, u32[]{:S(2)}) collective-permute-start(bf16[4,7,64,128]{3,2,1,0:T(8,128)(2,1)S(1)} %get-tuple-element.21.high_edge_ref), channel_id=1, source_target_pairs={{0,1},{1,2},{2,3},{4,5},{5,6},{6,7},{8,9},{9,10},{10,11},{12,13},{... | collective-permute-start | bytes 1376264 | tf_op jit(solution)/shard_map/ppermute | solution.py:30
  12.0 3.4 %collective-permute-start.1 = (bf16[7,6,64,128]{3,2,1,0:T(8,128)(2,1)S(1)}, bf16[7,6,64,128]{3,2,1,0:T(8,128)(2,1)S(1)}, u32[]{:S(2)}, u32[]{:S(2)}) collective-permute-start(bf16[7,6,64,128]{3,2,1,0:T(8,128)(2,1)S(1)} %get-tuple-element.16), channel_id=1, source_target_pairs={{0,4},{4,8},{8,12},{12,16},{16,20},{20,24},{24,28},{1,5},{5,9},{9,... | collective-permute-start | bytes 2064392 | tf_op jit(solution)/shard_map/ppermute | solution.py:30
  15.4 0.0 slice-done
  15.5 26.6 %coarsen.1 = (f32[3,4,5,128,128]{4,3,2,1,0:T(8,128)S(1)}, bf16[7,12,64,128]{3,2,1,0:T(8,128)(2,1)S(1)}, bf16[4,7,64,128]{3,2,1,0:T(8,128)(2,1)S(1)}, bf16[4,7,64,128]{3,2,1,0:T(8,128)(2,1)S(1)}) custom-call(s32[32]{0:T(128)S(1)} %copy-done.1, s32[4,4]{1,0:T(4,128)S(1)} %copy-done, bf16[4,7,12,64,448]{4,3,2,1,0:T(8,128)(2,1)} %a_ref.3, ...), custom_call_target="tpu_custom_call" | custom-call | flops 16911433728 | bytes 41943040 | tf_op jit(solution)/shard_map/coarsen/pallas_call | solution.py:277
  42.1 0.0 collective-permute-done.3.right_ref
  42.1 0.0 collective-permute-done.2.left_ref
  42.1 2.3 %edges.1 = (f32[3,4,5,128,128]{4,3,2,1,0:T(8,128)S(1)}, bf16[3,4,128,128]{3,2,1,0:T(8,128)(2,1)S(1)}) custom-call(s32[32]{0:T(128)S(1)} %copy-done.1, bf16[4,7,64,128]{3,2,1,0:T(8,128)(2,1)S(1)} %get-tuple-element.18.first_ref, bf16[4,7,64,128]{3,2,1,0:T(8,128)(2,1)S(1)} %get-tuple-element.19.last_ref, ...), custom_call_target="tpu_custom_call", output_to_operand_aliasing={{0}: (7, {})} | custom-call | tf_op jit(solution)/shard_map/edges/pallas_call | solution.py:333
  44.4 1.9 %collective-permute-start.4 = (bf16[3,4,128,128]{3,2,1,0:T(8,128)(2,1)S(1)}, bf16[3,4,128,128]{3,2,1,0:T(8,128)(2,1)S(1)}, u32[]{:S(2)}, u32[]{:S(2)}) collective-permute-start(bf16[3,4,128,128]{3,2,1,0:T(8,128)(2,1)S(1)} %get-tuple-element.25), channel_id=1, source_target_pairs={{4,0},{8,4},{12,8},{16,12},{20,16},{24,20},{28,24},{5,1},{9,5},{13... | collective-permute-start | bytes 1179656 | tf_op jit(solution)/shard_map/ppermute | solution.py:30
  46.4 0.0 collective-permute-done.theirs_ref
  46.4 2.3 %lower.1.lower_ref = f32[4,128,128]{2,1,0:T(8,128)S(1)} custom-call(s32[4,4]{1,0:T(4,128)S(1)} %copy-done, bf16[7,12,64,128]{3,2,1,0:T(8,128)(2,1)S(1)} %collective-permute-done.theirs_ref, bf16[7,12,64,128]{3,2,1,0:T(8,128)(2,1)S(1)} %get-tuple-element.17.a_ref, bf16[4,7,12,64,128]{4,3,2,1,0:T(8,128)(2,1)S(1)} %bitcast.1), custom_call_target="tpu_custom_call" | custom-call | tf_op jit(solution)/shard_map/lower/pallas_call | solution.py:376
  48.7 10.0 %collective-permute-done.1.pairs_ref = bf16[7,6,64,128]{3,2,1,0:T(8,128)(2,1)S(1)} collective-permute-done((bf16[7,6,64,128]{3,2,1,0:T(8,128)(2,1)S(1)}, bf16[7,6,64,128]{3,2,1,0:T(8,128)(2,1)S(1)}, u32[]{:S(2)}, u32[]{:S(2)}) %collective-permute-start.1) | collective-permute-done | bytes 688160 | tf_op jit(solution)/shard_map/ppermute | solution.py:30
  58.7 2.2 %upper.1 = (f32[3,4,5,128,128]{4,3,2,1,0:T(8,128)S(1)}, bf16[4,128,128]{2,1,0:T(8,128)(2,1)S(1)}) custom-call(s32[32]{0:T(128)S(1)} %copy-done.1, s32[4,4]{1,0:T(4,128)S(1)} %copy-done, bf16[7,12,64,128]{3,2,1,0:T(8,128)(2,1)S(1)} %collective-permute-done.theirs_ref, ...), custom_call_target="tpu_custom_call", output_to_operand_aliasing={{0}: (6, {})} | custom-call | tf_op jit(solution)/shard_map/upper/pallas_call | solution.py:425
  60.8 1.9 %collective-permute-start.5 = (bf16[4,128,128]{2,1,0:T(8,128)(2,1)S(1)}, bf16[4,128,128]{2,1,0:T(8,128)(2,1)S(1)}, u32[]{:S(2)}, u32[]{:S(2)}) collective-permute-start(bf16[4,128,128]{2,1,0:T(8,128)(2,1)S(1)} %get-tuple-element.26), channel_id=1, source_target_pairs={{4,0},{8,4},{12,8},{16,12},{20,16},{24,20},{28,24},{5,1},{9,5},{13... | collective-permute-start | bytes 393224 | tf_op jit(solution)/shard_map/ppermute | solution.py:30
  62.8 1.5 %owned.1.old_ref = bf16[2,4,128,640]{3,2,1,0:T(8,128)(2,1)} custom-call(f32[3,4,5,128,128]{4,3,2,1,0:T(8,128)S(1)} %get-tuple-element.24.sums_ref), custom_call_target="tpu_custom_call" | custom-call | tf_op jit(solution)/shard_map/owned/pallas_call | solution.py:472
  64.2 0.0 collective-permute-done.4.early_ref
  64.2 4.4 %collective-permute-done.5.late_ref = bf16[4,128,128]{2,1,0:T(8,128)(2,1)S(1)} collective-permute-done((bf16[4,128,128]{2,1,0:T(8,128)(2,1)S(1)}, bf16[4,128,128]{2,1,0:T(8,128)(2,1)S(1)}, u32[]{:S(2)}, u32[]{:S(2)}) %collective-permute-start.5) | collective-permute-done | bytes 131104 | tf_op jit(solution)/shard_map/ppermute | solution.py:30
  68.6 1.4 %finish.1 = bf16[2,4,128,640]{3,2,1,0:T(8,128)(2,1)} custom-call(s32[32]{0:T(128)S(1)} %copy-done.1, f32[3,4,5,128,128]{4,3,2,1,0:T(8,128)S(1)} %get-tuple-element.24.sums_ref, bf16[3,4,128,128]{3,2,1,0:T(8,128)(2,1)S(1)} %collective-permute-done.4.early_ref, ...), custom_call_target="tpu_custom_call", output_to_operand_aliasing={{}: (4, {})} | custom-call | tf_op jit(solution)/shard_map/finish/pallas_call | solution.py:485
  (5 shorter events, 0.0 us)
Async XLA Ops:
  0.0 15.4 %slice-start = ((s8[5505024]{0:T(1024)(128)(4,1)}), s8[4194304]{0:T(1024)(128)(4,1)S(1)}, s32[]{:S(2)}) async-start(s8[5505024]{0:T(1024)(128)(4,1)} %bitcast), calls=%async_computation | async-start | bytes 8388608
  1.5 13.9 %slice-start.1 = ((s8[5505024]{0:T(1024)(128)(4,1)}), s8[1310720]{0:T(1024)(128)(4,1)S(1)}, s32[]{:S(2)}) async-start(s8[5505024]{0:T(1024)(128)(4,1)} %bitcast), calls=%async_computation.1 | async-start | bytes 2621440
  1.5 13.9 %copy-start = (s32[4,4]{1,0:T(4,128)S(1)}, s32[4,4]{1,0:T(4,128)}, u32[]{:S(2)}) copy-start(s32[4,4]{1,0:T(4,128)} %xlen_ref.5) | copy-start | bytes 196
  1.5 13.9 %copy-start.1 = (s32[32]{0:T(128)S(1)}, s32[32]{0:T(128)}, u32[]{:S(2)}) copy-start(s32[32]{0:T(128)} %zagg_ref.7) | copy-start | bytes 388
  1.5 44.8 %collective-permute-start = (bf16[7,12,64,128]{3,2,1,0:T(8,128)(2,1)S(1)}, bf16[7,12,64,128]{3,2,1,0:T(8,128)(2,1)S(1)}, u32[]{:S(2)}, u32[]{:S(2)}) collective-permute-start(bf16[7,12,64,128]{3,2,1,0:T(8,128)(2,1)S(1)} %top.1.after_ref), channel_id=1, source_target_pairs={{0,4},{4,8},{8,12},{12,16},{16,20},{20,24},{24,28},{1,5},{5,9},{9,... | collective-permute-start | bytes 4128776 | tf_op jit(solution)/shard_map/ppermute | solution.py:30
  7.6 34.5 %collective-permute-start.3 = (bf16[4,7,64,128]{3,2,1,0:T(8,128)(2,1)S(1)}, bf16[4,7,64,128]{3,2,1,0:T(8,128)(2,1)S(1)}, u32[]{:S(2)}, u32[]{:S(2)}) collective-permute-start(bf16[4,7,64,128]{3,2,1,0:T(8,128)(2,1)S(1)} %get-tuple-element.20.low_edge_ref), channel_id=1, source_target_pairs={{1,0},{2,1},{3,2},{5,4},{6,5},{7,6},{9,8},{10,9},{11,10},{13,12},{... | collective-permute-start | bytes 1376264 | tf_op jit(solution)/shard_map/ppermute | solution.py:30
  9.6 32.5 %collective-permute-start.2 = (bf16[4,7,64,128]{3,2,1,0:T(8,128)(2,1)S(1)}, bf16[4,7,64,128]{3,2,1,0:T(8,128)(2,1)S(1)}, u32[]{:S(2)}, u32[]{:S(2)}) collective-permute-start(bf16[4,7,64,128]{3,2,1,0:T(8,128)(2,1)S(1)} %get-tuple-element.21.high_edge_ref), channel_id=1, source_target_pairs={{0,1},{1,2},{2,3},{4,5},{5,6},{6,7},{8,9},{9,10},{10,11},{12,13},{... | collective-permute-start | bytes 1376264 | tf_op jit(solution)/shard_map/ppermute | solution.py:30
  12.0 46.7 %collective-permute-start.1 = (bf16[7,6,64,128]{3,2,1,0:T(8,128)(2,1)S(1)}, bf16[7,6,64,128]{3,2,1,0:T(8,128)(2,1)S(1)}, u32[]{:S(2)}, u32[]{:S(2)}) collective-permute-start(bf16[7,6,64,128]{3,2,1,0:T(8,128)(2,1)S(1)} %get-tuple-element.16), channel_id=1, source_target_pairs={{0,4},{4,8},{8,12},{12,16},{16,20},{20,24},{24,28},{1,5},{5,9},{9,... | collective-permute-start | bytes 2064392 | tf_op jit(solution)/shard_map/ppermute | solution.py:30
  44.4 19.8 %collective-permute-start.4 = (bf16[3,4,128,128]{3,2,1,0:T(8,128)(2,1)S(1)}, bf16[3,4,128,128]{3,2,1,0:T(8,128)(2,1)S(1)}, u32[]{:S(2)}, u32[]{:S(2)}) collective-permute-start(bf16[3,4,128,128]{3,2,1,0:T(8,128)(2,1)S(1)} %get-tuple-element.25), channel_id=1, source_target_pairs={{4,0},{8,4},{12,8},{16,12},{20,16},{24,20},{28,24},{5,1},{9,5},{13... | collective-permute-start | bytes 1179656 | tf_op jit(solution)/shard_map/ppermute | solution.py:30
  60.8 7.8 %collective-permute-start.5 = (bf16[4,128,128]{2,1,0:T(8,128)(2,1)S(1)}, bf16[4,128,128]{2,1,0:T(8,128)(2,1)S(1)}, u32[]{:S(2)}, u32[]{:S(2)}) collective-permute-start(bf16[4,128,128]{2,1,0:T(8,128)(2,1)S(1)} %get-tuple-element.26), channel_id=1, source_target_pairs={{4,0},{8,4},{12,8},{16,12},{20,16},{24,20},{28,24},{5,1},{9,5},{13... | collective-permute-start | bytes 393224 | tf_op jit(solution)/shard_map/ppermute | solution.py:30

commit v6 on v5

--- a/solution.py
+++ b/solution.py
@@ -48,6 +48,10 @@
 
 def aligned(low, high, end):
     return low // LANES * LANES, min(-(-high // LANES) * LANES, end)
+
+
+def group_of(columns):
+    return 2 if columns % 4 == 0 else 1
 
 
 def factor(flag, shape):
@@ -86,7 +90,7 @@
     )(prolong)
 
 
-def pack_kernel(a_ref, p_ref, after_ref, pairs_ref, left_ref, right_ref, sems):
+def pack_kernel(a_ref, p_ref, after_ref, most_ref, rest_ref, left_ref, right_ref, sems):
     _, depth, block, _ = left_ref.shape
     copies = [
         pltpu.make_async_copy(p_ref.at[:, :, 0], left_ref, sems.at[0]),
@@ -95,13 +99,16 @@
     for copy in copies:
         copy.start()
 
-    def body(i, _):
-        for y in range(depth):
-            pair = [a_ref[0, y, 2 * i + j, :, :block] for j in range(2)]
-            pairs_ref[y, i] = jnp.concatenate(pair, axis=-1)
-        return 0
-
-    lax.fori_loop(0, pairs_ref.shape[1], body, 0)
+    most = most_ref.shape[1]
+    for first, out_ref in ((0, most_ref), (most, rest_ref)):
+
+        def body(i, _, first=first, out_ref=out_ref):
+            for y in range(depth):
+                pair = [a_ref[0, y, 2 * (first + i) + j, :, :block] for j in range(2)]
+                out_ref[y, i] = jnp.concatenate(pair, axis=-1)
+            return 0
+
+        lax.fori_loop(0, out_ref.shape[1], body, 0)
     for copy in copies:
         copy.wait()
 
@@ -109,7 +116,10 @@
 def pack(a_blocks, prolong, after):
     layers, depth, columns, block, coarse = prolong.shape
     low, _ = aligned(6 * block, 7 * block, 7 * block)
-    pairs = jax.ShapeDtypeStruct((depth, columns // 2, block, 2 * block), BF16)
+    rest = group_of(columns)
+    pairs = [
+        jax.ShapeDtypeStruct((depth, count, block, 2 * block), BF16) for count in (columns // 2 - rest, rest)
+    ]
     edge = jax.ShapeDtypeStruct((layers, depth, block, coarse), BF16)
     return pl.pallas_call(
         pack_kernel,
@@ -119,8 +129,8 @@
             pl.BlockSpec(memory_space=pltpu.HBM),
             pl.BlockSpec(memory_space=pl.ANY),
         ],
-        out_specs=[in_vmem()] * 3,
-        out_shape=[pairs, edge, edge],
+        out_specs=[in_vmem()] * 4,
+        out_shape=pairs + [edge, edge],
         scratch_shapes=[pltpu.SemaphoreType.DMA((2,))],
         compiler_params=pltpu.CompilerParams(vmem_limit_bytes=LIMIT),
         name="pack",
@@ -347,7 +357,7 @@
     lower_ref[...] = jnp.zeros_like(lower_ref)
     low, high = aligned(5 * block, 6 * block, 7 * block)
 
-    group = 2 if columns % 4 == 0 else 1
+    group = group_of(columns)
 
     def body(step, _):
         rows = []
@@ -383,30 +393,32 @@
     )(xlen, theirs, bottom, prolong)
 
 
-def upper_kernel(zagg_ref, xlen_ref, theirs_ref, pairs_ref, own_ref, lower_ref, old_ref, sums_ref, late_ref, upper_ref):
+def upper_kernel(zagg_ref, xlen_ref, theirs_ref, most_ref, rest_ref, own_ref, lower_ref, old_ref, sums_ref, late_ref, upper_ref):
     depth, columns, block, coarse = theirs_ref.shape
     dom, grp = lax.axis_index("dom"), lax.axis_index("grp")
     upper_ref[...] = jnp.zeros_like(upper_ref)
-    group = 2 if columns % 4 == 0 else 1
-
-    def body(step, _):
+    group = group_of(columns)
+
+    def body(step, pairs_ref, start):
         rows = []
         for n in range(group):
             q = group * step + n
             halves = [[], []]
             for y in range(depth):
-                mine = [own_ref[0, y, 2 * q + j] for j in range(2)]
+                mine = [own_ref[0, y, 2 * (start + q) + j] for j in range(2)]
                 both = matmul(pairs_ref[y, q], diagonal(mine, 0, 0, 2 * block))
                 for j in range(2):
                     halves[j].append(both[:, j * coarse : (j + 1) * coarse].astype(BF16))
             rows.extend(jnp.concatenate(half, axis=0) for half in halves)
         for n, right in enumerate(rows):
-            x = 2 * group * step + n
+            x = 2 * (start + group * step) + n
             theirs = theirs_ref[:, x].reshape(depth * block, coarse)
             upper_ref[interval_of(xlen_ref, grp, x)] += transposed_matmul(theirs, right)
         return 0
 
-    lax.fori_loop(0, columns // (2 * group), body, 0)
+    most = most_ref.shape[1]
+    lax.fori_loop(0, most // group, lambda step, _: body(step, most_ref, 0), 0)
+    lax.fori_loop(0, rest_ref.shape[1] // group, lambda step, _: body(step, rest_ref, most), 0)
     layers = zagg_ref.shape[0] // lax.axis_size("dom")
     at = dom * layers
     same = (at > 0) & (zagg_ref[jnp.where(at > 0, at - 1, 0)] == zagg_ref[at])
@@ -420,18 +432,18 @@
     lax.fori_loop(0, late_ref.shape[0], emit, 0)
 
 
-def upper_sums(zagg, xlen, theirs, pairs, own, lower, sums):
+def upper_sums(zagg, xlen, theirs, most, rest, own, lower, sums):
     late = jax.ShapeDtypeStruct(lower.shape, BF16)
     return pl.pallas_call(
         upper_kernel,
-        in_specs=[scalars(), scalars()] + [in_vmem()] * 5,
+        in_specs=[scalars(), scalars()] + [in_vmem()] * 6,
         out_specs=[in_vmem()] * 2,
         out_shape=[sums, late],
         scratch_shapes=[pltpu.VMEM(late.shape, F32)],
-        input_output_aliases={6: 0},
+        input_output_aliases={7: 0},
         compiler_params=pltpu.CompilerParams(vmem_limit_bytes=LIMIT),
         name="upper",
-    )(zagg, xlen, theirs, pairs, own, lower, sums)
+    )(zagg, xlen, theirs, most, rest, own, lower, sums)
 
 
 def owned_kernel(sums_ref, out_ref):
@@ -502,15 +514,16 @@
     outside = pltpu.with_memory_space_constraint(prolong, pltpu.HBM)
     rows = top(outside)
     theirs = shifted(rows, "dom", 1)
-    pairs, low_edge, high_edge = pack(a_blocks, outside, rows)
-    pairs = shifted(pairs, "dom", 1)
+    most, rest, low_edge, high_edge = pack(a_blocks, outside, rows)
+    most = shifted(most, "dom", 1)
+    rest = shifted(rest, "dom", 1)
     left = shifted(high_edge, "grp", 1)
     right = shifted(low_edge, "grp", -1)
     sums, bottom, *pieces = main(halves, zagg, xlen, a_blocks, prolong)
     sums, early = edges(halves, zagg, pieces, low_edge, high_edge, left, right, sums)
     lower = lower_sums(xlen, theirs, bottom, prolong)
     early = shifted(early, "dom", -1)
-    sums, late = upper_sums(zagg, xlen, theirs, pairs, prolong, lower, sums)
+    sums, late = upper_sums(zagg, xlen, theirs, most, rest, prolong, lower, sums)
     late = shifted(late, "dom", -1)
     return last(zagg, sums, early, late, owned(halves, sums))
 

time: 70.4 us -> 76.4 us (1.085)
  the two profiles are of different devices: /device:TPU:14 before, /device:TPU:20 now
where the time goes in v6:
time: 76.4 us; the launch traced here: 76.1 us
  Pallas kernels  40.3 us (53%)
  starting transfers between devices  20 us (26%)
  waiting for transfers between devices  15.5 us (20%)
    pallas_call x1, Pallas kernels, main(): pl.pallas_call(functools.partial(main_kernel, halves), grid=(layers,), in...  26.6 us
    ppermute x7, starting transfers between devices, shifted(): return lax.ppermute(block, axis, route)  20 us
    ppermute x7, waiting for transfers between devices, shifted(): return lax.ppermute(block, axis, route)  15.5 us
    pallas_call x1, Pallas kernels, pack(): pl.pallas_call(pack_kernel, grid=(1,), in_specs=[vmem_block((1, depth, co...  2.52 us
    pallas_call x1, Pallas kernels, lower_sums(): pl.pallas_call(lower_kernel, in_specs=[scalars()] + [in_vmem()] * 3, out_...  2.32 us
    pallas_call x1, Pallas kernels, edges(): pl.pallas_call(functools.partial(edge_kernel, halves), in_specs=[scalars(...  2.3 us
    pallas_call x1, Pallas kernels, upper_sums(): pl.pallas_call(upper_kernel, in_specs=[scalars(), scalars()] + [in_vmem()...  2.18 us
  transfers between devices with their start and end apart: 7, of which 2 were waited for; matrix products, arithmetic and copies ran while one was open for 0% of the time, Pallas kernels for 49%

profile of v6, /device:TPU:20, one launch (start us, length us, event | category | flops | bytes accessed | tf_op | source)
XLA Modules:
  0.0 76.1 jit_solution(13502358848317596980)
XLA Ops:
  0.0 1.5 %top.1.after_ref = bf16[7,12,64,128]{3,2,1,0:T(8,128)(2,1)S(1)} custom-call(bf16[4,7,12,64,128]{4,3,2,1,0:T(8,128)(2,1)} %own_ref.3), custom_call_target="tpu_custom_call" | custom-call | tf_op jit(solution)/shard_map/top/pallas_call | solution.py:82
  1.5 0.0 slice-start.1
  1.5 0.0 copy-start
  1.5 0.0 copy-start.1
  1.5 3.6 %collective-permute-start = (bf16[7,12,64,128]{3,2,1,0:T(8,128)(2,1)S(1)}, bf16[7,12,64,128]{3,2,1,0:T(8,128)(2,1)S(1)}, u32[]{:S(2)}, u32[]{:S(2)}) collective-permute-start(bf16[7,12,64,128]{3,2,1,0:T(8,128)(2,1)S(1)} %top.1.after_ref), channel_id=1, source_target_pairs={{0,4},{4,8},{8,12},{12,16},{16,20},{20,24},{24,28},{1,5},{5,9},{9,... | collective-permute-start | bytes 4128776 | tf_op jit(solution)/shard_map/ppermute | solution.py:30
  5.1 2.5 %pack.1 = (bf16[7,4,64,128]{3,2,1,0:T(8,128)(2,1)S(1)}, bf16[7,2,64,128]{3,2,1,0:T(8,128)(2,1)S(1)}, bf16[4,7,64,128]{3,2,1,0:T(8,128)(2,1)S(1)}, bf16[4,7,64,128]{3,2,1,0:T(8,128)(2,1)S(1)}) custom-call(bf16[4,7,12,64,448]{4,3,2,1,0:T(8,128)(2,1)} %a_ref.3, bf16[4,7,12,64,128]{4,3,2,1,0:T(8,128)(2,1)} %own_ref.3, bf16[7,12,64,128]{3,2,1,0:T(8,128)(2,1)S(1)} %top.1.after_ref), custom_call_target="tpu_custom_call" | custom-call | tf_op jit(solution)/shard_map/pack/pallas_call | solution.py:124
  7.6 3.4 %collective-permute-start.1 = (bf16[7,4,64,128]{3,2,1,0:T(8,128)(2,1)S(1)}, bf16[7,4,64,128]{3,2,1,0:T(8,128)(2,1)S(1)}, u32[]{:S(2)}, u32[]{:S(2)}) collective-permute-start(bf16[7,4,64,128]{3,2,1,0:T(8,128)(2,1)S(1)} %get-tuple-element.17), channel_id=1, source_target_pairs={{0,4},{4,8},{8,12},{12,16},{16,20},{20,24},{24,28},{1,5},{5,9},{9,... | collective-permute-start | bytes 1376264 | tf_op jit(solution)/shard_map/ppermute | solution.py:30
  11.1 1.3 %collective-permute-start.4 = (bf16[4,7,64,128]{3,2,1,0:T(8,128)(2,1)S(1)}, bf16[4,7,64,128]{3,2,1,0:T(8,128)(2,1)S(1)}, u32[]{:S(2)}, u32[]{:S(2)}) collective-permute-start(bf16[4,7,64,128]{3,2,1,0:T(8,128)(2,1)S(1)} %get-tuple-element.22.low_edge_ref), channel_id=1, source_target_pairs={{1,0},{2,1},{3,2},{5,4},{6,5},{7,6},{9,8},{10,9},{11,10},{13,12},{... | collective-permute-start | bytes 1376264 | tf_op jit(solution)/shard_map/ppermute | solution.py:30
  12.4 3.1 %collective-permute-start.3 = (bf16[4,7,64,128]{3,2,1,0:T(8,128)(2,1)S(1)}, bf16[4,7,64,128]{3,2,1,0:T(8,128)(2,1)S(1)}, u32[]{:S(2)}, u32[]{:S(2)}) collective-permute-start(bf16[4,7,64,128]{3,2,1,0:T(8,128)(2,1)S(1)} %get-tuple-element.23.high_edge_ref), channel_id=1, source_target_pairs={{0,1},{1,2},{2,3},{4,5},{5,6},{6,7},{8,9},{9,10},{10,11},{12,13},{... | collective-permute-start | bytes 1376264 | tf_op jit(solution)/shard_map/ppermute | solution.py:30
  15.5 26.6 %coarsen.1 = (f32[3,4,5,128,128]{4,3,2,1,0:T(8,128)S(1)}, bf16[7,12,64,128]{3,2,1,0:T(8,128)(2,1)S(1)}, bf16[4,7,64,128]{3,2,1,0:T(8,128)(2,1)S(1)}, bf16[4,7,64,128]{3,2,1,0:T(8,128)(2,1)S(1)}) custom-call(s32[32]{0:T(128)S(1)} %copy-done.1, s32[4,4]{1,0:T(4,128)S(1)} %copy-done, bf16[4,7,12,64,448]{4,3,2,1,0:T(8,128)(2,1)} %a_ref.3, ...), custom_call_target="tpu_custom_call" | custom-call | flops 16911433728 | bytes 41943040 | tf_op jit(solution)/shard_map/coarsen/pallas_call | solution.py:287
  42.1 0.0 collective-permute-done.4.right_ref
  42.1 0.0 collective-permute-done.3.left_ref
  42.1 2.3 %edges.1 = (f32[3,4,5,128,128]{4,3,2,1,0:T(8,128)S(1)}, bf16[3,4,128,128]{3,2,1,0:T(8,128)(2,1)S(1)}) custom-call(s32[32]{0:T(128)S(1)} %copy-done.1, bf16[4,7,64,128]{3,2,1,0:T(8,128)(2,1)S(1)} %get-tuple-element.20.first_ref, bf16[4,7,64,128]{3,2,1,0:T(8,128)(2,1)S(1)} %get-tuple-element.21.last_ref, ...), custom_call_target="tpu_custom_call", output_to_operand_aliasing={{0}: (7, {})} | custom-call | tf_op jit(solution)/shard_map/edges/pallas_call | solution.py:343
  44.5 1.9 %collective-permute-start.5 = (bf16[3,4,128,128]{3,2,1,0:T(8,128)(2,1)S(1)}, bf16[3,4,128,128]{3,2,1,0:T(8,128)(2,1)S(1)}, u32[]{:S(2)}, u32[]{:S(2)}) collective-permute-start(bf16[3,4,128,128]{3,2,1,0:T(8,128)(2,1)S(1)} %get-tuple-element.27), channel_id=1, source_target_pairs={{4,0},{8,4},{12,8},{16,12},{20,16},{24,20},{28,24},{5,1},{9,5},{13... | collective-permute-start | bytes 1179656 | tf_op jit(solution)/shard_map/ppermute | solution.py:30
  46.4 4.8 %collective-permute-start.2 = (bf16[7,2,64,128]{3,2,1,0:T(8,128)(2,1)S(1)}, bf16[7,2,64,128]{3,2,1,0:T(8,128)(2,1)S(1)}, u32[]{:S(2)}, u32[]{:S(2)}) collective-permute-start(bf16[7,2,64,128]{3,2,1,0:T(8,128)(2,1)S(1)} %get-tuple-element.18), channel_id=1, source_target_pairs={{0,4},{4,8},{8,12},{12,16},{16,20},{20,24},{24,28},{1,5},{5,9},{9,... | collective-permute-start | bytes 688136 | tf_op jit(solution)/shard_map/ppermute | solution.py:30
  51.2 0.0 collective-permute-done.theirs_ref
  51.2 2.3 %lower.1.lower_ref = f32[4,128,128]{2,1,0:T(8,128)S(1)} custom-call(s32[4,4]{1,0:T(4,128)S(1)} %copy-done, bf16[7,12,64,128]{3,2,1,0:T(8,128)(2,1)S(1)} %collective-permute-done.theirs_ref, bf16[7,12,64,128]{3,2,1,0:T(8,128)(2,1)S(1)} %get-tuple-element.19.a_ref, bf16[4,7,12,64,128]{4,3,2,1,0:T(8,128)(2,1)S(1)} %bitcast.1), custom_call_target="tpu_custom_call" | custom-call | tf_op jit(solution)/shard_map/lower/pallas_call | solution.py:386
  53.5 10.6 %collective-permute-done.2.rest_ref = bf16[7,2,64,128]{3,2,1,0:T(8,128)(2,1)S(1)} collective-permute-done((bf16[7,2,64,128]{3,2,1,0:T(8,128)(2,1)S(1)}, bf16[7,2,64,128]{3,2,1,0:T(8,128)(2,1)S(1)}, u32[]{:S(2)}, u32[]{:S(2)}) %collective-permute-start.2) | collective-permute-done | bytes 229408 | tf_op jit(solution)/shard_map/ppermute | solution.py:30
  64.1 2.2 %upper.1 = (f32[3,4,5,128,128]{4,3,2,1,0:T(8,128)S(1)}, bf16[4,128,128]{2,1,0:T(8,128)(2,1)S(1)}) custom-call(s32[32]{0:T(128)S(1)} %copy-done.1, s32[4,4]{1,0:T(4,128)S(1)} %copy-done, bf16[7,12,64,128]{3,2,1,0:T(8,128)(2,1)S(1)} %collective-permute-done.theirs_ref, ...), custom_call_target="tpu_custom_call", output_to_operand_aliasing={{0}: (7, {})} | custom-call | tf_op jit(solution)/shard_map/upper/pallas_call | solution.py:437
  66.3 1.9 %collective-permute-start.6 = (bf16[4,128,128]{2,1,0:T(8,128)(2,1)S(1)}, bf16[4,128,128]{2,1,0:T(8,128)(2,1)S(1)}, u32[]{:S(2)}, u32[]{:S(2)}) collective-permute-start(bf16[4,128,128]{2,1,0:T(8,128)(2,1)S(1)} %get-tuple-element.28), channel_id=1, source_target_pairs={{4,0},{8,4},{12,8},{16,12},{20,16},{24,20},{28,24},{5,1},{9,5},{13... | collective-permute-start | bytes 393224 | tf_op jit(solution)/shard_map/ppermute | solution.py:30
  68.3 1.5 %owned.1.old_ref = bf16[2,4,128,640]{3,2,1,0:T(8,128)(2,1)} custom-call(f32[3,4,5,128,128]{4,3,2,1,0:T(8,128)S(1)} %get-tuple-element.26.sums_ref), custom_call_target="tpu_custom_call" | custom-call | tf_op jit(solution)/shard_map/owned/pallas_call | solution.py:484
  69.7 0.0 collective-permute-done.5.early_ref
  69.7 4.9 %collective-permute-done.6.late_ref = bf16[4,128,128]{2,1,0:T(8,128)(2,1)S(1)} collective-permute-done((bf16[4,128,128]{2,1,0:T(8,128)(2,1)S(1)}, bf16[4,128,128]{2,1,0:T(8,128)(2,1)S(1)}, u32[]{:S(2)}, u32[]{:S(2)}) %collective-permute-start.6) | collective-permute-done | bytes 131104 | tf_op jit(solution)/shard_map/ppermute | solution.py:30
  74.6 1.4 %finish.1 = bf16[2,4,128,640]{3,2,1,0:T(8,128)(2,1)} custom-call(s32[32]{0:T(128)S(1)} %copy-done.1, f32[3,4,5,128,128]{4,3,2,1,0:T(8,128)S(1)} %get-tuple-element.26.sums_ref, bf16[3,4,128,128]{3,2,1,0:T(8,128)(2,1)S(1)} %collective-permute-done.5.early_ref, ...), custom_call_target="tpu_custom_call", output_to_operand_aliasing={{}: (4, {})} | custom-call | tf_op jit(solution)/shard_map/finish/pallas_call | solution.py:497
  (7 shorter events, 0.0 us)
Async XLA Ops:
  0.0 15.4 %slice-start = ((s8[5505024]{0:T(1024)(128)(4,1)}), s8[4194304]{0:T(1024)(128)(4,1)S(1)}, s32[]{:S(2)}) async-start(s8[5505024]{0:T(1024)(128)(4,1)} %bitcast), calls=%async_computation | async-start | bytes 8388608
  1.5 13.9 %slice-start.1 = ((s8[5505024]{0:T(1024)(128)(4,1)}), s8[1310720]{0:T(1024)(128)(4,1)S(1)}, s32[]{:S(2)}) async-start(s8[5505024]{0:T(1024)(128)(4,1)} %bitcast), calls=%async_computation.1 | async-start | bytes 2621440
  1.5 13.9 %copy-start = (s32[4,4]{1,0:T(4,128)S(1)}, s32[4,4]{1,0:T(4,128)}, u32[]{:S(2)}) copy-start(s32[4,4]{1,0:T(4,128)} %xlen_ref.5) | copy-start | bytes 196
  1.5 13.9 %copy-start.1 = (s32[32]{0:T(128)S(1)}, s32[32]{0:T(128)}, u32[]{:S(2)}) copy-start(s32[32]{0:T(128)} %zagg_ref.7) | copy-start | bytes 388
  1.5 49.7 %collective-permute-start = (bf16[7,12,64,128]{3,2,1,0:T(8,128)(2,1)S(1)}, bf16[7,12,64,128]{3,2,1,0:T(8,128)(2,1)S(1)}, u32[]{:S(2)}, u32[]{:S(2)}) collective-permute-start(bf16[7,12,64,128]{3,2,1,0:T(8,128)(2,1)S(1)} %top.1.after_ref), channel_id=1, source_target_pairs={{0,4},{4,8},{8,12},{12,16},{16,20},{20,24},{24,28},{1,5},{5,9},{9,... | collective-permute-start | bytes 4128776 | tf_op jit(solution)/shard_map/ppermute | solution.py:30
  7.6 56.5 %collective-permute-start.1 = (bf16[7,4,64,128]{3,2,1,0:T(8,128)(2,1)S(1)}, bf16[7,4,64,128]{3,2,1,0:T(8,128)(2,1)S(1)}, u32[]{:S(2)}, u32[]{:S(2)}) collective-permute-start(bf16[7,4,64,128]{3,2,1,0:T(8,128)(2,1)S(1)} %get-tuple-element.17), channel_id=1, source_target_pairs={{0,4},{4,8},{8,12},{12,16},{16,20},{20,24},{24,28},{1,5},{5,9},{9,... | collective-permute-start | bytes 1376264 | tf_op jit(solution)/shard_map/ppermute | solution.py:30
  11.1 31.1 %collective-permute-start.4 = (bf16[4,7,64,128]{3,2,1,0:T(8,128)(2,1)S(1)}, bf16[4,7,64,128]{3,2,1,0:T(8,128)(2,1)S(1)}, u32[]{:S(2)}, u32[]{:S(2)}) collective-permute-start(bf16[4,7,64,128]{3,2,1,0:T(8,128)(2,1)S(1)} %get-tuple-element.22.low_edge_ref), channel_id=1, source_target_pairs={{1,0},{2,1},{3,2},{5,4},{6,5},{7,6},{9,8},{10,9},{11,10},{13,12},{... | collective-permute-start | bytes 1376264 | tf_op jit(solution)/shard_map/ppermute | solution.py:30
  12.4 29.8 %collective-permute-start.3 = (bf16[4,7,64,128]{3,2,1,0:T(8,128)(2,1)S(1)}, bf16[4,7,64,128]{3,2,1,0:T(8,128)(2,1)S(1)}, u32[]{:S(2)}, u32[]{:S(2)}) collective-permute-start(bf16[4,7,64,128]{3,2,1,0:T(8,128)(2,1)S(1)} %get-tuple-element.23.high_edge_ref), channel_id=1, source_target_pairs={{0,1},{1,2},{2,3},{4,5},{5,6},{6,7},{8,9},{9,10},{10,11},{12,13},{... | collective-permute-start | bytes 1376264 | tf_op jit(solution)/shard_map/ppermute | solution.py:30
  44.5 25.3 %collective-permute-start.5 = (bf16[3,4,128,128]{3,2,1,0:T(8,128)(2,1)S(1)}, bf16[3,4,128,128]{3,2,1,0:T(8,128)(2,1)S(1)}, u32[]{:S(2)}, u32[]{:S(2)}) collective-permute-start(bf16[3,4,128,128]{3,2,1,0:T(8,128)(2,1)S(1)} %get-tuple-element.27), channel_id=1, source_target_pairs={{4,0},{8,4},{12,8},{16,12},{20,16},{24,20},{28,24},{5,1},{9,5},{13... | collective-permute-start | bytes 1179656 | tf_op jit(solution)/shard_map/ppermute | solution.py:30
  46.4 17.8 %collective-permute-start.2 = (bf16[7,2,64,128]{3,2,1,0:T(8,128)(2,1)S(1)}, bf16[7,2,64,128]{3,2,1,0:T(8,128)(2,1)S(1)}, u32[]{:S(2)}, u32[]{:S(2)}) collective-permute-start(bf16[7,2,64,128]{3,2,1,0:T(8,128)(2,1)S(1)} %get-tuple-element.18), channel_id=1, source_target_pairs={{0,4},{4,8},{8,12},{12,16},{16,20},{20,24},{24,28},{1,5},{5,9},{9,... | collective-permute-start | bytes 688136 | tf_op jit(solution)/shard_map/ppermute | solution.py:30
  66.3 8.3 %collective-permute-start.6 = (bf16[4,128,128]{2,1,0:T(8,128)(2,1)S(1)}, bf16[4,128,128]{2,1,0:T(8,128)(2,1)S(1)}, u32[]{:S(2)}, u32[]{:S(2)}) collective-permute-start(bf16[4,128,128]{2,1,0:T(8,128)(2,1)S(1)} %get-tuple-element.28), channel_id=1, source_target_pairs={{4,0},{8,4},{12,8},{16,12},{20,16},{24,20},{28,24},{5,1},{9,5},{13... | collective-permute-start | bytes 393224 | tf_op jit(solution)/shard_map/ppermute | solution.py:30

commit v7 on v6

--- a/solution.py
+++ b/solution.py
@@ -116,9 +116,8 @@
 def pack(a_blocks, prolong, after):
     layers, depth, columns, block, coarse = prolong.shape
     low, _ = aligned(6 * block, 7 * block, 7 * block)
-    rest = group_of(columns)
     pairs = [
-        jax.ShapeDtypeStruct((depth, count, block, 2 * block), BF16) for count in (columns // 2 - rest, rest)
+        jax.ShapeDtypeStruct((depth, count, block, 2 * block), BF16) for count in (columns // 2 - 1, 1)
     ]
     edge = jax.ShapeDtypeStruct((layers, depth, block, coarse), BF16)
     return pl.pallas_call(
@@ -399,26 +398,29 @@
     upper_ref[...] = jnp.zeros_like(upper_ref)
     group = group_of(columns)
 
-    def body(step, pairs_ref, start):
+    def body(entries):
         rows = []
-        for n in range(group):
-            q = group * step + n
+        for pairs_ref, at, q in entries:
             halves = [[], []]
             for y in range(depth):
-                mine = [own_ref[0, y, 2 * (start + q) + j] for j in range(2)]
-                both = matmul(pairs_ref[y, q], diagonal(mine, 0, 0, 2 * block))
+                mine = [own_ref[0, y, 2 * q + j] for j in range(2)]
+                both = matmul(pairs_ref[y, at], diagonal(mine, 0, 0, 2 * block))
                 for j in range(2):
                     halves[j].append(both[:, j * coarse : (j + 1) * coarse].astype(BF16))
-            rows.extend(jnp.concatenate(half, axis=0) for half in halves)
-        for n, right in enumerate(rows):
-            x = 2 * (start + group * step) + n
+            rows.extend((2 * q + j, jnp.concatenate(half, axis=0)) for j, half in enumerate(halves))
+        for x, right in rows:
             theirs = theirs_ref[:, x].reshape(depth * block, coarse)
             upper_ref[interval_of(xlen_ref, grp, x)] += transposed_matmul(theirs, right)
         return 0
 
     most = most_ref.shape[1]
-    lax.fori_loop(0, most // group, lambda step, _: body(step, most_ref, 0), 0)
-    lax.fori_loop(0, rest_ref.shape[1] // group, lambda step, _: body(step, rest_ref, most), 0)
+    steps = (most + 1 - group) // group
+
+    def several(step, _):
+        return body([(most_ref, group * step + n, group * step + n) for n in range(group)])
+
+    lax.fori_loop(0, steps, several, 0)
+    body([(most_ref, q, q) for q in range(group * steps, most)] + [(rest_ref, 0, most)])
     layers = zagg_ref.shape[0] // lax.axis_size("dom")
     at = dom * layers
     same = (at > 0) & (zagg_ref[jnp.where(at > 0, at - 1, 0)] == zagg_ref[at])

time: 76.4 us -> 73.8 us (0.966)
  waiting for transfers between devices: 15.5 us -> 13 us
    ppermute x7, waiting for transfers between devices: 15.5 us -> 13 us  [shifted(): return lax.ppermute(block, axis, route)]
  transfers between devices with their start and end apart: 7 -> 7, of which waited for: 2 -> 2; matrix products, arithmetic and copies ran while one was open for 0% -> 0% of each run, Pallas kernels for 49% -> 51%
where the time goes in v7:
time: 73.8 us; the launch traced here: 73.5 us
  Pallas kernels  40.3 us (55%)
  starting transfers between devices  20 us (27%)
  waiting for transfers between devices  13 us (18%)
    pallas_call x1, Pallas kernels, main(): pl.pallas_call(functools.partial(main_kernel, halves), grid=(layers,), in...  26.6 us
    ppermute x7, starting transfers between devices, shifted(): return lax.ppermute(block, axis, route)  20 us
    ppermute x7, waiting for transfers between devices, shifted(): return lax.ppermute(block, axis, route)  13 us
    pallas_call x1, Pallas kernels, pack(): pl.pallas_call(pack_kernel, grid=(1,), in_specs=[vmem_block((1, depth, co...  2.52 us
    pallas_call x1, Pallas kernels, lower_sums(): pl.pallas_call(lower_kernel, in_specs=[scalars()] + [in_vmem()] * 3, out_...  2.31 us
    pallas_call x1, Pallas kernels, edges(): pl.pallas_call(functools.partial(edge_kernel, halves), in_specs=[scalars(...  2.3 us
    pallas_call x1, Pallas kernels, upper_sums(): pl.pallas_call(upper_kernel, in_specs=[scalars(), scalars()] + [in_vmem()...  2.18 us
    pallas_call x1, Pallas kernels, top(): pl.pallas_call(top_kernel, in_specs=[pl.BlockSpec(memory_space=pltpu.HBM)...  1.5 us
  transfers between devices with their start and end apart: 7, of which 2 were waited for; matrix products, arithmetic and copies ran while one was open for 0% of the time, Pallas kernels for 51%

profile of v7, /device:TPU:20, one launch (start us, length us, event | category | flops | bytes accessed | tf_op | source)
XLA Modules:
  0.0 73.5 jit_solution(15743498383719001655)
XLA Ops:
  0.0 1.5 %top.1.after_ref = bf16[7,12,64,128]{3,2,1,0:T(8,128)(2,1)S(1)} custom-call(bf16[4,7,12,64,128]{4,3,2,1,0:T(8,128)(2,1)} %own_ref.3), custom_call_target="tpu_custom_call" | custom-call | tf_op jit(solution)/shard_map/top/pallas_call | solution.py:82
  1.5 0.0 slice-start.1
  1.5 0.0 copy-start
  1.5 0.0 copy-start.1
  1.5 3.6 %collective-permute-start = (bf16[7,12,64,128]{3,2,1,0:T(8,128)(2,1)S(1)}, bf16[7,12,64,128]{3,2,1,0:T(8,128)(2,1)S(1)}, u32[]{:S(2)}, u32[]{:S(2)}) collective-permute-start(bf16[7,12,64,128]{3,2,1,0:T(8,128)(2,1)S(1)} %top.1.after_ref), channel_id=1, source_target_pairs={{0,4},{4,8},{8,12},{12,16},{16,20},{20,24},{24,28},{1,5},{5,9},{9,... | collective-permute-start | bytes 4128776 | tf_op jit(solution)/shard_map/ppermute | solution.py:30
  5.1 2.5 %pack.1 = (bf16[7,5,64,128]{3,2,1,0:T(8,128)(2,1)S(1)}, bf16[7,1,64,128]{3,2,1,0:T(8,128)(2,1)S(1)}, bf16[4,7,64,128]{3,2,1,0:T(8,128)(2,1)S(1)}, bf16[4,7,64,128]{3,2,1,0:T(8,128)(2,1)S(1)}) custom-call(bf16[4,7,12,64,448]{4,3,2,1,0:T(8,128)(2,1)} %a_ref.3, bf16[4,7,12,64,128]{4,3,2,1,0:T(8,128)(2,1)} %own_ref.3, bf16[7,12,64,128]{3,2,1,0:T(8,128)(2,1)S(1)} %top.1.after_ref), custom_call_target="tpu_custom_call" | custom-call | tf_op jit(solution)/shard_map/pack/pallas_call | solution.py:123
  7.6 1.3 %collective-permute-start.4 = (bf16[4,7,64,128]{3,2,1,0:T(8,128)(2,1)S(1)}, bf16[4,7,64,128]{3,2,1,0:T(8,128)(2,1)S(1)}, u32[]{:S(2)}, u32[]{:S(2)}) collective-permute-start(bf16[4,7,64,128]{3,2,1,0:T(8,128)(2,1)S(1)} %get-tuple-element.22.low_edge_ref), channel_id=1, source_target_pairs={{1,0},{2,1},{3,2},{5,4},{6,5},{7,6},{9,8},{10,9},{11,10},{13,12},{... | collective-permute-start | bytes 1376264 | tf_op jit(solution)/shard_map/ppermute | solution.py:30
  8.9 3.1 %collective-permute-start.3 = (bf16[4,7,64,128]{3,2,1,0:T(8,128)(2,1)S(1)}, bf16[4,7,64,128]{3,2,1,0:T(8,128)(2,1)S(1)}, u32[]{:S(2)}, u32[]{:S(2)}) collective-permute-start(bf16[4,7,64,128]{3,2,1,0:T(8,128)(2,1)S(1)} %get-tuple-element.23.high_edge_ref), channel_id=1, source_target_pairs={{0,1},{1,2},{2,3},{4,5},{5,6},{6,7},{8,9},{9,10},{10,11},{12,13},{... | collective-permute-start | bytes 1376264 | tf_op jit(solution)/shard_map/ppermute | solution.py:30
  12.0 3.4 %collective-permute-start.1 = (bf16[7,5,64,128]{3,2,1,0:T(8,128)(2,1)S(1)}, bf16[7,5,64,128]{3,2,1,0:T(8,128)(2,1)S(1)}, u32[]{:S(2)}, u32[]{:S(2)}) collective-permute-start(bf16[7,5,64,128]{3,2,1,0:T(8,128)(2,1)S(1)} %get-tuple-element.17), channel_id=1, source_target_pairs={{0,4},{4,8},{8,12},{12,16},{16,20},{20,24},{24,28},{1,5},{5,9},{9,... | collective-permute-start | bytes 1720328 | tf_op jit(solution)/shard_map/ppermute | solution.py:30
  15.5 26.6 %coarsen.1 = (f32[3,4,5,128,128]{4,3,2,1,0:T(8,128)S(1)}, bf16[7,12,64,128]{3,2,1,0:T(8,128)(2,1)S(1)}, bf16[4,7,64,128]{3,2,1,0:T(8,128)(2,1)S(1)}, bf16[4,7,64,128]{3,2,1,0:T(8,128)(2,1)S(1)}) custom-call(s32[32]{0:T(128)S(1)} %copy-done.1, s32[4,4]{1,0:T(4,128)S(1)} %copy-done, bf16[4,7,12,64,448]{4,3,2,1,0:T(8,128)(2,1)} %a_ref.3, ...), custom_call_target="tpu_custom_call" | custom-call | flops 16911433728 | bytes 41943040 | tf_op jit(solution)/shard_map/coarsen/pallas_call | solution.py:286
  42.1 0.0 collective-permute-done.4.right_ref
  42.1 0.0 collective-permute-done.3.left_ref
  42.1 2.3 %edges.1 = (f32[3,4,5,128,128]{4,3,2,1,0:T(8,128)S(1)}, bf16[3,4,128,128]{3,2,1,0:T(8,128)(2,1)S(1)}) custom-call(s32[32]{0:T(128)S(1)} %copy-done.1, bf16[4,7,64,128]{3,2,1,0:T(8,128)(2,1)S(1)} %get-tuple-element.20.first_ref, bf16[4,7,64,128]{3,2,1,0:T(8,128)(2,1)S(1)} %get-tuple-element.21.last_ref, ...), custom_call_target="tpu_custom_call", output_to_operand_aliasing={{0}: (7, {})} | custom-call | tf_op jit(solution)/shard_map/edges/pallas_call | solution.py:342
  44.5 1.9 %collective-permute-start.5 = (bf16[3,4,128,128]{3,2,1,0:T(8,128)(2,1)S(1)}, bf16[3,4,128,128]{3,2,1,0:T(8,128)(2,1)S(1)}, u32[]{:S(2)}, u32[]{:S(2)}) collective-permute-start(bf16[3,4,128,128]{3,2,1,0:T(8,128)(2,1)S(1)} %get-tuple-element.27), channel_id=1, source_target_pairs={{4,0},{8,4},{12,8},{16,12},{20,16},{24,20},{28,24},{5,1},{9,5},{13... | collective-permute-start | bytes 1179656 | tf_op jit(solution)/shard_map/ppermute | solution.py:30
  46.4 4.8 %collective-permute-start.2 = (bf16[7,1,64,128]{3,2,1,0:T(8,128)(2,1)S(1)}, bf16[7,1,64,128]{3,2,1,0:T(8,128)(2,1)S(1)}, u32[]{:S(2)}, u32[]{:S(2)}) collective-permute-start(bf16[7,1,64,128]{3,2,1,0:T(8,128)(2,1)S(1)} %get-tuple-element.18), channel_id=1, source_target_pairs={{0,4},{4,8},{8,12},{12,16},{16,20},{20,24},{24,28},{1,5},{5,9},{9,... | collective-permute-start | bytes 344072 | tf_op jit(solution)/shard_map/ppermute | solution.py:30
  51.2 0.0 collective-permute-done.theirs_ref
  51.2 2.3 %lower.1.lower_ref = f32[4,128,128]{2,1,0:T(8,128)S(1)} custom-call(s32[4,4]{1,0:T(4,128)S(1)} %copy-done, bf16[7,12,64,128]{3,2,1,0:T(8,128)(2,1)S(1)} %collective-permute-done.theirs_ref, bf16[7,12,64,128]{3,2,1,0:T(8,128)(2,1)S(1)} %get-tuple-element.19.a_ref, bf16[4,7,12,64,128]{4,3,2,1,0:T(8,128)(2,1)S(1)} %bitcast.1), custom_call_target="tpu_custom_call" | custom-call | tf_op jit(solution)/shard_map/lower/pallas_call | solution.py:385
  53.5 8.0 %collective-permute-done.2.rest_ref = bf16[7,1,64,128]{3,2,1,0:T(8,128)(2,1)S(1)} collective-permute-done((bf16[7,1,64,128]{3,2,1,0:T(8,128)(2,1)S(1)}, bf16[7,1,64,128]{3,2,1,0:T(8,128)(2,1)S(1)}, u32[]{:S(2)}, u32[]{:S(2)}) %collective-permute-start.2) | collective-permute-done | bytes 114720 | tf_op jit(solution)/shard_map/ppermute | solution.py:30
  61.6 0.0 collective-permute-done.1.most_ref
  61.6 2.2 %upper.1 = (f32[3,4,5,128,128]{4,3,2,1,0:T(8,128)S(1)}, bf16[4,128,128]{2,1,0:T(8,128)(2,1)S(1)}) custom-call(s32[32]{0:T(128)S(1)} %copy-done.1, s32[4,4]{1,0:T(4,128)S(1)} %copy-done, bf16[7,12,64,128]{3,2,1,0:T(8,128)(2,1)S(1)} %collective-permute-done.theirs_ref, ...), custom_call_target="tpu_custom_call", output_to_operand_aliasing={{0}: (7, {})} | custom-call | tf_op jit(solution)/shard_map/upper/pallas_call | solution.py:439
  63.8 1.9 %collective-permute-start.6 = (bf16[4,128,128]{2,1,0:T(8,128)(2,1)S(1)}, bf16[4,128,128]{2,1,0:T(8,128)(2,1)S(1)}, u32[]{:S(2)}, u32[]{:S(2)}) collective-permute-start(bf16[4,128,128]{2,1,0:T(8,128)(2,1)S(1)} %get-tuple-element.28), channel_id=1, source_target_pairs={{4,0},{8,4},{12,8},{16,12},{20,16},{24,20},{28,24},{5,1},{9,5},{13... | collective-permute-start | bytes 393224 | tf_op jit(solution)/shard_map/ppermute | solution.py:30
  65.7 1.5 %owned.1.old_ref = bf16[2,4,128,640]{3,2,1,0:T(8,128)(2,1)} custom-call(f32[3,4,5,128,128]{4,3,2,1,0:T(8,128)S(1)} %get-tuple-element.26.sums_ref), custom_call_target="tpu_custom_call" | custom-call | tf_op jit(solution)/shard_map/owned/pallas_call | solution.py:486
  67.2 4.9 %collective-permute-done.6.late_ref = bf16[4,128,128]{2,1,0:T(8,128)(2,1)S(1)} collective-permute-done((bf16[4,128,128]{2,1,0:T(8,128)(2,1)S(1)}, bf16[4,128,128]{2,1,0:T(8,128)(2,1)S(1)}, u32[]{:S(2)}, u32[]{:S(2)}) %collective-permute-start.6) | collective-permute-done | bytes 131104 | tf_op jit(solution)/shard_map/ppermute | solution.py:30
  72.1 1.4 %finish.1 = bf16[2,4,128,640]{3,2,1,0:T(8,128)(2,1)} custom-call(s32[32]{0:T(128)S(1)} %copy-done.1, f32[3,4,5,128,128]{4,3,2,1,0:T(8,128)S(1)} %get-tuple-element.26.sums_ref, bf16[3,4,128,128]{3,2,1,0:T(8,128)(2,1)S(1)} %collective-permute-done.5.early_ref, ...), custom_call_target="tpu_custom_call", output_to_operand_aliasing={{}: (4, {})} | custom-call | tf_op jit(solution)/shard_map/finish/pallas_call | solution.py:499
  (7 shorter events, 0.0 us)
Async XLA Ops:
  0.0 15.4 %slice-start = ((s8[5505024]{0:T(1024)(128)(4,1)}), s8[4194304]{0:T(1024)(128)(4,1)S(1)}, s32[]{:S(2)}) async-start(s8[5505024]{0:T(1024)(128)(4,1)} %bitcast), calls=%async_computation | async-start | bytes 8388608
  1.5 13.9 %slice-start.1 = ((s8[5505024]{0:T(1024)(128)(4,1)}), s8[1310720]{0:T(1024)(128)(4,1)S(1)}, s32[]{:S(2)}) async-start(s8[5505024]{0:T(1024)(128)(4,1)} %bitcast), calls=%async_computation.1 | async-start | bytes 2621440
  1.5 13.9 %copy-start = (s32[4,4]{1,0:T(4,128)S(1)}, s32[4,4]{1,0:T(4,128)}, u32[]{:S(2)}) copy-start(s32[4,4]{1,0:T(4,128)} %xlen_ref.5) | copy-start | bytes 196
  1.5 13.9 %copy-start.1 = (s32[32]{0:T(128)S(1)}, s32[32]{0:T(128)}, u32[]{:S(2)}) copy-start(s32[32]{0:T(128)} %zagg_ref.7) | copy-start | bytes 388
  1.5 49.7 %collective-permute-start = (bf16[7,12,64,128]{3,2,1,0:T(8,128)(2,1)S(1)}, bf16[7,12,64,128]{3,2,1,0:T(8,128)(2,1)S(1)}, u32[]{:S(2)}, u32[]{:S(2)}) collective-permute-start(bf16[7,12,64,128]{3,2,1,0:T(8,128)(2,1)S(1)} %top.1.after_ref), channel_id=1, source_target_pairs={{0,4},{4,8},{8,12},{12,16},{16,20},{20,24},{24,28},{1,5},{5,9},{9,... | collective-permute-start | bytes 4128776 | tf_op jit(solution)/shard_map/ppermute | solution.py:30
  7.6 34.5 %collective-permute-start.4 = (bf16[4,7,64,128]{3,2,1,0:T(8,128)(2,1)S(1)}, bf16[4,7,64,128]{3,2,1,0:T(8,128)(2,1)S(1)}, u32[]{:S(2)}, u32[]{:S(2)}) collective-permute-start(bf16[4,7,64,128]{3,2,1,0:T(8,128)(2,1)S(1)} %get-tuple-element.22.low_edge_ref), channel_id=1, source_target_pairs={{1,0},{2,1},{3,2},{5,4},{6,5},{7,6},{9,8},{10,9},{11,10},{13,12},{... | collective-permute-start | bytes 1376264 | tf_op jit(solution)/shard_map/ppermute | solution.py:30
  8.9 33.2 %collective-permute-start.3 = (bf16[4,7,64,128]{3,2,1,0:T(8,128)(2,1)S(1)}, bf16[4,7,64,128]{3,2,1,0:T(8,128)(2,1)S(1)}, u32[]{:S(2)}, u32[]{:S(2)}) collective-permute-start(bf16[4,7,64,128]{3,2,1,0:T(8,128)(2,1)S(1)} %get-tuple-element.23.high_edge_ref), channel_id=1, source_target_pairs={{0,1},{1,2},{2,3},{4,5},{5,6},{6,7},{8,9},{9,10},{10,11},{12,13},{... | collective-permute-start | bytes 1376264 | tf_op jit(solution)/shard_map/ppermute | solution.py:30
  12.0 49.6 %collective-permute-start.1 = (bf16[7,5,64,128]{3,2,1,0:T(8,128)(2,1)S(1)}, bf16[7,5,64,128]{3,2,1,0:T(8,128)(2,1)S(1)}, u32[]{:S(2)}, u32[]{:S(2)}) collective-permute-start(bf16[7,5,64,128]{3,2,1,0:T(8,128)(2,1)S(1)} %get-tuple-element.17), channel_id=1, source_target_pairs={{0,4},{4,8},{8,12},{12,16},{16,20},{20,24},{24,28},{1,5},{5,9},{9,... | collective-permute-start | bytes 1720328 | tf_op jit(solution)/shard_map/ppermute | solution.py:30
  44.5 22.7 %collective-permute-start.5 = (bf16[3,4,128,128]{3,2,1,0:T(8,128)(2,1)S(1)}, bf16[3,4,128,128]{3,2,1,0:T(8,128)(2,1)S(1)}, u32[]{:S(2)}, u32[]{:S(2)}) collective-permute-start(bf16[3,4,128,128]{3,2,1,0:T(8,128)(2,1)S(1)} %get-tuple-element.27), channel_id=1, source_target_pairs={{4,0},{8,4},{12,8},{16,12},{20,16},{24,20},{28,24},{5,1},{9,5},{13... | collective-permute-start | bytes 1179656 | tf_op jit(solution)/shard_map/ppermute | solution.py:30
  46.4 15.2 %collective-permute-start.2 = (bf16[7,1,64,128]{3,2,1,0:T(8,128)(2,1)S(1)}, bf16[7,1,64,128]{3,2,1,0:T(8,128)(2,1)S(1)}, u32[]{:S(2)}, u32[]{:S(2)}) collective-permute-start(bf16[7,1,64,128]{3,2,1,0:T(8,128)(2,1)S(1)} %get-tuple-element.18), channel_id=1, source_target_pairs={{0,4},{4,8},{8,12},{12,16},{16,20},{20,24},{24,28},{1,5},{5,9},{9,... | collective-permute-start | bytes 344072 | tf_op jit(solution)/shard_map/ppermute | solution.py:30
  63.8 8.3 %collective-permute-start.6 = (bf16[4,128,128]{2,1,0:T(8,128)(2,1)S(1)}, bf16[4,128,128]{2,1,0:T(8,128)(2,1)S(1)}, u32[]{:S(2)}, u32[]{:S(2)}) collective-permute-start(bf16[4,128,128]{2,1,0:T(8,128)(2,1)S(1)} %get-tuple-element.28), channel_id=1, source_target_pairs={{4,0},{8,4},{12,8},{16,12},{20,16},{24,20},{28,24},{5,1},{9,5},{13... | collective-permute-start | bytes 393224 | tf_op jit(solution)/shard_map/ppermute | solution.py:30

commit v8 on v7

--- a/solution.py
+++ b/solution.py
@@ -72,10 +72,15 @@
     return jnp.concatenate(parts, axis=0)
 
 
-def top_kernel(p_ref, out_ref, sem):
-    copy = pltpu.make_async_copy(p_ref.at[p_ref.shape[0] - 1], out_ref, sem)
-    copy.start()
-    copy.wait()
+def top_kernel(p_ref, out_ref, sems):
+    layer = p_ref.shape[0] - 1
+    copies = [
+        pltpu.make_async_copy(p_ref.at[layer, y], out_ref.at[y], sems.at[y]) for y in range(out_ref.shape[0])
+    ]
+    for copy in copies:
+        copy.start()
+    for copy in copies:
+        copy.wait()
 
 
 def top(prolong):
@@ -84,7 +89,7 @@
         in_specs=[pl.BlockSpec(memory_space=pltpu.HBM)],
         out_specs=in_vmem(),
         out_shape=jax.ShapeDtypeStruct(prolong.shape[1:], BF16),
-        scratch_shapes=[pltpu.SemaphoreType.DMA],
+        scratch_shapes=[pltpu.SemaphoreType.DMA((prolong.shape[1],))],
         compiler_params=pltpu.CompilerParams(vmem_limit_bytes=LIMIT),
         name="top",
     )(prolong)

time: 73.8 us -> 73.9 us (level)
  the two profiles are of different devices: /device:TPU:20 before, /device:TPU:12 now
where the time goes in v8:
time: 73.9 us; the launch traced here: 73.6 us
  Pallas kernels  40.5 us (55%)
  starting transfers between devices  20 us (27%)
  waiting for transfers between devices  12.9 us (17%)
    pallas_call x1, Pallas kernels, main(): pl.pallas_call(functools.partial(main_kernel, halves), grid=(layers,), in...  26.7 us
    ppermute x7, starting transfers between devices, shifted(): return lax.ppermute(block, axis, route)  20 us
    ppermute x7, waiting for transfers between devices, shifted(): return lax.ppermute(block, axis, route)  12.9 us
    pallas_call x1, Pallas kernels, pack(): pl.pallas_call(pack_kernel, grid=(1,), in_specs=[vmem_block((1, depth, co...  2.52 us
    pallas_call x1, Pallas kernels, lower_sums(): pl.pallas_call(lower_kernel, in_specs=[scalars()] + [in_vmem()] * 3, out_...  2.31 us
    pallas_call x1, Pallas kernels, edges(): pl.pallas_call(functools.partial(edge_kernel, halves), in_specs=[scalars(...  2.3 us
    pallas_call x1, Pallas kernels, upper_sums(): pl.pallas_call(upper_kernel, in_specs=[scalars(), scalars()] + [in_vmem()...  2.18 us
    pallas_call x1, Pallas kernels, top(): pl.pallas_call(top_kernel, in_specs=[pl.BlockSpec(memory_space=pltpu.HBM)...  1.6 us
  transfers between devices with their start and end apart: 7, of which 2 were waited for; matrix products, arithmetic and copies ran while one was open for 0% of the time, Pallas kernels for 51%

profile of v8, /device:TPU:12, one launch (start us, length us, event | category | flops | bytes accessed | tf_op | source)
XLA Modules:
  0.0 73.6 jit_solution(11208737101680098921)
XLA Ops:
  0.0 1.6 %top.1.after_ref = bf16[7,12,64,128]{3,2,1,0:T(8,128)(2,1)S(1)} custom-call(bf16[4,7,12,64,128]{4,3,2,1,0:T(8,128)(2,1)} %own_ref.3), custom_call_target="tpu_custom_call" | custom-call | tf_op jit(solution)/shard_map/top/pallas_call | solution.py:87
  1.6 0.0 slice-start.1
  1.6 0.0 copy-start
  1.6 0.0 copy-start.1
  1.6 3.6 %collective-permute-start = (bf16[7,12,64,128]{3,2,1,0:T(8,128)(2,1)S(1)}, bf16[7,12,64,128]{3,2,1,0:T(8,128)(2,1)S(1)}, u32[]{:S(2)}, u32[]{:S(2)}) collective-permute-start(bf16[7,12,64,128]{3,2,1,0:T(8,128)(2,1)S(1)} %top.1.after_ref), channel_id=1, source_target_pairs={{0,4},{4,8},{8,12},{12,16},{16,20},{20,24},{24,28},{1,5},{5,9},{9,... | collective-permute-start | bytes 4128776 | tf_op jit(solution)/shard_map/ppermute | solution.py:30
  5.2 2.5 %pack.1 = (bf16[7,5,64,128]{3,2,1,0:T(8,128)(2,1)S(1)}, bf16[7,1,64,128]{3,2,1,0:T(8,128)(2,1)S(1)}, bf16[4,7,64,128]{3,2,1,0:T(8,128)(2,1)S(1)}, bf16[4,7,64,128]{3,2,1,0:T(8,128)(2,1)S(1)}) custom-call(bf16[4,7,12,64,448]{4,3,2,1,0:T(8,128)(2,1)} %a_ref.3, bf16[4,7,12,64,128]{4,3,2,1,0:T(8,128)(2,1)} %own_ref.3, bf16[7,12,64,128]{3,2,1,0:T(8,128)(2,1)S(1)} %top.1.after_ref), custom_call_target="tpu_custom_call" | custom-call | tf_op jit(solution)/shard_map/pack/pallas_call | solution.py:128
  7.7 1.3 %collective-permute-start.4 = (bf16[4,7,64,128]{3,2,1,0:T(8,128)(2,1)S(1)}, bf16[4,7,64,128]{3,2,1,0:T(8,128)(2,1)S(1)}, u32[]{:S(2)}, u32[]{:S(2)}) collective-permute-start(bf16[4,7,64,128]{3,2,1,0:T(8,128)(2,1)S(1)} %get-tuple-element.22.low_edge_ref), channel_id=1, source_target_pairs={{1,0},{2,1},{3,2},{5,4},{6,5},{7,6},{9,8},{10,9},{11,10},{13,12},{... | collective-permute-start | bytes 1376264 | tf_op jit(solution)/shard_map/ppermute | solution.py:30
  9.0 3.1 %collective-permute-start.3 = (bf16[4,7,64,128]{3,2,1,0:T(8,128)(2,1)S(1)}, bf16[4,7,64,128]{3,2,1,0:T(8,128)(2,1)S(1)}, u32[]{:S(2)}, u32[]{:S(2)}) collective-permute-start(bf16[4,7,64,128]{3,2,1,0:T(8,128)(2,1)S(1)} %get-tuple-element.23.high_edge_ref), channel_id=1, source_target_pairs={{0,1},{1,2},{2,3},{4,5},{5,6},{6,7},{8,9},{9,10},{10,11},{12,13},{... | collective-permute-start | bytes 1376264 | tf_op jit(solution)/shard_map/ppermute | solution.py:30
  12.1 3.4 %collective-permute-start.1 = (bf16[7,5,64,128]{3,2,1,0:T(8,128)(2,1)S(1)}, bf16[7,5,64,128]{3,2,1,0:T(8,128)(2,1)S(1)}, u32[]{:S(2)}, u32[]{:S(2)}) collective-permute-start(bf16[7,5,64,128]{3,2,1,0:T(8,128)(2,1)S(1)} %get-tuple-element.17), channel_id=1, source_target_pairs={{0,4},{4,8},{8,12},{12,16},{16,20},{20,24},{24,28},{1,5},{5,9},{9,... | collective-permute-start | bytes 1720328 | tf_op jit(solution)/shard_map/ppermute | solution.py:30
  15.6 26.7 %coarsen.1 = (f32[3,4,5,128,128]{4,3,2,1,0:T(8,128)S(1)}, bf16[7,12,64,128]{3,2,1,0:T(8,128)(2,1)S(1)}, bf16[4,7,64,128]{3,2,1,0:T(8,128)(2,1)S(1)}, bf16[4,7,64,128]{3,2,1,0:T(8,128)(2,1)S(1)}) custom-call(s32[32]{0:T(128)S(1)} %copy-done.1, s32[4,4]{1,0:T(4,128)S(1)} %copy-done, bf16[4,7,12,64,448]{4,3,2,1,0:T(8,128)(2,1)} %a_ref.3, ...), custom_call_target="tpu_custom_call" | custom-call | flops 16911433728 | bytes 41943040 | tf_op jit(solution)/shard_map/coarsen/pallas_call | solution.py:291
  42.3 0.0 collective-permute-done.4.right_ref
  42.3 0.0 collective-permute-done.3.left_ref
  42.3 2.3 %edges.1 = (f32[3,4,5,128,128]{4,3,2,1,0:T(8,128)S(1)}, bf16[3,4,128,128]{3,2,1,0:T(8,128)(2,1)S(1)}) custom-call(s32[32]{0:T(128)S(1)} %copy-done.1, bf16[4,7,64,128]{3,2,1,0:T(8,128)(2,1)S(1)} %get-tuple-element.20.first_ref, bf16[4,7,64,128]{3,2,1,0:T(8,128)(2,1)S(1)} %get-tuple-element.21.last_ref, ...), custom_call_target="tpu_custom_call", output_to_operand_aliasing={{0}: (7, {})} | custom-call | tf_op jit(solution)/shard_map/edges/pallas_call | solution.py:347
  44.6 1.9 %collective-permute-start.5 = (bf16[3,4,128,128]{3,2,1,0:T(8,128)(2,1)S(1)}, bf16[3,4,128,128]{3,2,1,0:T(8,128)(2,1)S(1)}, u32[]{:S(2)}, u32[]{:S(2)}) collective-permute-start(bf16[3,4,128,128]{3,2,1,0:T(8,128)(2,1)S(1)} %get-tuple-element.27), channel_id=1, source_target_pairs={{4,0},{8,4},{12,8},{16,12},{20,16},{24,20},{28,24},{5,1},{9,5},{13... | collective-permute-start | bytes 1179656 | tf_op jit(solution)/shard_map/ppermute | solution.py:30
  46.5 4.8 %collective-permute-start.2 = (bf16[7,1,64,128]{3,2,1,0:T(8,128)(2,1)S(1)}, bf16[7,1,64,128]{3,2,1,0:T(8,128)(2,1)S(1)}, u32[]{:S(2)}, u32[]{:S(2)}) collective-permute-start(bf16[7,1,64,128]{3,2,1,0:T(8,128)(2,1)S(1)} %get-tuple-element.18), channel_id=1, source_target_pairs={{0,4},{4,8},{8,12},{12,16},{16,20},{20,24},{24,28},{1,5},{5,9},{9,... | collective-permute-start | bytes 344072 | tf_op jit(solution)/shard_map/ppermute | solution.py:30
  51.4 0.0 collective-permute-done.theirs_ref
  51.4 2.3 %lower.1.lower_ref = f32[4,128,128]{2,1,0:T(8,128)S(1)} custom-call(s32[4,4]{1,0:T(4,128)S(1)} %copy-done, bf16[7,12,64,128]{3,2,1,0:T(8,128)(2,1)S(1)} %collective-permute-done.theirs_ref, bf16[7,12,64,128]{3,2,1,0:T(8,128)(2,1)S(1)} %get-tuple-element.19.a_ref, bf16[4,7,12,64,128]{4,3,2,1,0:T(8,128)(2,1)S(1)} %bitcast.1), custom_call_target="tpu_custom_call" | custom-call | tf_op jit(solution)/shard_map/lower/pallas_call | solution.py:390
  53.7 8.0 %collective-permute-done.2.rest_ref = bf16[7,1,64,128]{3,2,1,0:T(8,128)(2,1)S(1)} collective-permute-done((bf16[7,1,64,128]{3,2,1,0:T(8,128)(2,1)S(1)}, bf16[7,1,64,128]{3,2,1,0:T(8,128)(2,1)S(1)}, u32[]{:S(2)}, u32[]{:S(2)}) %collective-permute-start.2) | collective-permute-done | bytes 114720 | tf_op jit(solution)/shard_map/ppermute | solution.py:30
  61.7 0.0 collective-permute-done.1.most_ref
  61.7 2.2 %upper.1 = (f32[3,4,5,128,128]{4,3,2,1,0:T(8,128)S(1)}, bf16[4,128,128]{2,1,0:T(8,128)(2,1)S(1)}) custom-call(s32[32]{0:T(128)S(1)} %copy-done.1, s32[4,4]{1,0:T(4,128)S(1)} %copy-done, bf16[7,12,64,128]{3,2,1,0:T(8,128)(2,1)S(1)} %collective-permute-done.theirs_ref, ...), custom_call_target="tpu_custom_call", output_to_operand_aliasing={{0}: (7, {})} | custom-call | tf_op jit(solution)/shard_map/upper/pallas_call | solution.py:444
  63.9 1.9 %collective-permute-start.6 = (bf16[4,128,128]{2,1,0:T(8,128)(2,1)S(1)}, bf16[4,128,128]{2,1,0:T(8,128)(2,1)S(1)}, u32[]{:S(2)}, u32[]{:S(2)}) collective-permute-start(bf16[4,128,128]{2,1,0:T(8,128)(2,1)S(1)} %get-tuple-element.28), channel_id=1, source_target_pairs={{4,0},{8,4},{12,8},{16,12},{20,16},{24,20},{28,24},{5,1},{9,5},{13... | collective-permute-start | bytes 393224 | tf_op jit(solution)/shard_map/ppermute | solution.py:30
  65.8 1.5 %owned.1.old_ref = bf16[2,4,128,640]{3,2,1,0:T(8,128)(2,1)} custom-call(f32[3,4,5,128,128]{4,3,2,1,0:T(8,128)S(1)} %get-tuple-element.26.sums_ref), custom_call_target="tpu_custom_call" | custom-call | tf_op jit(solution)/shard_map/owned/pallas_call | solution.py:491
  67.3 4.9 %collective-permute-done.6.late_ref = bf16[4,128,128]{2,1,0:T(8,128)(2,1)S(1)} collective-permute-done((bf16[4,128,128]{2,1,0:T(8,128)(2,1)S(1)}, bf16[4,128,128]{2,1,0:T(8,128)(2,1)S(1)}, u32[]{:S(2)}, u32[]{:S(2)}) %collective-permute-start.6) | collective-permute-done | bytes 131104 | tf_op jit(solution)/shard_map/ppermute | solution.py:30
  72.2 1.4 %finish.1 = bf16[2,4,128,640]{3,2,1,0:T(8,128)(2,1)} custom-call(s32[32]{0:T(128)S(1)} %copy-done.1, f32[3,4,5,128,128]{4,3,2,1,0:T(8,128)S(1)} %get-tuple-element.26.sums_ref, bf16[3,4,128,128]{3,2,1,0:T(8,128)(2,1)S(1)} %collective-permute-done.5.early_ref, ...), custom_call_target="tpu_custom_call", output_to_operand_aliasing={{}: (4, {})} | custom-call | tf_op jit(solution)/shard_map/finish/pallas_call | solution.py:504
  (7 shorter events, 0.0 us)
Async XLA Ops:
  0.0 15.5 %slice-start = ((s8[5505024]{0:T(1024)(128)(4,1)}), s8[4194304]{0:T(1024)(128)(4,1)S(1)}, s32[]{:S(2)}) async-start(s8[5505024]{0:T(1024)(128)(4,1)} %bitcast), calls=%async_computation | async-start | bytes 8388608
  1.6 13.9 %slice-start.1 = ((s8[5505024]{0:T(1024)(128)(4,1)}), s8[1310720]{0:T(1024)(128)(4,1)S(1)}, s32[]{:S(2)}) async-start(s8[5505024]{0:T(1024)(128)(4,1)} %bitcast), calls=%async_computation.1 | async-start | bytes 2621440
  1.6 13.9 %copy-start = (s32[4,4]{1,0:T(4,128)S(1)}, s32[4,4]{1,0:T(4,128)}, u32[]{:S(2)}) copy-start(s32[4,4]{1,0:T(4,128)} %xlen_ref.5) | copy-start | bytes 196
  1.6 13.9 %copy-start.1 = (s32[32]{0:T(128)S(1)}, s32[32]{0:T(128)}, u32[]{:S(2)}) copy-start(s32[32]{0:T(128)} %zagg_ref.7) | copy-start | bytes 388
  1.6 49.7 %collective-permute-start = (bf16[7,12,64,128]{3,2,1,0:T(8,128)(2,1)S(1)}, bf16[7,12,64,128]{3,2,1,0:T(8,128)(2,1)S(1)}, u32[]{:S(2)}, u32[]{:S(2)}) collective-permute-start(bf16[7,12,64,128]{3,2,1,0:T(8,128)(2,1)S(1)} %top.1.after_ref), channel_id=1, source_target_pairs={{0,4},{4,8},{8,12},{12,16},{16,20},{20,24},{24,28},{1,5},{5,9},{9,... | collective-permute-start | bytes 4128776 | tf_op jit(solution)/shard_map/ppermute | solution.py:30
  7.7 34.5 %collective-permute-start.4 = (bf16[4,7,64,128]{3,2,1,0:T(8,128)(2,1)S(1)}, bf16[4,7,64,128]{3,2,1,0:T(8,128)(2,1)S(1)}, u32[]{:S(2)}, u32[]{:S(2)}) collective-permute-start(bf16[4,7,64,128]{3,2,1,0:T(8,128)(2,1)S(1)} %get-tuple-element.22.low_edge_ref), channel_id=1, source_target_pairs={{1,0},{2,1},{3,2},{5,4},{6,5},{7,6},{9,8},{10,9},{11,10},{13,12},{... | collective-permute-start | bytes 1376264 | tf_op jit(solution)/shard_map/ppermute | solution.py:30
  9.0 33.2 %collective-permute-start.3 = (bf16[4,7,64,128]{3,2,1,0:T(8,128)(2,1)S(1)}, bf16[4,7,64,128]{3,2,1,0:T(8,128)(2,1)S(1)}, u32[]{:S(2)}, u32[]{:S(2)}) collective-permute-start(bf16[4,7,64,128]{3,2,1,0:T(8,128)(2,1)S(1)} %get-tuple-element.23.high_edge_ref), channel_id=1, source_target_pairs={{0,1},{1,2},{2,3},{4,5},{5,6},{6,7},{8,9},{9,10},{10,11},{12,13},{... | collective-permute-start | bytes 1376264 | tf_op jit(solution)/shard_map/ppermute | solution.py:30
  12.1 49.6 %collective-permute-start.1 = (bf16[7,5,64,128]{3,2,1,0:T(8,128)(2,1)S(1)}, bf16[7,5,64,128]{3,2,1,0:T(8,128)(2,1)S(1)}, u32[]{:S(2)}, u32[]{:S(2)}) collective-permute-start(bf16[7,5,64,128]{3,2,1,0:T(8,128)(2,1)S(1)} %get-tuple-element.17), channel_id=1, source_target_pairs={{0,4},{4,8},{8,12},{12,16},{16,20},{20,24},{24,28},{1,5},{5,9},{9,... | collective-permute-start | bytes 1720328 | tf_op jit(solution)/shard_map/ppermute | solution.py:30
  44.6 22.6 %collective-permute-start.5 = (bf16[3,4,128,128]{3,2,1,0:T(8,128)(2,1)S(1)}, bf16[3,4,128,128]{3,2,1,0:T(8,128)(2,1)S(1)}, u32[]{:S(2)}, u32[]{:S(2)}) collective-permute-start(bf16[3,4,128,128]{3,2,1,0:T(8,128)(2,1)S(1)} %get-tuple-element.27), channel_id=1, source_target_pairs={{4,0},{8,4},{12,8},{16,12},{20,16},{24,20},{28,24},{5,1},{9,5},{13... | collective-permute-start | bytes 1179656 | tf_op jit(solution)/shard_map/ppermute | solution.py:30
  46.5 15.1 %collective-permute-start.2 = (bf16[7,1,64,128]{3,2,1,0:T(8,128)(2,1)S(1)}, bf16[7,1,64,128]{3,2,1,0:T(8,128)(2,1)S(1)}, u32[]{:S(2)}, u32[]{:S(2)}) collective-permute-start(bf16[7,1,64,128]{3,2,1,0:T(8,128)(2,1)S(1)} %get-tuple-element.18), channel_id=1, source_target_pairs={{0,4},{4,8},{8,12},{12,16},{16,20},{20,24},{24,28},{1,5},{5,9},{9,... | collective-permute-start | bytes 344072 | tf_op jit(solution)/shard_map/ppermute | solution.py:30
  63.9 8.3 %collective-permute-start.6 = (bf16[4,128,128]{2,1,0:T(8,128)(2,1)S(1)}, bf16[4,128,128]{2,1,0:T(8,128)(2,1)S(1)}, u32[]{:S(2)}, u32[]{:S(2)}) collective-permute-start(bf16[4,128,128]{2,1,0:T(8,128)(2,1)S(1)} %get-tuple-element.28), channel_id=1, source_target_pairs={{4,0},{8,4},{12,8},{16,12},{20,16},{24,20},{28,24},{5,1},{9,5},{13... | collective-permute-start | bytes 393224 | tf_op jit(solution)/shard_map/ppermute | solution.py:30
